TPU v7x, 128 devices: a whole 4x4x4 slice. The times are simulated.
128 devices in a mesh: dp: 16 (over z, x), pair: 8 (over y, core).
Axes of the slice: x: 4, y: 4, z: 4, core: 2. Of those that a mesh axis runs over, the one named last changes fastest.
Arguments:
- table: float32 [65536, 512], P(('dp', 'pair')), may hold values from -6 to 6
- accum: float32 [65536], P(('dp', 'pair')), may hold values from 0.05 to 2
- item_row: int32 [49152], P(('dp', 'pair')), may hold values from 0 to 65535, as said below
- segments: int32 [16, 3072], P('dp'), may hold values from 0 to 1, never falling along the last dimension, each value on 1 to 2880 neighbouring positions
- pairs: int32 [16, 40, 2], P('dp'), may hold values from -1 to 7, as said below
- w_in: bfloat16 [512, 2048], replicated, may hold values from -0.25 to 0.25
- w_out: bfloat16 [512, 512], replicated, may hold values from -0.25 to 0.25
- out_grad: bfloat16 [49152, 512], P(('dp', 'pair')), may hold values from -6 to 6
Outputs:
- layer_out: bfloat16 [49152, 512], P(('dp', 'pair'))
- table_new: float32 [65536, 512], P(('dp', 'pair'))
- accum_new: float32 [65536], P(('dp', 'pair'))
- grad_in: float32 [512, 2048], P(('dp', 'pair'))
- grad_out: float32 [512, 512], P(('dp', 'pair'))
Inputs may be any that keep to these rules, and one draw needn't show every extreme that they name: Row r is held by device r // 512 at slot r % 512. The 384 actions of one device (aligned blocks of item_row) name rows of any one device at most 6 times, repeats counted; in every draw one device receives exactly 6 from every device. Row g lists causal block pairs (query block, key block) of the group, key block at most query block, each at most once; every diagonal pair and every pair with key block 0 is listed, the other causal pairs some of them; slots s * 5 to s * 5 + 4 belong to index s of pair; unused slots hold (-1, -1). `segments`: actions with equal ids in a group belong to one history.
All inputs are finite; a program needn't handle non-finite values.
Results may differ from a plain program's by a relative error of at most 0.0025.
The roundings to bfloat16 on the way count: a program that leaves them out, or rounds other values in their place, can miss the bound.
Values may be sent and summed in bfloat16 or wider, within the bound.
A program may use at most 192 MiB of HBM per device.

v0:
```python
import math

import jax
import jax.numpy as jnp
from jax import lax
from jax.sharding import PartitionSpec as P

HEADS = 8


norm_eps = 1e-05
learn_rate = 0.5


def normalize(values):
    row_mean = jnp.mean(values, axis=-1, keepdims=True)
    centred = values - row_mean
    spread = jnp.sqrt(jnp.mean(centred * centred, axis=-1, keepdims=True) + norm_eps)
    return (centred / spread, spread)


def norm_back(grad_rows, normed, spread):
    first_mean = jnp.mean(grad_rows, axis=-1, keepdims=True)
    second_mean = jnp.mean(grad_rows * normed, axis=-1, keepdims=True)
    return (grad_rows - first_mean - normed * second_mean) / spread


def silu_slope(values):
    sigmoid_value = jax.nn.sigmoid(values)
    return sigmoid_value * (1.0 + values * (1.0 - sigmoid_value))


def heads_of(matrix):
    return matrix.reshape(matrix.shape[0], HEADS, matrix.shape[1] // HEADS)


def pair_scores(query_rows, key_rows, score_scale):
    return (
        jnp.einsum(
            "rhd,chd->hrc",
            heads_of(query_rows),
            heads_of(key_rows),
            preferred_element_type=jnp.float32,
        )
        * score_scale
    )


def pair_forward(query_rows, key_rows, value_rows, visible, score_scale):
    scores = pair_scores(query_rows, key_rows, score_scale)
    weights = jnp.where(visible[None], jax.nn.silu(scores), 0.0).astype(jnp.bfloat16)
    attended = jnp.einsum(
        "hrc,chd->rhd", weights, heads_of(value_rows), preferred_element_type=jnp.float32
    )
    return attended.reshape(query_rows.shape[0], -1)


def pair_terms(query_rows, key_rows, value_rows, grad_rows, visible, score_scale):
    scores = pair_scores(query_rows, key_rows, score_scale)
    weights = jnp.where(visible[None], jax.nn.silu(scores), 0.0).astype(jnp.bfloat16)
    grad_weights = jnp.einsum(
        "rhd,chd->hrc",
        heads_of(grad_rows),
        heads_of(value_rows),
        preferred_element_type=jnp.float32,
    )
    grad_scores = jnp.where(
        visible[None], grad_weights * silu_slope(scores) * score_scale, 0.0
    ).astype(jnp.bfloat16)
    return (weights, grad_scores)


def to_query(grad_scores, key_rows):
    summed = jnp.einsum(
        "hrc,chd->rhd", grad_scores, heads_of(key_rows), preferred_element_type=jnp.float32
    )
    return summed.reshape(summed.shape[0], -1)


def to_key(grad_scores, query_rows):
    summed = jnp.einsum(
        "hrc,rhd->chd", grad_scores, heads_of(query_rows), preferred_element_type=jnp.float32
    )
    return summed.reshape(summed.shape[0], -1)


def body(table, accum, item_row, segments, pairs, w_in, w_out, out_grad):
    tokens = item_row.shape[0]
    rows_dev, model_width = table.shape
    shards = lax.axis_size(("dp", "pair"))
    group_span = lax.axis_size("pair")
    block_here = lax.axis_index("pair")
    bound_rows = 2 * (tokens // shards)
    score_scale = 1.0 / math.sqrt(model_width // HEADS)
    owner_ids = item_row // rows_dev
    row_slot = item_row % rows_dev
    onehot = (owner_ids[:, None] == jnp.arange(shards, dtype=jnp.int32)[None, :]).astype(jnp.int32)
    bucket_rank = jnp.sum(jnp.cumsum(onehot, axis=0) * onehot, axis=1) - 1
    target = owner_ids * bound_rows + bucket_rank
    request = (
        jnp.zeros((shards * bound_rows,), jnp.int32)
        .at[target]
        .set(row_slot)
        .reshape(shards, bound_rows)
    )
    slot_ids = lax.all_to_all(request, ("dp", "pair"), split_axis=0, concat_axis=0, tiled=True)
    found_rows = table[slot_ids].astype(jnp.bfloat16)
    fetched = lax.all_to_all(found_rows, ("dp", "pair"), split_axis=0, concat_axis=0, tiled=True)
    action_rows = fetched.reshape(shards * bound_rows, model_width)[target]
    action_float = action_rows.astype(jnp.float32)
    normed, action_spread = normalize(action_float)
    normed_low = normed.astype(jnp.bfloat16)
    pre_act = jnp.dot(normed_low, w_in, preferred_element_type=jnp.float32)
    hidden = jax.nn.silu(pre_act).astype(jnp.bfloat16)
    unit_gate = hidden[:, :model_width].astype(jnp.float32)
    value_own = hidden[:, model_width : 2 * model_width]
    query_own = hidden[:, 2 * model_width : 3 * model_width]
    key_own = hidden[:, 3 * model_width :]
    segment_ids = segments[0]
    pair_list = pairs[0]
    local_rows = jnp.arange(tokens, dtype=jnp.int32)
    own_pos = block_here * tokens + local_rows
    own_segment = lax.dynamic_slice_in_dim(segment_ids, block_here * tokens, tokens)
    blocks = jnp.arange(group_span, dtype=jnp.int32)
    present = jnp.any(
        (pair_list[:, 0, None, None] == blocks[None, :, None])
        & (pair_list[:, 1, None, None] == blocks[None, None, :]),
        axis=0,
    )

    def keys_seen(row_count):
        key_pos = jnp.arange(row_count, dtype=jnp.int32)
        listed = present[block_here][key_pos // tokens]
        return (
            listed[None, :]
            & (key_pos[None, :] <= own_pos[:, None])
            & (segment_ids[None, :] == own_segment[:, None])
        )

    def queries_seen(row_count):
        query_pos = jnp.arange(row_count, dtype=jnp.int32)
        listed = present[query_pos // tokens, block_here]
        return (
            listed[:, None]
            & (own_pos[None, :] <= query_pos[:, None])
            & (own_segment[None, :] == segment_ids[:, None])
        )

    zeros_rows = jnp.zeros((tokens, model_width), jnp.float32)
    value_rows = lax.all_gather(value_own, "pair", axis=0, tiled=True)
    key_rows = lax.all_gather(key_own, "pair", axis=0, tiled=True)
    visible = keys_seen(key_rows.shape[0])
    added = lax.cond(
        jnp.any(visible),
        lambda: pair_forward(query_own, key_rows, value_rows, visible, score_scale),
        lambda: jnp.zeros_like(zeros_rows),
    )
    attended = added
    attend_norm, attend_spread = normalize(attended)
    gated = (attend_norm * unit_gate).astype(jnp.bfloat16)
    layer_out = (jnp.dot(gated, w_out, preferred_element_type=jnp.float32) + action_float).astype(
        jnp.bfloat16
    )
    grad_gated = lax.dot_general(
        out_grad, w_out, (((1,), (1,)), ((), ())), preferred_element_type=jnp.float32
    )
    grad_attend = norm_back(grad_gated * unit_gate, attend_norm, attend_spread).astype(jnp.bfloat16)
    fold_value_rows = lax.all_gather(value_own, "pair", axis=0, tiled=True)
    fold_key_rows = lax.all_gather(key_own, "pair", axis=0, tiled=True)
    fold_visible = keys_seen(fold_key_rows.shape[0])

    def compute():
        weights, grad_scores = pair_terms(
            query_own, fold_key_rows, fold_value_rows, grad_attend, fold_visible, score_scale
        )
        return to_query(grad_scores, fold_key_rows)

    grad_query = lax.cond(jnp.any(fold_visible), compute, lambda: jnp.zeros_like(zeros_rows))

    def fold_key(running, arrived):
        query_rows, grad_rows = arrived
        visible = queries_seen(query_rows.shape[0])

        def compute():
            weights, grad_scores = pair_terms(
                query_rows, key_own, value_own, grad_rows, visible, score_scale
            )
            return (to_key(grad_scores, query_rows), to_key(weights, grad_rows))

        def nothing():
            return (jnp.zeros_like(running[0]), jnp.zeros_like(running[1]))

        added = lax.cond(jnp.any(visible), compute, nothing)
        return (added[0], added[1])

    grad_key, grad_value = fold_key(
        (zeros_rows, zeros_rows),
        (
            lax.all_gather(query_own, "pair", axis=0, tiled=True),
            lax.all_gather(grad_attend, "pair", axis=0, tiled=True),
        ),
    )
    grad_hidden = jnp.concatenate(
        [grad_gated * attend_norm, grad_value, grad_query, grad_key], axis=1
    )
    grad_pre = (grad_hidden * silu_slope(pre_act)).astype(jnp.bfloat16)
    grad_normed = lax.dot_general(
        grad_pre, w_in, (((1,), (1,)), ((), ())), preferred_element_type=jnp.float32
    )
    grad_action = norm_back(grad_normed, normed, action_spread) + out_grad.astype(jnp.float32)
    first_part = lax.dot_general(
        normed_low, grad_pre, (((0,), (0,)), ((), ())), preferred_element_type=jnp.float32
    )
    second_part = lax.dot_general(
        gated, out_grad, (((0,), (0,)), ((), ())), preferred_element_type=jnp.float32
    )
    combined = lax.psum_scatter(
        jnp.concatenate([first_part, second_part], axis=1),
        ("dp", "pair"),
        scatter_dimension=0,
        tiled=True,
    )
    factor = 1.0 / math.sqrt(tokens * shards)
    sending = (
        jnp.zeros((shards * bound_rows, model_width), jnp.float32)
        .at[target]
        .set(grad_action)
        .reshape(shards, bound_rows, model_width)
    )
    returned = lax.all_to_all(
        sending.astype(jnp.bfloat16), ("dp", "pair"), split_axis=0, concat_axis=0, tiled=True
    ).astype(sending.dtype)
    row_total = (
        jnp.zeros((rows_dev, model_width), jnp.float32)
        .at[slot_ids.reshape(-1)]
        .add(returned.reshape(-1, model_width))
    )
    accum_new = accum + jnp.mean(row_total * row_total, axis=1)
    table_new = table - learn_rate * row_total / jnp.sqrt(accum_new)[:, None]
    return (
        layer_out,
        table_new,
        accum_new,
        combined[:, : 4 * model_width] * factor,
        combined[:, 4 * model_width :] * factor,
    )


def solution(mesh):
    placed = (
        P(("dp", "pair"), None),
        P(("dp", "pair")),
        P(("dp", "pair")),
        P("dp", None),
        P("dp", None, None),
        P(),
        P(),
        P(("dp", "pair"), None),
    )
    return jax.shard_map(
        body,
        mesh=mesh,
        in_specs=placed,
        out_specs=(
            P(("dp", "pair"), None),
            P(("dp", "pair"), None),
            P(("dp", "pair")),
            P(("dp", "pair"), None),
            P(("dp", "pair"), None),
        ),
        check_vma=False,
    )
```

profile of v0, /device:TPU:1, one launch (start us, length us, event | category | flops | bytes accessed | tf_op | source)
XLA Modules:
  0.0 533.0 jit_solution(12694998078312262931)
XLA Ops:
  7.2 0.8 add_select_fusion
  8.7 2.9 scatter_custom_fusion
  11.8 20.9 %all_to_all.22 = s32[128,1,6]{2,1,0:T(1,128)S(1)} all-to-all(s32[128,1,6]{2,1,0:T(1,128)S(1)} %bitcast.93), channel_id=1, replica_groups=mesh['dp'=16,'pair'=8] {'dp','pair'}, dimensions={0} | all-to-all | bytes 6144 | tf_op jit(solution)/shard_map/all_to_all | solution.py:106
  33.5 2.9 gather_fusion
  36.5 2.1 reshape.391
  38.6 5.2 all-to-all-start.1
  43.9 18.5 %all-to-all-done.1 = bf16[128,6,512]{2,1,0:T(8,128)(2,1)} async-done(((bf16[128,6,512]{2,1,0:T(8,128)(2,1)}), bf16[128,6,512]{2,1,0:T(8,128)(2,1)}, u32[]{:S(2)}, u32[]{:S(2)}) %all-to-all-start.1) | async-done | bytes 786464 | tf_op jit(solution)/shard_map/all_to_all | solution.py:108
  62.4 1.4 reshape.302
  63.8 2.1 gather_fusion.1
  66.4 2.9 multiply_convert_fusion
  69.3 1.1 copy-done.12
  70.4 1.0 fusion.72
  71.5 0.7 all-gather.7.cloned.1.call-update
  72.2 0.7 all-gather.11.cloned.1.call-update
  74.1 4.5 select_reduce_fusion
  79.3 3.5 fusion.69
  83.5 12.6 %all-gather.5.cloned.1.call-done = bf16[3072,512]{1,0:T(8,128)(2,1)} async-done(((bf16[384,512]{1,0:T(8,128)(2,1)}), bf16[3072,512]{1,0:T(8,128)(2,1)}) %all-gather.5.cloned.1.call-update) | async-done | bytes 3145744 | tf_op jit(solution)/shard_map/all_gather | solution.py:151
  96.1 29.3 %all-gather.7.cloned.1.call-done = bf16[3072,512]{1,0:T(8,128)(2,1)} async-done(((bf16[384,512]{1,0:T(8,128)(2,1)}), bf16[3072,512]{1,0:T(8,128)(2,1)}) %all-gather.7.cloned.1.call-update) | async-done | bytes 3145744 | tf_op jit(solution)/shard_map/all_gather | solution.py:150
  125.4 30.1 %conditional.3 = (f32[384,1]{0,1:T(1,128)S(1)}, f32[384,512]{1,0:T(8,128)S(1)}) conditional(s32[]{:T(128)} %convert_element_type.61, () %tuple.32, (pred[384,3072]{1,0:T(8,128)(4,1)}, bf16[384,512]{1,0:T(8,128)(2,1)}, bf16[3072,512]{1,0:T(8,128)(2,1)}, bf16[3072,512]{1,0:T(8,128)(2,1)}) %tuple.33), branch_computations={%region_8.9_spmd, %region_9.11_spmd} | conditional | flops 2482175488 | bytes 25170476 | solution.py:153
  125.7 4.6 copy.67
  130.3 4.7 copy.68
  135.2 18.9 %fusion.71 = (f32[384]{0:T(512)S(1)}, f32[8,384,64]{1,2,0:T(8,128)}) fusion(bf16[3072,8,64]{0,2,1:T(8,128)(2,1)} %bitcast.81, pred[384,3072]{1,0:T(8,128)(4,1)} %get-tuple-element.33, bf16[384,8,64]{0,2,1:T(8,128)(2,1)S(1)} %bitcast.90, bf16[3072,8,64]{0,2,1:T(8,128)(2,1)} %bitcast.80), kind=kOutput, calls=%fused_computation.135 | convolution fusion | flops 2482175488 | bytes 8652288 | tf_op jit(solution)/shard_map/cond/branch_1_fun/hrc,chd->rhd/dot_general | solution.py:52
  154.2 1.4 copy.84
  155.9 1.8 fusion.47
  157.7 2.4 fusion.64
  160.3 25.3 %gather_fusion.2 = pred[3072]{0:T(1024)(128)(4,1)S(1)} fusion(pred[8,8]{1,0:T(8,128)(4,1)S(1)} %and_reduce_fusion, s32[3072]{0:T(1024)S(1)} %bitcast.74), kind=kCustom, calls=%fused_computation.2 | custom fusion | bytes 30720 | tf_op jit(solution)/shard_map/gather | solution.py:142
  185.6 4.1 fusion.67
  190.4 77.0 %conditional.5 = (f32[384,512]{1,0:T(8,128)}) conditional(s32[]{:T(128)} %convert_element_type.61, () %tuple.36, (pred[384,3072]{1,0:T(8,128)(4,1)}, bf16[384,512]{1,0:T(8,128)(2,1)}, bf16[3072,512]{1,0:T(8,128)(2,1)}, bf16[384,512]{1,0:T(8,128)(2,1)S(1)}, bf16[3072,512]{1,0:T(8,128)(2,1)}) %tuple.97), branch_computations={%region_17.18_spmd, %region_18.19_spmd} | conditional | flops 3737124864 | bytes 100270088 | solution.py:178
  207.3 4.7 copy.75
  211.9 1.9 copy.74
  213.9 16.2 %fusion.75 = f32[8,384,3072]{2,1,0:T(8,128)} fusion(bf16[384,8,64]{0,2,1:T(8,128)(2,1)} %bitcast.83, bf16[3072,8,64]{0,2,1:T(8,128)(2,1)} %bitcast.77), kind=kOutput, calls=%fused_computation.139 | convolution fusion | flops 1207959552 | bytes 41287680 | tf_op jit(solution)/shard_map/cond/branch_1_fun/rhd,chd->hrc/dot_general | solution.py:61
  230.1 4.6 copy.77
  234.7 0.9 copy.76
  235.7 29.4 %fusion.16 = f32[8,384,64]{1,2,0:T(8,128)} fusion(bf16[3072,8,64]{0,2,1:T(8,128)(2,1)} %bitcast.82, f32[8,384,3072]{2,1,0:T(8,128)} %fusion.75, pred[384,3072]{1,0:T(8,128)(4,1)} %get-tuple-element.42, bf16[384,8,64]{0,2,1:T(8,128)(2,1)} %bitcast.91), kind=kOutput, calls=%fused_computation.25 | convolution fusion | flops 2529165312 | bytes 43253760 | tf_op jit(solution)/shard_map/cond/branch_1_fun/hrc,chd->rhd/dot_general | solution.py:74
  265.1 2.3 copy.90
  267.4 2.8 fusion.58
  270.2 80.1 %conditional.4 = (f32[384,512]{1,0:T(8,128)}, f32[384,512]{1,0:T(8,128)}) conditional(s32[]{:T(128)} %convert_element_type.70, () %tuple.34, (pred[3072,384]{1,0:T(8,128)(4,1)}, bf16[3072,512]{1,0:T(8,128)(2,1)}, bf16[384,512]{1,0:T(8,128)(2,1)S(1)}, bf16[3072,512]{1,0:T(8,128)(2,1)}, bf16[384,512]{1,0:T(8,128)(2,1)}) %tuple.98), branch_computations={%region_15.16_spmd, %region_16.17_spmd} | conditional | flops 5011144704 | bytes 154140752 | solution.py:193
  270.2 4.7 copy.72
  275.1 16.2 %fusion.74 = f32[8,3072,384]{2,1,0:T(8,128)} fusion(bf16[3072,8,64]{0,2,1:T(8,128)(2,1)} %bitcast.75, bf16[384,8,64]{0,2,1:T(8,128)(2,1)S(1)} %bitcast.84), kind=kOutput, calls=%fused_computation.138 | convolution fusion | flops 1207959552 | bytes 41287680 | tf_op jit(solution)/shard_map/cond/branch_1_fun/rhd,chd->hrc/dot_general | solution.py:39
  291.3 4.7 copy.70
  296.0 0.9 copy.71
  296.9 30.0 %fusion.7 = f32[8,384,64]{1,2,0:T(8,128)} fusion(bf16[3072,8,64]{0,2,1:T(8,128)(2,1)} %bitcast.76, f32[8,3072,384]{2,1,0:T(8,128)} %fusion.74, pred[3072,384]{1,0:T(8,128)(4,1)} %get-tuple-element.37, bf16[3072,8,64]{0,2,1:T(8,128)(2,1)} %bitcast.78, bf16[384,8,64]{0,2,1:T(8,128)(2,1)} %bitcast.92), kind=kOutput, calls=%fused_computation.16 | convolution fusion | flops 2529165312 | bytes 46399488 | tf_op jit(solution)/shard_map/cond/branch_1_fun/hrc,rhd->chd/dot_general | solution.py:81
  326.9 2.3 copy.88
  329.2 18.5 %fusion.6 = f32[8,384,64]{1,2,0:T(8,128)} fusion(bf16[3072,8,64]{0,2,1:T(8,128)(2,1)} %bitcast.79, f32[8,3072,384]{2,1,0:T(8,128)} %fusion.74, pred[3072,384]{1,0:T(8,128)(4,1)S(1)} %copy-done.13), kind=kOutput, calls=%fused_computation.15 | convolution fusion | flops 1274019840 | bytes 42860544 | tf_op jit(solution)/shard_map/cond/branch_1_fun/hrc,rhd->chd/dot_general | solution.py:81
  347.7 2.3 copy.86
  350.3 3.5 fusion.26
  353.8 1.1 copy-done.9
  354.9 1.4 fusion.49
  356.4 2.8 pad_maximum_fusion
  359.2 2.5 fusion.65
  361.7 3.8 scatter_custom_fusion.1
  365.5 2.5 convert_element_type.74
  368.1 2.1 convert_element_type.75
  370.2 8.3 %all-to-all-start.2 = ((bf16[128,6,512]{2,1,0:T(8,128)(2,1)}), bf16[128,6,512]{2,1,0:T(8,128)(2,1)}, u32[]{:S(2)}, u32[]{:S(2)}) async-start(bf16[128,6,512]{2,1,0:T(8,128)(2,1)} %convert_element_type.75), calls=%async_computation.2 | async-start | bytes 2097152 | tf_op jit(solution)/shard_map/all_to_all | solution.py:230
  379.0 0.8 reduce.15
  380.0 2.4 fusion.27
  382.4 16.6 %all-to-all-done.2 = bf16[128,6,512]{2,1,0:T(8,128)(2,1)} async-done(((bf16[128,6,512]{2,1,0:T(8,128)(2,1)}), bf16[128,6,512]{2,1,0:T(8,128)(2,1)}, u32[]{:S(2)}, u32[]{:S(2)}) %all-to-all-start.2) | async-done | bytes 786464 | tf_op jit(solution)/shard_map/all_to_all | solution.py:230
  399.0 2.4 reshape.365
  401.4 8.3 %scatter_custom_fusion.2 = f32[512,512]{1,0:T(8,128)} fusion(s32[768]{0:T(1024)S(1)} %fusion.54, f32[768,512]{1,0:T(8,128)} %reshape.365, f32[]{:T(128)} %constant.119.clone.1), kind=kCustom, calls=%fused_computation.66 | custom fusion | flops 393216 | bytes 1049088 | tf_op jit(solution)/shard_map/scatter-add | solution.py:236
  409.7 1.4 multiply_reduce_fusion
  411.7 2.4 divide_subtract_fusion
  414.1 109.2 %all-reduce.4.cloned.1.call-done = f32[512,2560]{1,0:T(8,128)} async-done(((f32[512,2560]{1,0:T(8,128)}), f32[512,2560]{1,0:T(8,128)}) %all-reduce.4.cloned.1.call-update) | async-done | bytes 5242896
  523.2 1.5 dynamic-slice_multiply_fusion
  524.7 1.4 dynamic-slice_multiply_fusion.1
  (107 shorter events, 6.1 us)
Async XLA Ops:
  7.2 59.2 %copy-start = (bf16[512,2048]{1,0:T(8,128)(2,1)S(1)}, bf16[512,2048]{1,0:T(8,128)(2,1)}, u32[]{:S(2)}) copy-start(bf16[512,2048]{1,0:T(8,128)(2,1)} %param.19) | copy-start | bytes 6291460
  7.2 26.3 %copy-start.1 = (f32[512,512]{1,0:T(8,128)S(1)}, f32[512,512]{1,0:T(8,128)}, u32[]{:S(2)}) copy-start(f32[512,512]{1,0:T(8,128)} %param.14) | copy-start | bytes 3145732
  8.7 35.2 %copy-start.26 = (s32[384]{0:T(512)}, s32[384]{0:T(512)S(1)}, u32[]{:S(2)}) copy-start(s32[384]{0:T(512)S(1)} %compare_select_fusion.3) | copy-start | bytes 4612
  32.7 0.6 copy-start.15
  38.6 23.8 %all-to-all-start.1 = ((bf16[128,6,512]{2,1,0:T(8,128)(2,1)}), bf16[128,6,512]{2,1,0:T(8,128)(2,1)}, u32[]{:S(2)}, u32[]{:S(2)}) async-start(bf16[128,6,512]{2,1,0:T(8,128)(2,1)} %reshape.391), calls=%async_computation.1 | async-start | bytes 2097152 | tf_op jit(solution)/shard_map/all_to_all | solution.py:108
  43.9 52.2 %all-gather.5.cloned.1.call-start = ((), (), s32[]{:S(2)}) async-start(), calls=%async_computation.3 | async-start | bytes 3538944 | tf_op jit(solution)/shard_map/all_gather | solution.py:151
  65.9 3.3 copy-start.3
  66.1 3.2 copy-start.18
  66.4 2.9 copy-start.20
  69.2 1.1 copy-start.12
  69.2 3.7 copy-start.17
  69.3 3.9 copy-start.28
  71.4 54.0 %all-gather.7.cloned.1.call-start = ((), (), s32[]{:S(2)}) async-start(), calls=%async_computation.4 | async-start | bytes 3538944 | tf_op jit(solution)/shard_map/all_gather | solution.py:150
  72.2 197.9 %all-gather.11.cloned.1.call-start = ((), (), s32[]{:S(2)}) async-start(), calls=%async_computation.6 | async-start | bytes 3538944 | tf_op jit(solution)/shard_map/all_gather | solution.py:199
  72.9 197.2 %all-gather.9.cloned.1.call-start = ((), (), s32[]{:S(2)}) async-start(), calls=%async_computation.5 | async-start | bytes 3538944 | tf_op jit(solution)/shard_map/all_gather | solution.py:200
  130.3 4.7 copy-start.8
  155.6 111.8 %copy-start.5 = (f32[384,512]{1,0:T(8,128)}, f32[384,512]{1,0:T(8,128)S(1)}, u32[]{:S(2)}) copy-start(f32[384,512]{1,0:T(8,128)S(1)} %get-tuple-element.116) | copy-start | bytes 2359300
  155.6 111.8 %copy-start.22 = (f32[384]{0:T(512)}, f32[384]{0:T(512)S(1)}, u32[]{:S(2)}) copy-start(f32[384]{0:T(512)S(1)} %multiply_reduce_fusion.4) | copy-start | bytes 4612
  155.9 111.5 %copy-start.24 = (f32[384]{0:T(512)}, f32[384]{0:T(512)S(1)}, u32[]{:S(2)}) copy-start(f32[384]{0:T(512)S(1)} %add_sqrt_fusion) | copy-start | bytes 4612
  160.1 30.3 %copy-start.7 = (bf16[384,512]{1,0:T(8,128)(2,1)S(1)}, bf16[384,512]{1,0:T(8,128)(2,1)}, u32[]{:S(2)}) copy-start(bf16[384,512]{1,0:T(8,128)(2,1)} %get-tuple-element.136) | copy-start | bytes 1179652
  160.1 363.1 %all-reduce.4.cloned.1.call-start = ((), (), s32[]{:S(2)}) async-start(), calls=%async_computation.7 | async-start | bytes 10485760
  267.4 2.8 copy-start.10
  270.2 4.7 copy-start.11
  296.9 32.3 %copy-start.13 = (pred[3072,384]{1,0:T(8,128)(4,1)S(1)}, pred[3072,384]{1,0:T(8,128)(4,1)}, u32[]{:S(2)}) copy-start(pred[3072,384]{1,0:T(8,128)(4,1)} %get-tuple-element.37) | copy-start | bytes 3538948 | tf_op jit(solution)/shard_map/cond
  350.3 4.7 copy-start.4
  350.3 4.7 copy-start.19
  350.3 4.6 copy-start.21
  353.8 1.1 copy-start.9
  354.9 1.4 copy-start.14
  365.5 13.5 %copy-start.16 = (s32[128,1,6]{2,1,0:T(1,128)S(1)}, s32[128,1,6]{2,1,0:T(1,128)}, u32[]{:S(2)}) copy-start(s32[128,1,6]{2,1,0:T(1,128)} %copy-done.15) | copy-start | bytes 9220
  365.5 14.5 %copy-start.6 = (f32[384,512]{1,0:T(8,128)S(1)}, f32[384,512]{1,0:T(8,128)}, u32[]{:S(2)}) copy-start(f32[384,512]{1,0:T(8,128)} %copy-done.5) | copy-start | bytes 2359300
  365.5 14.5 %copy-start.23 = (f32[384]{0:T(512)S(1)}, f32[384]{0:T(512)}, u32[]{:S(2)}) copy-start(f32[384]{0:T(512)} %copy-done.22) | copy-start | bytes 4612
  365.5 14.5 %copy-start.25 = (f32[384]{0:T(512)S(1)}, f32[384]{0:T(512)}, u32[]{:S(2)}) copy-start(f32[384]{0:T(512)} %copy-done.24) | copy-start | bytes 4612
  370.2 28.8 %all-to-all-start.2 = ((bf16[128,6,512]{2,1,0:T(8,128)(2,1)}), bf16[128,6,512]{2,1,0:T(8,128)(2,1)}, u32[]{:S(2)}, u32[]{:S(2)}) async-start(bf16[128,6,512]{2,1,0:T(8,128)(2,1)} %convert_element_type.75), calls=%async_computation.2 | async-start | bytes 2097152 | tf_op jit(solution)/shard_map/all_to_all | solution.py:230
  382.4 28.7 %copy-start.27 = (f32[512]{0:T(512)S(1)}, f32[512]{0:T(512)}, u32[]{:S(2)}) copy-start(f32[512]{0:T(512)} %param.15) | copy-start | bytes 6148
  382.4 29.3 %copy-start.2 = (f32[512,512]{1,0:T(8,128)S(1)}, f32[512,512]{1,0:T(8,128)}, u32[]{:S(2)}) copy-start(f32[512,512]{1,0:T(8,128)} %param.14) | copy-start | bytes 3145732
Sparse Core Ops, SparseCore 0:
  71.6 24.4 all-gather.4
  97.8 27.6 all-gather.6
  127.1 27.6 all-gather.10
  160.3 27.4 all-gather.8
  359.3 163.8 all-reduce.3
where the time goes:
time: 542 us; the launch traced here: 533 us
  waiting for transfers between devices  188 us (35%)
  matrix products  143 us (26%)
  local copies, waits for them, and re-layouts  87.7 us (16%)
  other arithmetic  46.6 us (9%)
  blocking collectives  20.9 us (4%)
  loops' own time  17.4 us (3%)
  between operations  16 us (3%)
  starting transfers between devices  13.7 us (3%)
    unnamed x6, waiting for transfers between devices  111 us
    dot_general x2, matrix products, to_key(): jnp.einsum('hrc,rhd->chd', grad_scores, heads_of(query_rows), preferred_e...  48.5 us
    another operation x13, local copies, waits for them, and re-layouts  32.3 us
    dot_general x1, matrix products, to_query(): jnp.einsum('hrc,chd->rhd', grad_scores, heads_of(key_rows), preferred_ele...  29.4 us
    all_gather x1, waiting for transfers between devices, body(): value_rows = lax.all_gather(value_own, 'pair', axis=0, tiled=True)  29.3 us
    gather x1, local copies, waits for them, and re-layouts, queries_seen(): listed = present[query_pos // tokens, block_here]  25.3 us
    all_to_all x1, blocking collectives, body(): lax.all_to_all(request, ('dp', 'pair'), split_axis=0, concat_axis=0, tile...  20.9 us
    dot_general x1, matrix products, pair_forward(): jnp.einsum('hrc,chd->rhd', weights, heads_of(value_rows), preferred_eleme...  18.9 us
  transfers between devices with their start and end apart: 7, of which 5 were waited for; matrix products, arithmetic and copies ran while one was open for 31% of the time, Pallas kernels for 0%

commit v1 on v0

v1 whole, which is shorter than its diff:
```python
import functools
import math

import jax
import jax.numpy as jnp
from jax import lax
from jax.experimental import pallas as pl
from jax.experimental.pallas import tpu as pltpu
from jax.sharding import PartitionSpec as P

HEADS = 8
NORM_EPS = 1e-05
LEARN_RATE = 0.5
F32, BF16, I32 = jnp.float32, jnp.bfloat16, jnp.int32
VMEM = pltpu.VMEM
BIG = 62 * 1024 * 1024


def whole():
    return pl.BlockSpec(memory_space=pltpu.VMEM)


def params(**kw):
    return pltpu.CompilerParams(vmem_limit_bytes=BIG, **kw)


def dot(a, b):
    return lax.dot_general(a, b, (((1,), (0,)), ((), ())), preferred_element_type=F32)


def dot_t(a, b):
    return lax.dot_general(a, b, (((1,), (1,)), ((), ())), preferred_element_type=F32)


def iota(shape, axis):
    return lax.broadcasted_iota(I32, shape, axis)


def normalize(values):
    row_mean = jnp.mean(values, axis=-1, keepdims=True)
    centred = values - row_mean
    spread = jnp.sqrt(jnp.mean(centred * centred, axis=-1, keepdims=True) + NORM_EPS)
    return centred / spread, spread


def norm_back(grad_rows, normed, spread):
    first = jnp.mean(grad_rows, axis=-1, keepdims=True)
    second = jnp.mean(grad_rows * normed, axis=-1, keepdims=True)
    return (grad_rows - first - normed * second) / spread


def even_half(rows):
    lane = iota(rows.shape, 1) & 127
    return jnp.where(lane < 64, rows, jnp.zeros_like(rows))


def odd_half(rows):
    lane = iota(rows.shape, 1) & 127
    return jnp.where(lane < 64, jnp.zeros_like(rows), rows)


def route_kernel(rows_dev, row_ref, col_ref, seg_ref, pair_ref, req_ref, tr_ref, tc_ref, meta_ref, *, width):
    tokens = row_ref.shape[1]
    shards = req_ref.shape[0]
    shift = rows_dev.bit_length() - 1
    owner_r = row_ref[...] >> shift
    slot_r = (row_ref[...] & (rows_dev - 1)).astype(F32)
    owner_c = col_ref[...] >> shift
    same = owner_c == owner_r
    sub, lane = iota((tokens, tokens), 0), iota((tokens, tokens), 1)
    rank_c = jnp.sum(jnp.where(same & (lane < sub), 1.0, 0.0), axis=1, keepdims=True).astype(I32)
    rank_r = jnp.sum(jnp.where(same & (sub < lane), 1.0, 0.0), axis=0, keepdims=True).astype(I32)
    tr_ref[...] = owner_r * width + rank_r
    tc_ref[...] = owner_c * width + rank_c
    dest = iota((shards, tokens), 0) == owner_r
    place = iota((shards, 128), 1)
    req = jnp.zeros((shards, 128), F32)
    for k in range(2 * tokens // shards):
        picked = jnp.sum(jnp.where(dest & (rank_r == k), slot_r, 0.0), axis=1, keepdims=True)
        req = jnp.where(place == k, picked, req)
    req_ref[...] = req.astype(I32)
    own = lax.axis_index("pair")
    first, second = pair_ref[0:1, :], pair_ref[1:2, :]
    span = iota((8, first.shape[1]), 0)
    as_query = jnp.max(jnp.where((first == own) & (second == span), 1.0, 0.0), axis=1, keepdims=True)
    as_key = jnp.max(jnp.where((second == own) & (first == span), 1.0, 0.0), axis=1, keepdims=True)
    zeros = jnp.sum(jnp.where(seg_ref[...] == 0, 1.0, 0.0), axis=1, keepdims=True)
    at = iota((8, 128), 1)
    meta = jnp.where(at == 0, as_query, jnp.where(at == 1, as_key, jnp.where(at == 2, zeros, 0.0))).astype(I32)
    meta_ref[...] = jnp.where(at == 3, own, meta)


def slot_halves(slots):
    high = (slots >> 1).astype(F32).astype(BF16)
    low = (slots & 1).astype(F32).astype(BF16)
    return high, low


def find_kernel(slots_ref, table_ref, found_ref, *, width):
    shards = slots_ref.shape[0]
    rows_dev = table_ref.shape[0]
    count = shards * width
    spread = ((iota((count, shards), 0) // width) == iota((count, shards), 1)).astype(F32).astype(BF16)
    high, low = slot_halves(slots_ref[...])
    value = 2.0 * dot(spread, high) + dot(spread, low)
    mine = iota((count, 128), 1) == (iota((count, 128), 0) % width)
    slot = jnp.sum(jnp.where(mine, value, 0.0), axis=1, keepdims=True).astype(I32)
    pick = jnp.where(iota((count, rows_dev), 1) == slot, 1.0, 0.0).astype(BF16)
    found_ref[...] = dot(pick, table_ref[...].astype(BF16)).astype(BF16)


def project_kernel(fetched_ref, tc_ref, w_ref, x_ref, z_ref, u_ref, q_ref, kv_ref):
    count, width = fetched_ref.shape
    tokens = tc_ref.shape[0]
    pick = jnp.where(iota((tokens, count), 1) == tc_ref[...], 1.0, 0.0).astype(BF16)
    rows = dot(pick, fetched_ref[...])
    x_ref[...] = rows.astype(BF16)
    normed, _ = normalize(rows)
    low = normed.astype(BF16)
    outs = (u_ref.at[...], kv_ref.at[:, width:], q_ref.at[...], kv_ref.at[:, :width])
    for g in range(4):
        z = dot(low, w_ref[:, g * width : (g + 1) * width])
        z_ref[:, g * width : (g + 1) * width] = z
        half = 0.5 * z
        outs[g][...] = (half + half * jnp.tanh(half)).astype(BF16)


def visible(q_axis, size, q_block, k_block, zeros):
    q_pos = iota((size, size), q_axis) + q_block * size
    k_pos = iota((size, size), 1 - q_axis) + k_block * size
    least = jnp.where(q_pos >= zeros, zeros, 0)
    return jnp.where((k_pos >= least) & (k_pos <= q_pos), 1.0, 0.0)


def pair_live(meta_ref, row, lane, q_block, k_block, size):
    zeros = meta_ref[0, 2]
    apart = ((k_block + 1) * size <= zeros) & (q_block * size >= zeros)
    return (meta_ref[row, lane] == 1) & jnp.logical_not(apart)


def forward_kernel(
    meta_ref, q_ref, kv_ref, u_ref, x_ref, w_ref, og_ref, out_ref, da_ref, dhu_ref, gout_ref, qs, acc, mask
):
    j = pl.program_id(0)
    own = meta_ref[0, 3]
    size, width = q_ref.shape

    @pl.when(j == 0)
    def _():
        scaled = q_ref[...] * 0.0625
        qs[0] = even_half(scaled)
        qs[1] = odd_half(scaled)
        acc[...] = jnp.zeros_like(acc)

    @pl.when((j <= own) & pair_live(meta_ref, j, 0, own, j, size))
    def _():
        mask[...] = visible(0, size, own, j, meta_ref[0, 2])
        for s in range(width // 128):
            cols = slice(s * 128, s * 128 + 128)
            keys = kv_ref[:, cols]
            values = kv_ref[:, width + s * 128 : width + s * 128 + 128]
            weights = []
            for half in range(2):
                h = dot_t(qs[half, :, cols], keys)
                weights.append(((h + h * jnp.tanh(h)) * mask[...]).astype(BF16))
            both = jnp.concatenate([even_half(values), odd_half(values)], axis=0)
            acc[:, cols] += dot(jnp.concatenate(weights, axis=1), both)

    @pl.when(j == pl.num_programs(0) - 1)
    def _():
        normed, spread = normalize(acc[...])
        gate = u_ref[...].astype(F32)
        gated = (normed * gate).astype(BF16)
        out_ref[...] = (dot(gated, w_ref[...]) + x_ref[...].astype(F32)).astype(BF16)
        dy = dot_t(og_ref[...], w_ref[...])
        dhu_ref[...] = dy * normed
        da_ref[...] = norm_back(dy * gate, normed, spread).astype(BF16)
        gout_ref[...] = lax.dot_general(gated, og_ref[...], (((0,), (0,)), ((), ())), preferred_element_type=F32)


def query_kernel(meta_ref, q_ref, da_ref, kv_ref, dq_ref, qs, ds, mask):
    j = pl.program_id(0)
    own = meta_ref[0, 3]
    size, width = q_ref.shape

    @pl.when(j == 0)
    def _():
        scaled = q_ref[...] * 0.0625
        qs[0] = even_half(scaled)
        qs[1] = odd_half(scaled)
        scaled = da_ref[...] * 0.0625
        ds[0] = even_half(scaled)
        ds[1] = odd_half(scaled)
        dq_ref[...] = jnp.zeros_like(dq_ref)

    @pl.when((j <= own) & pair_live(meta_ref, j, 0, own, j, size))
    def _():
        mask[...] = visible(0, size, own, j, meta_ref[0, 2])
        for s in range(width // 128):
            cols = slice(s * 128, s * 128 + 128)
            keys = kv_ref[:, cols]
            values = kv_ref[:, width + s * 128 : width + s * 128 + 128]
            grads = []
            for half in range(2):
                h = dot_t(qs[half, :, cols], keys)
                t = jnp.tanh(h)
                slope = (1.0 + t) * (1.0 + h * (1.0 - t))
                grads.append((dot_t(ds[half, :, cols], values) * slope * mask[...]).astype(BF16))
            both = jnp.concatenate([even_half(keys), odd_half(keys)], axis=0)
            dq_ref[:, cols] += dot(jnp.concatenate(grads, axis=1), both)


def key_kernel(meta_ref, kv_ref, q_ref, da_ref, dk_ref, dv_ref, ks, vs, mask):
    i = pl.program_id(0)
    own = meta_ref[0, 3]
    size, width = q_ref.shape

    @pl.when(i == 0)
    def _():
        scaled = kv_ref[...] * 0.0625
        ks[0] = even_half(scaled[:, :width])
        ks[1] = odd_half(scaled[:, :width])
        vs[0] = even_half(scaled[:, width:])
        vs[1] = odd_half(scaled[:, width:])
        dk_ref[...] = jnp.zeros_like(dk_ref)
        dv_ref[...] = jnp.zeros_like(dv_ref)

    @pl.when((i >= own) & pair_live(meta_ref, i, 1, i, own, size))
    def _():
        mask[...] = visible(1, size, i, own, meta_ref[0, 2])
        for s in range(width // 128):
            cols = slice(s * 128, s * 128 + 128)
            queries = q_ref[:, cols]
            dafter = da_ref[:, cols]
            grads, weights = [], []
            for half in range(2):
                h = dot_t(ks[half, :, cols], queries)
                t = jnp.tanh(h)
                weights.append(((h + h * t) * mask[...]).astype(BF16))
                slope = (1.0 + t) * (1.0 + h * (1.0 - t))
                grads.append((dot_t(vs[half, :, cols], dafter) * slope * mask[...]).astype(BF16))
            q_both = jnp.concatenate([even_half(queries), odd_half(queries)], axis=0)
            a_both = jnp.concatenate([even_half(dafter), odd_half(dafter)], axis=0)
            dk_ref[:, cols] += dot(jnp.concatenate(grads, axis=1), q_both)
            dv_ref[:, cols] += dot(jnp.concatenate(weights, axis=1), a_both)


def finish_kernel(z_ref, dhu_ref, dv_ref, dq_ref, dk_ref, x_ref, w_ref, og_ref, tr_ref, gout_ref, grads_ref, send_ref):
    size, width = x_ref.shape
    normed, spread = normalize(x_ref[...].astype(F32))
    turned = jnp.transpose(normed).astype(BF16)
    dxn = jnp.zeros((size, width), F32)
    for g, grad in enumerate((dhu_ref, dv_ref, dq_ref, dk_ref)):
        cols = slice(g * width, (g + 1) * width)
        h = 0.5 * z_ref[:, cols]
        t = jnp.tanh(h)
        slope = 0.5 * (1.0 + t) * (1.0 + h * (1.0 - t))
        dz = (grad[...] * slope).astype(BF16)
        grads_ref[:, cols] = dot(turned, dz)
        dxn += dot_t(dz, w_ref[:, cols])
    grads_ref[:, 4 * width :] = gout_ref[...]
    dx = norm_back(dxn, normed, spread) + og_ref[...].astype(F32)
    count = send_ref.shape[0]
    pick = jnp.where(iota((count, size), 0) == tr_ref[...], 1.0, 0.0).astype(BF16)
    send_ref[...] = dot(pick, dx.astype(BF16)).astype(BF16)


def update_kernel(slots_ref, back_ref, table_ref, accum_ref, tnew_ref, anew_ref, *, width):
    shards = slots_ref.shape[0]
    rows_dev, model = table_ref.shape
    count = shards * width
    spread = ((iota((shards, count), 1) // width) == iota((shards, count), 0)).astype(F32).astype(BF16)
    high, low = slot_halves(slots_ref[...])
    turn = lambda a: lax.dot_general(a, spread, (((0,), (0,)), ((), ())), preferred_element_type=F32)
    value = 2.0 * turn(high) + turn(low)
    mine = iota((128, count), 0) == (iota((128, count), 1) % width)
    slot = jnp.sum(jnp.where(mine, value, 0.0), axis=0, keepdims=True).astype(I32)
    pick = jnp.where(iota((rows_dev, count), 0) == slot, 1.0, 0.0).astype(BF16)
    total = dot(pick, back_ref[...])
    square = jnp.mean(total * total, axis=1, keepdims=True)
    eye = iota((rows_dev, rows_dev), 0) == iota((rows_dev, rows_dev), 1)
    accum = jnp.sum(jnp.where(eye, accum_ref[...], 0.0), axis=1, keepdims=True) + square
    anew_ref[...] = jnp.sum(jnp.where(eye, accum, 0.0), axis=0, keepdims=True)
    tnew_ref[...] = table_ref[...] - LEARN_RATE * total / jnp.sqrt(accum)


def shape(dims, dtype):
    return jax.ShapeDtypeStruct(dims, dtype)


def cost(flops, moved):
    return pl.CostEstimate(flops=flops, bytes_accessed=moved, transcendentals=0)


def body(table, accum, item_row, segments, pairs, w_in, w_out, out_grad):
    tokens = item_row.shape[0]
    rows_dev, model = table.shape
    shards = lax.axis_size(("dp", "pair"))
    span = lax.axis_size("pair")
    width = -(-(2 * tokens // shards) // 8) * 8
    count = shards * width
    everyone = ("dp", "pair")

    call = pl.pallas_call(
        functools.partial(route_kernel, rows_dev, width=width),
        out_shape=(
            shape((shards, 128), I32),
            shape((1, tokens), I32),
            shape((tokens, 1), I32),
            shape((8, 128), I32),
        ),
        in_specs=[whole()] * 4,
        out_specs=[whole()] * 4,
        compiler_params=params(),
    )
    request, target_r, target_c, meta = call(
        item_row.reshape(1, tokens), item_row.reshape(tokens, 1), segments, pairs[0].T
    )
    asked = lax.all_to_all(request[:, :width], everyone, split_axis=0, concat_axis=0, tiled=True)
    slots = jnp.pad(asked, ((0, 0), (0, 128 - width)))
    found = pl.pallas_call(
        functools.partial(find_kernel, width=width),
        out_shape=shape((count, model), BF16),
        in_specs=[whole()] * 2,
        out_specs=whole(),
        compiler_params=params(),
    )(slots, table)
    fetched = lax.all_to_all(
        found.reshape(shards, width, model), everyone, split_axis=0, concat_axis=0, tiled=True
    ).reshape(count, model)
    x, z, u, q, kv = pl.pallas_call(
        project_kernel,
        out_shape=(
            shape((tokens, model), BF16),
            shape((tokens, 4 * model), F32),
            shape((tokens, model), BF16),
            shape((tokens, model), BF16),
            shape((tokens, 2 * model), BF16),
        ),
        in_specs=[whole()] * 3,
        out_specs=[whole()] * 5,
        compiler_params=params(),
    )(fetched, target_c, w_in)

    kv_all = lax.all_gather(kv, "pair", axis=0, tiled=True)
    q_all = lax.all_gather(q, "pair", axis=0, tiled=True)

    fixed = lambda cols: pl.BlockSpec((tokens, cols), lambda i, m: (0, 0))
    square = lambda rows, cols: pl.BlockSpec((rows, cols), lambda i, m: (0, 0))
    low_half = lambda cols: pl.BlockSpec((tokens, cols), lambda i, m: (jnp.minimum(i, m[0, 3]), 0))
    high_half = lambda cols: pl.BlockSpec((tokens, cols), lambda i, m: (jnp.maximum(i, m[0, 3]), 0))
    halves = VMEM((2, tokens, model), BF16)
    grid_spec = lambda ins, outs, scratch: pltpu.PrefetchScalarGridSpec(
        num_scalar_prefetch=1, grid=(span,), in_specs=ins, out_specs=outs, scratch_shapes=scratch
    )
    pair_flops = 2 * tokens * tokens * model * span
    layer_out, da, dhu, gout = pl.pallas_call(
        forward_kernel,
        out_shape=(
            shape((tokens, model), BF16),
            shape((tokens, model), BF16),
            shape((tokens, model), F32),
            shape((model, model), F32),
        ),
        grid_spec=grid_spec(
            [fixed(model), low_half(2 * model), fixed(model), fixed(model), square(model, model), fixed(model)],
            [fixed(model), fixed(model), fixed(model), square(model, model)],
            [halves, VMEM((tokens, model), F32), VMEM((tokens, tokens), F32)],
        ),
        compiler_params=params(),
        cost_estimate=cost(8 * pair_flops, 6 * 2**20),
    )(meta, q, kv_all, u, x, w_out, out_grad)

    da_all = lax.all_gather(da, "pair", axis=0, tiled=True)
    dq = pl.pallas_call(
        query_kernel,
        out_shape=shape((tokens, model), F32),
        grid_spec=grid_spec(
            [fixed(model), fixed(model), low_half(2 * model)],
            fixed(model),
            [halves, halves, VMEM((tokens, tokens), F32)],
        ),
        compiler_params=params(),
        cost_estimate=cost(12 * pair_flops, 6 * 2**20),
    )(meta, q, da, kv_all)
    dk, dv = pl.pallas_call(
        key_kernel,
        out_shape=(shape((tokens, model), F32), shape((tokens, model), F32)),
        grid_spec=grid_spec(
            [fixed(2 * model), high_half(model), high_half(model)],
            [fixed(model), fixed(model)],
            [halves, halves, VMEM((tokens, tokens), F32)],
        ),
        compiler_params=params(),
        cost_estimate=cost(16 * pair_flops, 6 * 2**20),
    )(meta, kv, q_all, da_all)

    grads, send = pl.pallas_call(
        finish_kernel,
        out_shape=(shape((model, 5 * model), F32), shape((count, model), BF16)),
        in_specs=[whole()] * 10,
        out_specs=[whole()] * 2,
        compiler_params=params(),
    )(z, dhu, dv, dq, dk, x, w_in, out_grad, target_r, gout)
    combined = lax.psum_scatter(grads, "dp", scatter_dimension=0, tiled=True)
    combined = lax.psum_scatter(combined, "pair", scatter_dimension=0, tiled=True)
    factor = 1.0 / math.sqrt(tokens * shards)
    back = lax.all_to_all(
        send.reshape(shards, width, model), everyone, split_axis=0, concat_axis=0, tiled=True
    ).reshape(count, model)
    table_new, accum_new = pl.pallas_call(
        functools.partial(update_kernel, width=width),
        out_shape=(shape((rows_dev, model), F32), shape((1, rows_dev), F32)),
        in_specs=[whole()] * 4,
        out_specs=[whole()] * 2,
        compiler_params=params(),
    )(slots, back, table, accum.reshape(1, rows_dev))
    return (
        layer_out,
        table_new,
        accum_new.reshape(rows_dev),
        combined[:, : 4 * model] * factor,
        combined[:, 4 * model :] * factor,
    )


def solution(mesh):
    both = ("dp", "pair")
    return jax.shard_map(
        body,
        mesh=mesh,
        in_specs=(
            P(both, None),
            P(both),
            P(both),
            P("dp", None),
            P("dp", None, None),
            P(),
            P(),
            P(both, None),
        ),
        out_specs=(P(both, None), P(both, None), P(both), P(both, None), P(both, None)),
        check_vma=False,
    )
```

time: 542 us -> 362 us (0.67); the launches traced: 533 us -> 359 us
  matrix products: 143 us -> 0 us
  local copies, waits for them, and re-layouts: 87.7 us -> 4.9 us
  Pallas kernels: 0 us -> 58.9 us
  other arithmetic: 46.6 us -> 2.85 us
  blocking collectives: 20.9 us -> 45.1 us
  waiting for transfers between devices: 188 us -> 212 us
  loops' own time: 17.4 us -> 0 us
  starting transfers between devices: 13.7 us -> 20.6 us
    dot_general x12 -> x0, matrix products: 143 us -> none  [the longest x2 48.5 us: to_key(): jnp.einsum('hrc,rhd->chd', grad_scores, heads_of(query_rows), preferred_e...]
    reduce_scatter x0 -> x1, waiting for transfers between devices: none -> 77.9 us  [body(): combined = lax.psum_scatter(grads, 'dp', scatter_dimension=0, tiled=True)]
    pallas_call x0 -> x8, Pallas kernels: none -> 58.9 us  [the longest x1 16.3 us: body(): pl.pallas_call(key_kernel, out_shape=(shape((tokens, model), F32), shape(...]
    unnamed x6, waiting for transfers between devices: 111 us -> 56.4 us
    all_gather x4 -> x3, waiting for transfers between devices: 42 us -> 78.1 us  [the longest x1 37 us: body(): kv_all = lax.all_gather(kv, 'pair', axis=0, tiled=True)]
    all_to_all x2 -> x1, waiting for transfers between devices: 35.1 us -> 0.01 us  [body(): lax.all_to_all(send.reshape(shards, width, model), everyone, split_axis=0...]
    another operation x13 -> x0, local copies, waits for them, and re-layouts: 32.3 us -> none
    gather x4 -> x0, local copies, waits for them, and re-layouts: 31 us -> none  [the longest x1 25.3 us: queries_seen(): listed = present[query_pos // tokens, block_here]]
  transfers between devices with their start and end apart: 7 -> 6, of which waited for: 5 -> 5; matrix products, arithmetic and copies ran while one was open for 31% -> 0% of each run, Pallas kernels for 0% -> 6%
where the time goes in v1:
time: 362 us; the launch traced here: 359 us
  waiting for transfers between devices  212 us (59%)
  Pallas kernels  58.9 us (16%)
  blocking collectives  45.1 us (12%)
  starting transfers between devices  20.6 us (6%)
  between operations  14.5 us (4%)
  local copies, waits for them, and re-layouts  4.9 us (1%)
    reduce_scatter x1, waiting for transfers between devices, body(): combined = lax.psum_scatter(grads, 'dp', scatter_dimension=0, tiled=True)  77.9 us
    unnamed x6, waiting for transfers between devices  56.4 us
    all_gather x1, waiting for transfers between devices, body(): kv_all = lax.all_gather(kv, 'pair', axis=0, tiled=True)  37 us
    all_gather x1, waiting for transfers between devices, body(): da_all = lax.all_gather(da, 'pair', axis=0, tiled=True)  29.3 us
    all_to_all x1, blocking collectives, body(): lax.all_to_all(found.reshape(shards, width, model), everyone, split_axis=...  24 us
    all_to_all x1, blocking collectives, body(): lax.all_to_all(request[:, :width], everyone, split_axis=0, concat_axis=0,...  21.1 us
    all_to_all x1, starting transfers between devices, body(): lax.all_to_all(send.reshape(shards, width, model), everyone, split_axis=0...  20.2 us
    pallas_call x1, Pallas kernels, body(): pl.pallas_call(key_kernel, out_shape=(shape((tokens, model), F32), shape(...  16.3 us
  transfers between devices with their start and end apart: 6, of which 5 were waited for; matrix products, arithmetic and copies ran while one was open for 0% of the time, Pallas kernels for 6%

profile of v1, /device:TPU:1, one launch (start us, length us, event | category | flops | bytes accessed | tf_op | source)
XLA Modules:
  0.0 359.2 jit_solution(9488716406011760105)
XLA Ops:
  7.2 0.0 all-gather.4.cloned.1.call-start
  7.2 1.5 reshape.45.col_ref
  8.7 1.2 reshape.36.row_ref
  9.9 2.0 shard_map.119
  11.9 21.1 %all_to_all.22 = s32[128,1,8]{2,1,0:T(1,128)S(1)} all-to-all(s32[128,1,8]{2,1,0:T(1,128)} %bitcast.19), channel_id=1, replica_groups=mesh['dp'=16,'pair'=8] {'dp','pair'}, dimensions={0} | all-to-all | bytes 8192 | tf_op jit(solution)/shard_map/all_to_all | solution.py:319
  33.0 0.6 pad.4.slots_ref
  33.6 3.2 shard_map.120
  36.7 24.0 %all_to_all.23 = bf16[128,8,512]{2,1,0:T(8,128)(2,1)} all-to-all(bf16[128,8,512]{2,1,0:T(8,128)(2,1)} %bitcast.17), channel_id=1, replica_groups=mesh['dp'=16,'pair'=8] {'dp','pair'}, dimensions={0} | all-to-all | bytes 2097152 | tf_op jit(solution)/shard_map/all_to_all | solution.py:328
  60.8 6.1 %shard_map.121 = (bf16[384,512]{1,0:T(8,128)(2,1)}, f32[384,2048]{1,0:T(8,128)}, bf16[384,512]{1,0:T(8,128)(2,1)}, bf16[384,512]{1,0:T(8,128)(2,1)}, bf16[384,1024]{1,0:T(8,128)(2,1)}) custom-call(bf16[1024,512]{1,0:T(8,128)(2,1)} %bitcast.15, s32[384,1]{1,0:T(8,128)} %get-tuple-element.26.tc_ref, bf16[512,2048]{1,0:T(8,128)(2,1)} %w_ref.5), custom_call_target="tpu_custom_call" | custom-call | tf_op jit(solution)/shard_map/pallas_call | solution.py:331
  66.9 0.0 all-gather.4.cloned.1.call-update
  66.9 0.0 all-gather.6.cloned.1.call-start
  66.9 0.7 all-gather.6.cloned.1.call-update
  67.6 0.0 all-gather.8.cloned.1.call-start
  67.7 37.0 %all-gather.4.cloned.1.call-done.kv_ref = bf16[3072,1024]{1,0:T(8,128)(2,1)} async-done(((bf16[384,1024]{1,0:T(8,128)(2,1)}), bf16[3072,1024]{1,0:T(8,128)(2,1)}) %all-gather.4.cloned.1.call-update) | async-done | bytes 6291472 | tf_op jit(solution)/shard_map/all_gather | solution.py:345
  104.7 8.9 %shard_map.122 = (bf16[384,512]{1,0:T(8,128)(2,1)}, bf16[384,512]{1,0:T(8,128)(2,1)}, f32[384,512]{1,0:T(8,128)}, f32[512,512]{1,0:T(8,128)}) custom-call(s32[8,128]{1,0:T(8,128)} %get-tuple-element.24.meta_ref, bf16[384,512]{1,0:T(8,128)(2,1)} %get-tuple-element.27.q_ref, bf16[3072,1024]{1,0:T(8,128)(2,1)} %all-gather.4.cloned.1.call-done.kv_ref, ...), custom_call_target="tpu_custom_call" | custom-call | flops 9663676416 | bytes 6291456 | tf_op jit(solution)/shard_map/pallas_call | solution.py:357
  113.6 0.0 all-gather.8.cloned.1.call-update
  113.6 0.2 reduce-scatter.2.cloned.1.call-start
  113.9 8.6 %shard_map.124.dq_ref = f32[384,512]{1,0:T(8,128)} custom-call(s32[8,128]{1,0:T(8,128)} %get-tuple-element.24.meta_ref, bf16[384,512]{1,0:T(8,128)(2,1)} %get-tuple-element.27.q_ref, bf16[384,512]{1,0:T(8,128)(2,1)} %get-tuple-element.34.da_ref, bf16[3072,1024]{1,0:T(8,128)(2,1)} %all-gather.4.cloned.1.call-done.kv_ref), custom_call_target="tpu_custom_call" | custom-call | flops 14495514624 | bytes 6291456 | tf_op jit(solution)/shard_map/pallas_call | solution.py:375
  122.5 11.7 %all-gather.6.cloned.1.call-done.q_ref = bf16[3072,512]{1,0:T(8,128)(2,1)} async-done(((bf16[384,512]{1,0:T(8,128)(2,1)}), bf16[3072,512]{1,0:T(8,128)(2,1)}) %all-gather.6.cloned.1.call-update) | async-done | bytes 3145744 | tf_op jit(solution)/shard_map/all_gather | solution.py:346
  134.2 29.3 %all-gather.8.cloned.1.call-done.da_ref = bf16[3072,512]{1,0:T(8,128)(2,1)} async-done(((bf16[384,512]{1,0:T(8,128)(2,1)}), bf16[3072,512]{1,0:T(8,128)(2,1)}) %all-gather.8.cloned.1.call-update) | async-done | bytes 3145744 | tf_op jit(solution)/shard_map/all_gather | solution.py:374
  163.5 16.3 %shard_map.123 = (f32[384,512]{1,0:T(8,128)}, f32[384,512]{1,0:T(8,128)}) custom-call(s32[8,128]{1,0:T(8,128)} %get-tuple-element.24.meta_ref, bf16[384,1024]{1,0:T(8,128)(2,1)} %get-tuple-element.28.kv_ref, bf16[3072,512]{1,0:T(8,128)(2,1)} %all-gather.6.cloned.1.call-done.q_ref, bf16[3072,512]{1,0:T(8,128)(2,1)} %all-gather.8.cloned.1.call-done.da_ref), custom_call_target="tpu_custom_call" | custom-call | flops 19327352832 | bytes 6291456 | tf_op jit(solution)/shard_map/pallas_call | solution.py:386
  179.8 10.2 %shard_map.125 = (f32[512,2560]{1,0:T(8,128)}, bf16[1024,512]{1,0:T(8,128)(2,1)}) custom-call(f32[384,2048]{1,0:T(8,128)} %get-tuple-element.32.z_ref, f32[384,512]{1,0:T(8,128)} %get-tuple-element.33.dhu_ref, f32[384,512]{1,0:T(8,128)} %get-tuple-element.35.dv_ref, f32[384,512]{1,0:T(8,128)} %shard_map.124.dq_ref, f32[384,512]{1,0:T(8,128)} %get-tuple-element.36.dk_ref, ...), custom_call_target="tpu_custom_call" | custom-call | tf_op jit(solution)/shard_map/pallas_call | solution.py:398
  190.0 0.0 copy-start.1
  190.0 0.0 reduce-scatter.2.cloned.1.call-update
  190.1 20.2 %all-to-all-start.2 = ((bf16[128,8,512]{2,1,0:T(8,128)(2,1)}), bf16[128,8,512]{2,1,0:T(8,128)(2,1)S(1)}, u32[]{:S(2)}, u32[]{:S(2)}) async-start(bf16[128,8,512]{2,1,0:T(8,128)(2,1)} %bitcast.7), calls=%async_computation.2 | async-start | bytes 2097152 | tf_op jit(solution)/shard_map/all_to_all | solution.py:408
  210.3 0.0 all-reduce.4.cloned.1.call-start
  210.3 77.9 %reduce-scatter.2.cloned.1.call-done = f32[32,2560]{1,0:T(8,128)} async-done(((f32[512,2560]{1,0:T(8,128)}), f32[32,2560]{1,0:T(8,128)}) %reduce-scatter.2.cloned.1.call-update) | async-done | bytes 327696 | tf_op jit(solution)/shard_map/reduce_scatter | solution.py:405
  288.3 0.0 all-reduce.4.cloned.1.call-update
  288.3 0.0 copy-done.1
  288.3 0.6 dynamic-slice
  289.5 0.0 all-to-all-done.2
  289.5 0.0 copy-start
  289.5 1.0 copy-done
  290.5 3.7 %shard_map.126 = (f32[512,512]{1,0:T(8,128)}, f32[1,512]{1,0:T(1,128)}) custom-call(s32[128,128]{1,0:T(8,128)} %pad.4.slots_ref, bf16[1024,512]{1,0:T(8,128)(2,1)} %bitcast.16, f32[512,512]{1,0:T(8,128)} %table_ref.3, f32[1,512]{1,0:T(1,128)} %bitcast.20), custom_call_target="tpu_custom_call" | custom-call | tf_op jit(solution)/shard_map/pallas_call | solution.py:411
  294.2 55.6 %all-reduce.4.cloned.1.call-done = f32[32,2560]{1,0:T(8,128)} async-done(((f32[32,2560]{1,0:T(8,128)}), f32[32,2560]{1,0:T(8,128)}) %all-reduce.4.cloned.1.call-update) | async-done | bytes 327696
  349.8 1.5 dynamic-slice_multiply_fusion
  351.3 1.4 dynamic-slice_multiply_fusion.1
Async XLA Ops:
  7.2 97.5 %all-gather.4.cloned.1.call-start = ((), (), s32[]{:S(2)}) async-start(), calls=%async_computation.4 | async-start | bytes 7077888 | tf_op jit(solution)/shard_map/all_gather | solution.py:345
  66.9 67.3 %all-gather.6.cloned.1.call-start = ((), (), s32[]{:S(2)}) async-start(), calls=%async_computation.5 | async-start | bytes 3538944 | tf_op jit(solution)/shard_map/all_gather | solution.py:346
  67.6 95.9 %all-gather.8.cloned.1.call-start = ((), (), s32[]{:S(2)}) async-start(), calls=%async_computation.6 | async-start | bytes 3538944 | tf_op jit(solution)/shard_map/all_gather | solution.py:374
  113.6 174.6 %reduce-scatter.2.cloned.1.call-start = ((), (), s32[]{:S(2)}) async-start(), calls=%async_computation.7 | async-start | bytes 5570560 | tf_op jit(solution)/shard_map/reduce_scatter | solution.py:405
  190.0 98.3 %copy-start.1 = (u32[128]{0:T(128)S(1)}, u32[128]{0:T(128)}, u32[]{:S(2)}) copy-start(u32[128]{0:T(128)} %constant.11) | copy-start | bytes 1540
  190.1 99.5 %all-to-all-start.2 = ((bf16[128,8,512]{2,1,0:T(8,128)(2,1)}), bf16[128,8,512]{2,1,0:T(8,128)(2,1)S(1)}, u32[]{:S(2)}, u32[]{:S(2)}) async-start(bf16[128,8,512]{2,1,0:T(8,128)(2,1)} %bitcast.7), calls=%async_computation.2 | async-start | bytes 2097152 | tf_op jit(solution)/shard_map/all_to_all | solution.py:408
  210.3 139.6 %all-reduce.4.cloned.1.call-start = ((), (), s32[]{:S(2)}) async-start(), calls=%async_computation.8 | async-start | bytes 655360
  289.5 1.0 copy-start
Sparse Core Ops, SparseCore 0:
  67.0 37.6 all-gather.3
  106.4 27.7 all-gather.5
  135.9 27.6 all-gather.7
  190.2 98.0 reduce-scatter.1
  290.4 59.3 all-reduce.3

commit v2 on v1

--- a/solution.py
+++ b/solution.py
@@ -13,6 +13,7 @@
 LEARN_RATE = 0.5
 F32, BF16, I32 = jnp.float32, jnp.bfloat16, jnp.int32
 VMEM = pltpu.VMEM
+MESH = pl.DeviceIdType.MESH
 BIG = 62 * 1024 * 1024
 
 
@@ -245,27 +246,135 @@
             dv_ref[:, cols] += dot(jnp.concatenate(weights, axis=1), a_both)
 
 
-def finish_kernel(z_ref, dhu_ref, dv_ref, dq_ref, dk_ref, x_ref, w_ref, og_ref, tr_ref, gout_ref, grads_ref, send_ref):
+def finish_kernel(
+    z_ref, dhu_ref, dv_ref, dq_ref, dk_ref, x_ref, w_ref, og_ref, tr_ref, gout_ref, grads_ref, send_ref, hold, *, rows
+):
     size, width = x_ref.shape
     normed, spread = normalize(x_ref[...].astype(F32))
     turned = jnp.transpose(normed).astype(BF16)
     dxn = jnp.zeros((size, width), F32)
+
+    def place(upper, lower, at):
+        count, cols = upper.shape
+        top = (iota((count, cols), 0) % (2 * rows)) < rows
+        first = jnp.where(top, upper, pltpu.roll(lower, rows, 0))
+        second = jnp.where(top, pltpu.roll(upper, count - rows, 0), lower)
+        whole_shape = (count // (2 * rows), 2 * rows, cols)
+        grads_ref[0, :, :, at : at + cols] = first.reshape(whole_shape)
+        grads_ref[1, :, :, at : at + cols] = second.reshape(whole_shape)
+
     for g, grad in enumerate((dhu_ref, dv_ref, dq_ref, dk_ref)):
         cols = slice(g * width, (g + 1) * width)
         h = 0.5 * z_ref[:, cols]
         t = jnp.tanh(h)
         slope = 0.5 * (1.0 + t) * (1.0 + h * (1.0 - t))
         dz = (grad[...] * slope).astype(BF16)
-        grads_ref[:, cols] = dot(turned, dz)
+        part = dot(turned, dz)
+        if g == 0:
+            hold[...] = part
+        elif g == 1:
+            place(part, gout_ref[...], width)
+        elif g == 2:
+            place(part[:, : width // 2], part[:, width // 2 :], 2 * width)
+        else:
+            place(hold[...], part, 0)
         dxn += dot_t(dz, w_ref[:, cols])
-    grads_ref[:, 4 * width :] = gout_ref[...]
     dx = norm_back(dxn, normed, spread) + og_ref[...].astype(F32)
     count = send_ref.shape[0]
     pick = jnp.where(iota((count, size), 0) == tr_ref[...], 1.0, 0.0).astype(BF16)
     send_ref[...] = dot(pick, dx.astype(BF16)).astype(BF16)
 
 
-def update_kernel(slots_ref, back_ref, table_ref, accum_ref, tnew_ref, anew_ref, *, width):
+def partner(k, groups, span):
+    g, p = lax.axis_index("dp"), lax.axis_index("pair")
+    chips, side = span // 2, math.isqrt(groups)
+    to_p = ((p // 2 + (k // 2) % chips) % chips) * 2 + (p % 2 + k % 2) % 2
+    shift = k // span
+    to_g = ((g // side + shift // side) % side) * side + (g % side + shift % side) % side
+    return to_g, to_p
+
+
+def greet(groups, span):
+    barrier = pltpu.get_barrier_semaphore()
+
+    def hello(k, carry):
+        pl.semaphore_signal(barrier, inc=1, device_id=partner(k, groups, span), device_id_type=MESH)
+        return carry
+
+    lax.fori_loop(1, groups * span, hello, 0)
+    pl.semaphore_wait(barrier, groups * span - 1)
+
+
+def drain(ref, count, sem):
+    part = ref.at[pl.ds(0, count)]
+    pltpu.make_async_copy(part, part, sem).wait()
+
+
+def tail_kernel(rows_ref, grads_ref, back_ref, parts_ref, got, part, sems, *, groups, span):
+    total = groups * span
+    g, p = lax.axis_index("dp"), lax.axis_index("pair")
+    me, core = g * span + p, p % 2
+    chip, chips = me // 2, total // 2
+    own = pltpu.make_async_copy(rows_ref.at[me], back_ref.at[me], sems.at[0])
+    own.start()
+    greet(groups, span)
+    swap = pltpu.make_async_remote_copy(
+        src_ref=grads_ref.at[1 - core],
+        dst_ref=got,
+        send_sem=sems.at[1],
+        recv_sem=sems.at[2],
+        device_id=(g, p + 1 - 2 * core),
+        device_id_type=MESH,
+    )
+    swap.start()
+
+    def push_rows(k, carry):
+        to_g, to_p = partner(k, groups, span)
+        pltpu.make_async_remote_copy(
+            src_ref=rows_ref.at[to_g * span + to_p],
+            dst_ref=back_ref.at[me],
+            send_sem=sems.at[3],
+            recv_sem=sems.at[4],
+            device_id=(to_g, to_p),
+            device_id_type=MESH,
+        ).start()
+        return carry
+
+    lax.fori_loop(1, total, push_rows, 0)
+    swap.wait()
+
+    def add(m, carry):
+        part[m] = (grads_ref[core, m] + got[m]).astype(BF16)
+        return carry
+
+    lax.fori_loop(0, chips, add, 0)
+    mine = pltpu.make_async_copy(part.at[chip], parts_ref.at[chip], sems.at[5])
+    mine.start()
+
+    def push_part(k, carry):
+        to_g, to_p = partner(2 * k, groups, span)
+        pltpu.make_async_remote_copy(
+            src_ref=part.at[(to_g * span + to_p) // 2],
+            dst_ref=parts_ref.at[chip],
+            send_sem=sems.at[6],
+            recv_sem=sems.at[7],
+            device_id=(to_g, to_p),
+            device_id_type=MESH,
+        ).start()
+        return carry
+
+    lax.fori_loop(1, chips, push_part, 0)
+    own.wait()
+    mine.wait()
+    drain(back_ref, total - 1, sems.at[3])
+    drain(back_ref, total - 1, sems.at[4])
+    drain(parts_ref, chips - 1, sems.at[6])
+    drain(parts_ref, chips - 1, sems.at[7])
+
+
+def update_kernel(
+    slots_ref, back_ref, table_ref, accum_ref, parts_ref, tnew_ref, anew_ref, gin_ref, gout_ref, *, width, factor
+):
     shards = slots_ref.shape[0]
     rows_dev, model = table_ref.shape
     count = shards * width
@@ -283,6 +392,19 @@
     anew_ref[...] = jnp.sum(jnp.where(eye, accum, 0.0), axis=0, keepdims=True)
     tnew_ref[...] = table_ref[...] - LEARN_RATE * total / jnp.sqrt(accum)
 
+    def add(m, summed):
+        return summed + parts_ref[m].astype(F32)
+
+    summed = lax.fori_loop(0, parts_ref.shape[0], add, jnp.zeros(parts_ref.shape[1:], F32)) * factor
+    rows = gin_ref.shape[0]
+    upper, lower = summed[:rows], summed[rows:]
+    gin_ref[:, :model] = upper[:, :model]
+    gin_ref[:, model : 2 * model] = upper[:, model : 2 * model]
+    gin_ref[:, 2 * model : 2 * model + model // 2] = upper[:, 2 * model :]
+    gin_ref[:, 2 * model + model // 2 : 3 * model] = lower[:, 2 * model :]
+    gin_ref[:, 3 * model :] = lower[:, :model]
+    gout_ref[...] = lower[:, model : 2 * model]
+
 
 def shape(dims, dtype):
     return jax.ShapeDtypeStruct(dims, dtype)
@@ -395,33 +517,41 @@
         cost_estimate=cost(16 * pair_flops, 6 * 2**20),
     )(meta, kv, q_all, da_all)
 
+    rows = model // shards
+    chunk = (2 * rows, 5 * model // 2)
     grads, send = pl.pallas_call(
-        finish_kernel,
-        out_shape=(shape((model, 5 * model), F32), shape((count, model), BF16)),
+        functools.partial(finish_kernel, rows=rows),
+        out_shape=(shape((2, shards // 2) + chunk, F32), shape((count, model), BF16)),
         in_specs=[whole()] * 10,
         out_specs=[whole()] * 2,
+        scratch_shapes=[VMEM((model, model), F32)],
         compiler_params=params(),
     )(z, dhu, dv, dq, dk, x, w_in, out_grad, target_r, gout)
-    combined = lax.psum_scatter(grads, "dp", scatter_dimension=0, tiled=True)
-    combined = lax.psum_scatter(combined, "pair", scatter_dimension=0, tiled=True)
-    factor = 1.0 / math.sqrt(tokens * shards)
-    back = lax.all_to_all(
-        send.reshape(shards, width, model), everyone, split_axis=0, concat_axis=0, tiled=True
-    ).reshape(count, model)
-    table_new, accum_new = pl.pallas_call(
-        functools.partial(update_kernel, width=width),
-        out_shape=(shape((rows_dev, model), F32), shape((1, rows_dev), F32)),
-        in_specs=[whole()] * 4,
+    back, parts = pl.pallas_call(
+        functools.partial(tail_kernel, groups=shards // span, span=span),
+        out_shape=(shape((shards, width, model), BF16), shape((shards // 2,) + chunk, BF16)),
+        in_specs=[whole()] * 2,
         out_specs=[whole()] * 2,
-        compiler_params=params(),
-    )(slots, back, table, accum.reshape(1, rows_dev))
-    return (
-        layer_out,
-        table_new,
-        accum_new.reshape(rows_dev),
-        combined[:, : 4 * model] * factor,
-        combined[:, 4 * model :] * factor,
-    )
+        scratch_shapes=[
+            VMEM((shards // 2,) + chunk, F32),
+            VMEM((shards // 2,) + chunk, BF16),
+            pltpu.SemaphoreType.DMA((8,)),
+        ],
+        compiler_params=params(collective_id=0, has_side_effects=True),
+    )(send.reshape(shards, width, model), grads)
+    table_new, accum_new, grad_in, grad_out = pl.pallas_call(
+        functools.partial(update_kernel, width=width, factor=1.0 / math.sqrt(tokens * shards)),
+        out_shape=(
+            shape((rows_dev, model), F32),
+            shape((1, rows_dev), F32),
+            shape((rows, 4 * model), F32),
+            shape((rows, model), F32),
+        ),
+        in_specs=[whole()] * 5,
+        out_specs=[whole()] * 4,
+        compiler_params=params(),
+    )(slots, back.reshape(count, model), table, accum.reshape(1, rows_dev), parts)
+    return layer_out, table_new, accum_new.reshape(rows_dev), grad_in, grad_out
 
 
 def solution(mesh):

time: 362 us -> 263 us (0.73)
  waiting for transfers between devices: 212 us -> 78.9 us
  Pallas kernels: 58.9 us -> 120 us
  starting transfers between devices: 20.6 us -> 0.3 us
    reduce_scatter x1 -> x0, waiting for transfers between devices: 77.9 us -> none  [body(): combined = lax.psum_scatter(grads, 'dp', scatter_dimension=0, tiled=True)]
    pallas_call x2 -> x3, Pallas kernels: 13.9 us -> 80.5 us  [the longest x1 66.5 us: body(): pl.pallas_call(functools.partial(tail_kernel, groups=shards // span, span...]
    unnamed x6 -> x3, waiting for transfers between devices: 56.4 us -> 0.73 us
    all_to_all x1 -> x0, starting transfers between devices: 20.2 us -> none  [body(): lax.all_to_all(send.reshape(shards, width, model), everyone, split_axis=0...]
    pallas_call x1, Pallas kernels: 16.3 us -> 10.5 us  [body(): pl.pallas_call(key_kernel, out_shape=(shape((tokens, model), F32), shape(...]
  transfers between devices with their start and end apart: 6 -> 3, of which waited for: 5 -> 3; matrix products, arithmetic and copies ran while one was open for 0% -> 0% of each run, Pallas kernels for 6% -> 7%
where the time goes in v2:
time: 263 us; the launch traced here: 261 us
  Pallas kernels  120 us (46%)
  waiting for transfers between devices  78.9 us (30%)
  blocking collectives  45.1 us (17%)
  between operations  13.8 us (5%)
  local copies, waits for them, and re-layouts  3.35 us (1%)
    pallas_call x1, Pallas kernels, body(): pl.pallas_call(functools.partial(tail_kernel, groups=shards // span, span...  66.5 us
    all_gather x1, waiting for transfers between devices, body(): kv_all = lax.all_gather(kv, 'pair', axis=0, tiled=True)  36.8 us
    all_gather x1, waiting for transfers between devices, body(): da_all = lax.all_gather(da, 'pair', axis=0, tiled=True)  29.3 us
    all_to_all x1, blocking collectives, body(): lax.all_to_all(found.reshape(shards, width, model), everyone, split_axis=...  24 us
    all_to_all x1, blocking collectives, body(): lax.all_to_all(request[:, :width], everyone, split_axis=0, concat_axis=0,...  21.1 us
    all_gather x1, waiting for transfers between devices, body(): q_all = lax.all_gather(q, 'pair', axis=0, tiled=True)  11.9 us
    pallas_call x1, Pallas kernels, body(): pl.pallas_call(key_kernel, out_shape=(shape((tokens, model), F32), shape(...  10.5 us
    pallas_call x1, Pallas kernels, body(): pl.pallas_call(functools.partial(finish_kernel, rows=rows), out_shape=(sh...  9.43 us
  transfers between devices with their start and end apart: 3, of which 3 were waited for; matrix products, arithmetic and copies ran while one was open for 0% of the time, Pallas kernels for 7%

profile of v2, /device:TPU:1, one launch (start us, length us, event | category | flops | bytes accessed | tf_op | source)
XLA Modules:
  0.0 261.1 jit_solution(6467964682749420391)
XLA Ops:
  7.2 0.0 all-gather.4.cloned.1.call-start
  7.2 1.5 reshape.44.col_ref
  8.7 1.2 reshape.36.row_ref
  9.9 2.0 shard_map.119
  11.9 21.1 %all_to_all.17 = s32[128,1,8]{2,1,0:T(1,128)S(1)} all-to-all(s32[128,1,8]{2,1,0:T(1,128)} %bitcast.19), channel_id=1, replica_groups=mesh['dp'=16,'pair'=8] {'dp','pair'}, dimensions={0} | all-to-all | bytes 8192 | tf_op jit(solution)/shard_map/all_to_all | solution.py:441
  33.0 0.6 pad.4.slots_ref
  33.6 3.2 %shard_map.120 = bf16[1024,512]{1,0:T(8,128)(2,1)} custom-call(s32[128,128]{1,0:T(8,128)} %pad.4.slots_ref, f32[512,512]{1,0:T(8,128)} %table_ref.3), custom_call_target="tpu_custom_call" | custom-call | tf_op jit(solution)/shard_map/pallas_call | solution.py:443
  36.7 24.0 %all_to_all.18 = bf16[128,8,512]{2,1,0:T(8,128)(2,1)} all-to-all(bf16[128,8,512]{2,1,0:T(8,128)(2,1)} %bitcast.15), channel_id=1, replica_groups=mesh['dp'=16,'pair'=8] {'dp','pair'}, dimensions={0} | all-to-all | bytes 2097152 | tf_op jit(solution)/shard_map/all_to_all | solution.py:450
  60.8 6.1 %shard_map.121 = (bf16[384,512]{1,0:T(8,128)(2,1)}, f32[384,2048]{1,0:T(8,128)}, bf16[384,512]{1,0:T(8,128)(2,1)}, bf16[384,512]{1,0:T(8,128)(2,1)}, bf16[384,1024]{1,0:T(8,128)(2,1)}) custom-call(bf16[1024,512]{1,0:T(8,128)(2,1)} %bitcast.14, s32[384,1]{1,0:T(8,128)} %get-tuple-element.30.tc_ref, bf16[512,2048]{1,0:T(8,128)(2,1)} %w_ref.5), custom_call_target="tpu_custom_call" | custom-call | tf_op jit(solution)/shard_map/pallas_call | solution.py:453
  66.9 0.0 all-gather.4.cloned.1.call-update
  66.9 0.0 all-gather.6.cloned.1.call-start
  67.0 0.7 all-gather.6.cloned.1.call-update
  67.7 0.2 all-gather.8.cloned.1.call-start
  67.9 36.8 %all-gather.4.cloned.1.call-done.kv_ref = bf16[3072,1024]{1,0:T(8,128)(2,1)} async-done(((bf16[384,1024]{1,0:T(8,128)(2,1)}), bf16[3072,1024]{1,0:T(8,128)(2,1)}) %all-gather.4.cloned.1.call-update) | async-done | bytes 6291472 | tf_op jit(solution)/shard_map/all_gather | solution.py:467
  104.8 8.9 %shard_map.122 = (bf16[384,512]{1,0:T(8,128)(2,1)}, bf16[384,512]{1,0:T(8,128)(2,1)}, f32[384,512]{1,0:T(8,128)}, f32[512,512]{1,0:T(8,128)}) custom-call(s32[8,128]{1,0:T(8,128)} %get-tuple-element.28.meta_ref, bf16[384,512]{1,0:T(8,128)(2,1)} %get-tuple-element.31.q_ref, bf16[3072,1024]{1,0:T(8,128)(2,1)} %all-gather.4.cloned.1.call-done.kv_ref, ...), custom_call_target="tpu_custom_call" | custom-call | flops 9663676416 | bytes 6291456 | tf_op jit(solution)/shard_map/pallas_call | solution.py:479
  113.6 0.0 all-gather.8.cloned.1.call-update
  113.7 8.6 %shard_map.124.dq_ref = f32[384,512]{1,0:T(8,128)} custom-call(s32[8,128]{1,0:T(8,128)} %get-tuple-element.28.meta_ref, bf16[384,512]{1,0:T(8,128)(2,1)} %get-tuple-element.31.q_ref, bf16[384,512]{1,0:T(8,128)(2,1)} %get-tuple-element.38.da_ref, bf16[3072,1024]{1,0:T(8,128)(2,1)} %all-gather.4.cloned.1.call-done.kv_ref), custom_call_target="tpu_custom_call" | custom-call | flops 14495514624 | bytes 6291456 | tf_op jit(solution)/shard_map/pallas_call | solution.py:497
  122.3 11.9 %all-gather.6.cloned.1.call-done.q_ref = bf16[3072,512]{1,0:T(8,128)(2,1)} async-done(((bf16[384,512]{1,0:T(8,128)(2,1)}), bf16[3072,512]{1,0:T(8,128)(2,1)}) %all-gather.6.cloned.1.call-update) | async-done | bytes 3145744 | tf_op jit(solution)/shard_map/all_gather | solution.py:468
  134.2 29.3 %all-gather.8.cloned.1.call-done.da_ref = bf16[3072,512]{1,0:T(8,128)(2,1)} async-done(((bf16[384,512]{1,0:T(8,128)(2,1)}), bf16[3072,512]{1,0:T(8,128)(2,1)}) %all-gather.8.cloned.1.call-update) | async-done | bytes 3145744 | tf_op jit(solution)/shard_map/all_gather | solution.py:496
  163.6 10.5 %shard_map.123 = (f32[384,512]{1,0:T(8,128)}, f32[384,512]{1,0:T(8,128)}) custom-call(s32[8,128]{1,0:T(8,128)} %get-tuple-element.28.meta_ref, bf16[384,1024]{1,0:T(8,128)(2,1)} %get-tuple-element.32.kv_ref, bf16[3072,512]{1,0:T(8,128)(2,1)} %all-gather.6.cloned.1.call-done.q_ref, bf16[3072,512]{1,0:T(8,128)(2,1)} %all-gather.8.cloned.1.call-done.da_ref), custom_call_target="tpu_custom_call" | custom-call | flops 19327352832 | bytes 6291456 | tf_op jit(solution)/shard_map/pallas_call | solution.py:508
  174.0 9.4 %shard_map.125 = (f32[2,64,8,1280]{3,2,1,0:T(8,128)}, bf16[1024,512]{1,0:T(8,128)(2,1)}) custom-call(f32[384,2048]{1,0:T(8,128)} %get-tuple-element.36.z_ref, f32[384,512]{1,0:T(8,128)} %get-tuple-element.37.dhu_ref, f32[384,512]{1,0:T(8,128)} %get-tuple-element.39.dv_ref, f32[384,512]{1,0:T(8,128)} %shard_map.124.dq_ref, ...), custom_call_target="tpu_custom_call" | custom-call | tf_op jit(solution)/shard_map/pallas_call | solution.py:522
  183.5 66.5 %shard_map.126 = (bf16[128,8,512]{2,1,0:T(8,128)(2,1)}, bf16[64,8,1280]{2,1,0:T(8,128)(2,1)}) custom-call(bf16[128,8,512]{2,1,0:T(8,128)(2,1)} %bitcast.17, f32[2,64,8,1280]{3,2,1,0:T(8,128)} %get-tuple-element.44.grads_ref), custom_call_target="tpu_custom_call" | custom-call | tf_op jit(solution)/shard_map/pallas_call | solution.py:530
  250.0 4.5 %shard_map.127 = (f32[512,512]{1,0:T(8,128)}, f32[1,512]{1,0:T(1,128)}, f32[4,2048]{1,0:T(4,128)}, f32[4,512]{1,0:T(4,128)}) custom-call(s32[128,128]{1,0:T(8,128)} %pad.4.slots_ref, bf16[1024,512]{1,0:T(8,128)(2,1)} %bitcast.16, f32[512,512]{1,0:T(8,128)} %table_ref.3, f32[1,512]{1,0:T(1,128)} %bitcast.20, bf16[64,8,1280]{2,1,0:T(8,128)(2,1)} %get-tuple-element.46.parts_ref), custom_call_target="tpu_custom_call" | custom-call | tf_op jit(solution)/shard_map/pallas_call | solution.py:542
Async XLA Ops:
  7.2 97.6 %all-gather.4.cloned.1.call-start = ((), (), s32[]{:S(2)}) async-start(), calls=%async_computation.2 | async-start | bytes 7077888 | tf_op jit(solution)/shard_map/all_gather | solution.py:467
  66.9 67.3 %all-gather.6.cloned.1.call-start = ((), (), s32[]{:S(2)}) async-start(), calls=%async_computation.3 | async-start | bytes 3538944 | tf_op jit(solution)/shard_map/all_gather | solution.py:468
  67.7 95.9 %all-gather.8.cloned.1.call-start = ((), (), s32[]{:S(2)}) async-start(), calls=%async_computation.4 | async-start | bytes 3538944 | tf_op jit(solution)/shard_map/all_gather | solution.py:496
Sparse Core Ops, SparseCore 0:
  67.1 37.6 all-gather.3
  106.4 27.7 all-gather.5
  135.9 27.6 all-gather.7

commit v3 on v2

--- a/solution.py
+++ b/solution.py
@@ -133,117 +133,301 @@
     return jnp.where((k_pos >= least) & (k_pos <= q_pos), 1.0, 0.0)
 
 
-def pair_live(meta_ref, row, lane, q_block, k_block, size):
+class Ring:
+    def __init__(self, source, gathered, send, recv, local, span):
+        self.source, self.gathered, self.send, self.recv, self.local = source, gathered, send, recv, local
+        chips = span // 2
+        self.g, self.p = lax.axis_index("dp"), lax.axis_index("pair")
+        core, chip = self.p % 2, self.p // 2
+        at = lambda step: ((chip + step) % chips) * 2 + core
+        self.up, self.down, self.far = at(1), at(chips - 1), at(2)
+        self.other = chip * 2 + 1 - core
+
+    def copy(self, i):
+        p, up, down, far, other = self.p, self.up, self.down, self.far, self.other
+        owner, part, to = (
+            (p, 0, up),
+            (p, 1, up),
+            (p, 1, down),
+            (p, 0, down),
+            (p, 0, other),
+            (p, 1, other),
+            (down, 0, up),
+            (up, 1, down),
+            (down, 0, other),
+            (down, 1, other),
+            (up, 1, other),
+            (up, 0, other),
+            (far, 0, other),
+            (far, 1, other),
+        )[i]
+        half = self.source.shape[0] // 2
+        rows = pl.ds(part * half, half)
+        return pltpu.make_async_remote_copy(
+            src_ref=self.source.at[rows] if i < 6 else self.gathered.at[owner, rows],
+            dst_ref=self.gathered.at[owner, rows],
+            send_sem=self.send.at[i],
+            recv_sem=self.recv.at[i],
+            device_id=(self.g, to),
+            device_id_type=MESH,
+        )
+
+    def own(self):
+        return pltpu.make_async_copy(self.source, self.gathered.at[self.p], self.local)
+
+    def start(self):
+        self.own().start()
+        for i in (0, 2, 1, 3, 4, 5):
+            self.copy(i).start()
+
+    def arrive(self, *which):
+        for i in which:
+            self.copy(i).wait_recv()
+
+    def after(self, arrived, *sent):
+        self.arrive(arrived)
+        for i in sent:
+            self.copy(i).start()
+
+    def first(self):
+        self.after(0, 6, 8)
+        self.after(2, 7, 10)
+
+    def second(self):
+        self.after(1, 9)
+        self.after(3, 11)
+
+    def last(self):
+        self.after(6, 12)
+        self.after(7, 13)
+
+    def sent(self):
+        for i in range(14):
+            self.copy(i).wait_send()
+
+
+def attend_kernel(
+    meta_ref,
+    q_ref,
+    kv_ref,
+    u_ref,
+    x_ref,
+    w_ref,
+    og_ref,
+    out_ref,
+    dhu_ref,
+    gout_ref,
+    dq_ref,
+    dk_ref,
+    dv_ref,
+    kv_all,
+    q_all,
+    da_all,
+    da,
+    parts,
+    acc,
+    mask,
+    local,
+    send,
+    recv,
+    *,
+    span,
+):
+    own = lax.axis_index("pair")
+    chips, core, chip = span // 2, own % 2, own // 2
+    size, width = q_ref.shape
+    kv_ring, q_ring, da_ring = (
+        Ring(source, gathered, send.at[i], recv.at[i], local.at[i], span)
+        for i, (source, gathered) in enumerate(((kv_ref, kv_all), (q_ref, q_all), (da, da_all)))
+    )
+    barrier = pltpu.get_barrier_semaphore()
+    for to in (kv_ring.other, kv_ring.up, kv_ring.down):
+        pl.semaphore_signal(barrier, inc=1, device_id=(kv_ring.g, to), device_id_type=MESH)
+    pl.semaphore_wait(barrier, 3)
+    kv_ring.start()
+
+    def block_at(step):
+        turn = step // 2
+        shift = (3 * turn - (turn * (turn - 1)) // 2) % 4
+        return ((chip + shift) % chips) * 2 + (core + step % 2) % 2
+
+    def split(value, at):
+        parts[at] = even_half(value)
+        parts[at + 1] = odd_half(value)
+
+    def slabs(work):
+        def one(s, carry):
+            first = pl.multiple_of(s * 128, 128)
+            work(pl.ds(first, 128), pl.ds(pl.multiple_of(width + s * 128, 128), 128))
+            return carry
+
+        lax.fori_loop(0, width // 128, one, 0)
+
+    def both(rows):
+        return jnp.concatenate([even_half(rows), odd_half(rows)], axis=0)
+
     zeros = meta_ref[0, 2]
-    apart = ((k_block + 1) * size <= zeros) & (q_block * size >= zeros)
-    return (meta_ref[row, lane] == 1) & jnp.logical_not(apart)
-
-
-def forward_kernel(
-    meta_ref, q_ref, kv_ref, u_ref, x_ref, w_ref, og_ref, out_ref, da_ref, dhu_ref, gout_ref, qs, acc, mask
-):
-    j = pl.program_id(0)
-    own = meta_ref[0, 3]
-    size, width = q_ref.shape
-
-    @pl.when(j == 0)
-    def _():
-        scaled = q_ref[...] * 0.0625
-        qs[0] = even_half(scaled)
-        qs[1] = odd_half(scaled)
-        acc[...] = jnp.zeros_like(acc)
-
-    @pl.when((j <= own) & pair_live(meta_ref, j, 0, own, j, size))
-    def _():
-        mask[...] = visible(0, size, own, j, meta_ref[0, 2])
-        for s in range(width // 128):
-            cols = slice(s * 128, s * 128 + 128)
-            keys = kv_ref[:, cols]
-            values = kv_ref[:, width + s * 128 : width + s * 128 + 128]
-            weights = []
-            for half in range(2):
-                h = dot_t(qs[half, :, cols], keys)
-                weights.append(((h + h * jnp.tanh(h)) * mask[...]).astype(BF16))
-            both = jnp.concatenate([even_half(values), odd_half(values)], axis=0)
-            acc[:, cols] += dot(jnp.concatenate(weights, axis=1), both)
-
-    @pl.when(j == pl.num_programs(0) - 1)
-    def _():
-        normed, spread = normalize(acc[...])
-        gate = u_ref[...].astype(F32)
-        gated = (normed * gate).astype(BF16)
-        out_ref[...] = (dot(gated, w_ref[...]) + x_ref[...].astype(F32)).astype(BF16)
-        dy = dot_t(og_ref[...], w_ref[...])
-        dhu_ref[...] = dy * normed
-        da_ref[...] = norm_back(dy * gate, normed, spread).astype(BF16)
-        gout_ref[...] = lax.dot_general(gated, og_ref[...], (((0,), (0,)), ((), ())), preferred_element_type=F32)
-
-
-def query_kernel(meta_ref, q_ref, da_ref, kv_ref, dq_ref, qs, ds, mask):
-    j = pl.program_id(0)
-    own = meta_ref[0, 3]
-    size, width = q_ref.shape
-
-    @pl.when(j == 0)
-    def _():
-        scaled = q_ref[...] * 0.0625
-        qs[0] = even_half(scaled)
-        qs[1] = odd_half(scaled)
-        scaled = da_ref[...] * 0.0625
-        ds[0] = even_half(scaled)
-        ds[1] = odd_half(scaled)
-        dq_ref[...] = jnp.zeros_like(dq_ref)
-
-    @pl.when((j <= own) & pair_live(meta_ref, j, 0, own, j, size))
-    def _():
-        mask[...] = visible(0, size, own, j, meta_ref[0, 2])
-        for s in range(width // 128):
-            cols = slice(s * 128, s * 128 + 128)
-            keys = kv_ref[:, cols]
-            values = kv_ref[:, width + s * 128 : width + s * 128 + 128]
-            grads = []
-            for half in range(2):
-                h = dot_t(qs[half, :, cols], keys)
-                t = jnp.tanh(h)
-                slope = (1.0 + t) * (1.0 + h * (1.0 - t))
-                grads.append((dot_t(ds[half, :, cols], values) * slope * mask[...]).astype(BF16))
-            both = jnp.concatenate([even_half(keys), odd_half(keys)], axis=0)
-            dq_ref[:, cols] += dot(jnp.concatenate(grads, axis=1), both)
-
-
-def key_kernel(meta_ref, kv_ref, q_ref, da_ref, dk_ref, dv_ref, ks, vs, mask):
-    i = pl.program_id(0)
-    own = meta_ref[0, 3]
-    size, width = q_ref.shape
-
-    @pl.when(i == 0)
-    def _():
-        scaled = kv_ref[...] * 0.0625
-        ks[0] = even_half(scaled[:, :width])
-        ks[1] = odd_half(scaled[:, :width])
-        vs[0] = even_half(scaled[:, width:])
-        vs[1] = odd_half(scaled[:, width:])
-        dk_ref[...] = jnp.zeros_like(dk_ref)
-        dv_ref[...] = jnp.zeros_like(dv_ref)
-
-    @pl.when((i >= own) & pair_live(meta_ref, i, 1, i, own, size))
-    def _():
-        mask[...] = visible(1, size, i, own, meta_ref[0, 2])
-        for s in range(width // 128):
-            cols = slice(s * 128, s * 128 + 128)
-            queries = q_ref[:, cols]
-            dafter = da_ref[:, cols]
-            grads, weights = [], []
-            for half in range(2):
-                h = dot_t(ks[half, :, cols], queries)
-                t = jnp.tanh(h)
-                weights.append(((h + h * t) * mask[...]).astype(BF16))
-                slope = (1.0 + t) * (1.0 + h * (1.0 - t))
-                grads.append((dot_t(vs[half, :, cols], dafter) * slope * mask[...]).astype(BF16))
-            q_both = jnp.concatenate([even_half(queries), odd_half(queries)], axis=0)
-            a_both = jnp.concatenate([even_half(dafter), odd_half(dafter)], axis=0)
-            dk_ref[:, cols] += dot(jnp.concatenate(grads, axis=1), q_both)
-            dv_ref[:, cols] += dot(jnp.concatenate(weights, axis=1), a_both)
+    split(q_ref[...] * 0.0625, 0)
+    split(kv_ref[:, :width] * 0.0625, 4)
+    split(kv_ref[:, width:] * 0.0625, 6)
+    acc[...] = jnp.zeros_like(acc)
+    dq_ref[...] = jnp.zeros_like(dq_ref)
+    dk_ref[...] = jnp.zeros_like(dk_ref)
+    dv_ref[...] = jnp.zeros_like(dv_ref)
+
+    def forward(step, carry):
+        j = block_at(step)
+
+        @pl.when(step == 0)
+        def _():
+            kv_ring.own().wait()
+
+        @pl.when(step == 1)
+        def _():
+            kv_ring.arrive(4, 5)
+
+        @pl.when(step == 2)
+        def _():
+            kv_ring.first()
+            kv_ring.second()
+            q_ring.start()
+
+        @pl.when(step == 3)
+        def _():
+            kv_ring.arrive(8, 9)
+
+        @pl.when(step == 5)
+        def _():
+            kv_ring.arrive(10, 11)
+
+        @pl.when(step == 6)
+        def _():
+            kv_ring.last()
+
+        @pl.when(step == 7)
+        def _():
+            kv_ring.arrive(12, 13)
+
+        @pl.when(j <= own)
+        def _():
+            mask[...] = visible(0, size, own, j, zeros) * meta_ref[j, 0].astype(F32)
+
+            def work(cols, late):
+                keys = kv_all[j, :, cols]
+                weights = []
+                for half in range(2):
+                    h = dot_t(parts[half, :, cols], keys)
+                    weights.append(((h + h * jnp.tanh(h)) * mask[...]).astype(BF16))
+                acc[:, cols] += dot(jnp.concatenate(weights, axis=1), both(kv_all[j, :, late]))
+
+            slabs(work)
+
+        return carry
+
+    lax.fori_loop(0, span, forward, 0)
+
+    normed, spread = normalize(acc[...])
+    gate = u_ref[...].astype(F32)
+    gated = (normed * gate).astype(BF16)
+    dy = dot_t(og_ref[...], w_ref[...])
+    da[...] = norm_back(dy * gate, normed, spread).astype(BF16)
+    q_ring.first()
+    da_ring.start()
+    split(da[...] * 0.0625, 2)
+    dhu_ref[...] = dy * normed
+    out_ref[...] = (dot(gated, w_ref[...]) + x_ref[...].astype(F32)).astype(BF16)
+    gout_ref[...] = lax.dot_general(gated, og_ref[...], (((0,), (0,)), ((), ())), preferred_element_type=F32)
+    q_ring.second()
+
+    def by_query(step, carry):
+        j = block_at(step)
+
+        @pl.when(step == 4)
+        def _():
+            q_ring.last()
+
+        @pl.when(j <= own)
+        def _():
+            mask[...] = visible(0, size, own, j, zeros) * meta_ref[j, 0].astype(F32)
+
+            def work(cols, late):
+                keys = kv_all[j, :, cols]
+                values = kv_all[j, :, late]
+                grads = []
+                for half in range(2):
+                    h = dot_t(parts[half, :, cols], keys)
+                    t = jnp.tanh(h)
+                    slope = (1.0 + t) * (1.0 + h * (1.0 - t))
+                    grads.append((dot_t(parts[2 + half, :, cols], values) * slope * mask[...]).astype(BF16))
+                dq_ref[:, cols] += dot(jnp.concatenate(grads, axis=1), both(keys))
+
+            slabs(work)
+
+        return carry
+
+    lax.fori_loop(0, span, by_query, 0)
+
+    def by_key(step, carry):
+        i = block_at(step)
+
+        @pl.when(step == 0)
+        def _():
+            q_ring.own().wait()
+            da_ring.own().wait()
+
+        @pl.when(step == 1)
+        def _():
+            q_ring.arrive(4, 5)
+            da_ring.arrive(4, 5)
+
+        @pl.when(step == 2)
+        def _():
+            da_ring.first()
+            da_ring.second()
+
+        @pl.when(step == 3)
+        def _():
+            q_ring.arrive(8, 9)
+            da_ring.arrive(8, 9)
+
+        @pl.when(step == 5)
+        def _():
+            q_ring.arrive(10, 11)
+            da_ring.arrive(10, 11)
+
+        @pl.when(step == 6)
+        def _():
+            da_ring.last()
+
+        @pl.when(step == 7)
+        def _():
+            q_ring.arrive(12, 13)
+            da_ring.arrive(12, 13)
+
+        @pl.when(i >= own)
+        def _():
+            mask[...] = visible(1, size, i, own, zeros) * meta_ref[i, 1].astype(F32)
+
+            def work(cols, late):
+                queries = q_all[i, :, cols]
+                dafter = da_all[i, :, cols]
+                grads, weights = [], []
+                for half in range(2):
+                    h = dot_t(parts[4 + half, :, cols], queries)
+                    t = jnp.tanh(h)
+                    weights.append(((h + h * t) * mask[...]).astype(BF16))
+                    slope = (1.0 + t) * (1.0 + h * (1.0 - t))
+                    grads.append((dot_t(parts[6 + half, :, cols], dafter) * slope * mask[...]).astype(BF16))
+                dk_ref[:, cols] += dot(jnp.concatenate(grads, axis=1), both(queries))
+                dv_ref[:, cols] += dot(jnp.concatenate(weights, axis=1), both(dafter))
+
+            slabs(work)
+
+        return carry
+
+    lax.fori_loop(0, span, by_key, 0)
+    for ring in (kv_ring, q_ring, da_ring):
+        ring.sent()
 
 
 def finish_kernel(
@@ -464,58 +648,33 @@
         compiler_params=params(),
     )(fetched, target_c, w_in)
 
-    kv_all = lax.all_gather(kv, "pair", axis=0, tiled=True)
-    q_all = lax.all_gather(q, "pair", axis=0, tiled=True)
-
-    fixed = lambda cols: pl.BlockSpec((tokens, cols), lambda i, m: (0, 0))
-    square = lambda rows, cols: pl.BlockSpec((rows, cols), lambda i, m: (0, 0))
-    low_half = lambda cols: pl.BlockSpec((tokens, cols), lambda i, m: (jnp.minimum(i, m[0, 3]), 0))
-    high_half = lambda cols: pl.BlockSpec((tokens, cols), lambda i, m: (jnp.maximum(i, m[0, 3]), 0))
-    halves = VMEM((2, tokens, model), BF16)
-    grid_spec = lambda ins, outs, scratch: pltpu.PrefetchScalarGridSpec(
-        num_scalar_prefetch=1, grid=(span,), in_specs=ins, out_specs=outs, scratch_shapes=scratch
-    )
-    pair_flops = 2 * tokens * tokens * model * span
-    layer_out, da, dhu, gout = pl.pallas_call(
-        forward_kernel,
+    block = lambda cols, dtype: VMEM((span, tokens, cols), dtype)
+    layer_out, dhu, gout, dq, dk, dv = pl.pallas_call(
+        functools.partial(attend_kernel, span=span),
         out_shape=(
-            shape((tokens, model), BF16),
             shape((tokens, model), BF16),
             shape((tokens, model), F32),
             shape((model, model), F32),
+            shape((tokens, model), F32),
+            shape((tokens, model), F32),
+            shape((tokens, model), F32),
         ),
-        grid_spec=grid_spec(
-            [fixed(model), low_half(2 * model), fixed(model), fixed(model), square(model, model), fixed(model)],
-            [fixed(model), fixed(model), fixed(model), square(model, model)],
-            [halves, VMEM((tokens, model), F32), VMEM((tokens, tokens), F32)],
-        ),
-        compiler_params=params(),
-        cost_estimate=cost(8 * pair_flops, 6 * 2**20),
-    )(meta, q, kv_all, u, x, w_out, out_grad)
-
-    da_all = lax.all_gather(da, "pair", axis=0, tiled=True)
-    dq = pl.pallas_call(
-        query_kernel,
-        out_shape=shape((tokens, model), F32),
-        grid_spec=grid_spec(
-            [fixed(model), fixed(model), low_half(2 * model)],
-            fixed(model),
-            [halves, halves, VMEM((tokens, tokens), F32)],
-        ),
-        compiler_params=params(),
-        cost_estimate=cost(12 * pair_flops, 6 * 2**20),
-    )(meta, q, da, kv_all)
-    dk, dv = pl.pallas_call(
-        key_kernel,
-        out_shape=(shape((tokens, model), F32), shape((tokens, model), F32)),
-        grid_spec=grid_spec(
-            [fixed(2 * model), high_half(model), high_half(model)],
-            [fixed(model), fixed(model)],
-            [halves, halves, VMEM((tokens, tokens), F32)],
-        ),
-        compiler_params=params(),
-        cost_estimate=cost(16 * pair_flops, 6 * 2**20),
-    )(meta, kv, q_all, da_all)
+        in_specs=[pl.BlockSpec(memory_space=pltpu.SMEM)] + [whole()] * 6,
+        out_specs=[whole()] * 6,
+        scratch_shapes=[
+            block(2 * model, BF16),
+            block(model, BF16),
+            block(model, BF16),
+            VMEM((tokens, model), BF16),
+            VMEM((8, tokens, model), BF16),
+            VMEM((tokens, model), F32),
+            VMEM((tokens, tokens), F32),
+            pltpu.SemaphoreType.DMA((3,)),
+            pltpu.SemaphoreType.DMA((3, 14)),
+            pltpu.SemaphoreType.DMA((3, 14)),
+        ],
+        compiler_params=params(collective_id=1, has_side_effects=True),
+    )(meta, q, kv, u, x, w_out, out_grad)
 
     rows = model // shards
     chunk = (2 * rows, 5 * model // 2)

time: 263 us -> 207 us (0.79)
  waiting for transfers between devices: 78.9 us -> 0 us
  Pallas kernels: 120 us -> 157 us
  between operations: 13.8 us -> 0.66 us
    all_gather x3 -> x0, waiting for transfers between devices: 78.1 us -> none  [the longest x1 36.8 us: body(): kv_all = lax.all_gather(kv, 'pair', axis=0, tiled=True)]
    pallas_call x3 -> x1, Pallas kernels: 28 us -> 84 us  [body(): pl.pallas_call(functools.partial(attend_kernel, span=span), out_shape=(sh...]
    pallas_call x1, Pallas kernels: 66.5 us -> 47.4 us  [body(): pl.pallas_call(functools.partial(tail_kernel, groups=shards // span, span...]
  transfers between devices with their start and end apart: 3 -> 0, of which waited for: 3 -> 0; matrix products, arithmetic and copies ran while one was open for 0% -> 0% of each run, Pallas kernels for 7% -> 0%
where the time goes in v3:
time: 207 us
  Pallas kernels  157 us (76%)
  blocking collectives  45.1 us (22%)
  local copies, waits for them, and re-layouts  4.11 us (2%)
    pallas_call x1, Pallas kernels, body(): pl.pallas_call(functools.partial(attend_kernel, span=span), out_shape=(sh...  84 us
    pallas_call x1, Pallas kernels, body(): pl.pallas_call(functools.partial(tail_kernel, groups=shards // span, span...  47.4 us
    all_to_all x1, blocking collectives, body(): lax.all_to_all(found.reshape(shards, width, model), everyone, split_axis=...  24.1 us
    all_to_all x1, blocking collectives, body(): lax.all_to_all(request[:, :width], everyone, split_axis=0, concat_axis=0,...  21.1 us
    pallas_call x1, Pallas kernels, body(): pl.pallas_call(functools.partial(finish_kernel, rows=rows), out_shape=(sh...  9.52 us
    pallas_call x1, Pallas kernels, body(): pl.pallas_call(project_kernel, out_shape=(shape((tokens, model), BF16), s...  6.02 us
    pallas_call x1, Pallas kernels, body(): pl.pallas_call(functools.partial(update_kernel, width=width, factor=1.0 /...  4.58 us

profile of v3, /device:TPU:1, one launch (start us, length us, event | category | flops | bytes accessed | tf_op | source)
XLA Modules:
  0.0 206.5 jit_solution(17955123645200337629)
XLA Ops:
  0.6 1.2 reshape.36.row_ref
  1.9 1.5 reshape.44.col_ref
  3.4 2.0 shard_map.119
  5.3 21.1 %all_to_all.17 = s32[128,1,8]{2,1,0:T(1,128)S(1)} all-to-all(s32[128,1,8]{2,1,0:T(1,128)} %bitcast.19), channel_id=1, replica_groups=mesh['dp'=16,'pair'=8] {'dp','pair'}, dimensions={0} | all-to-all | bytes 8192 | tf_op jit(solution)/shard_map/all_to_all | solution.py:625
  26.4 0.6 pad.4.slots_ref
  27.0 3.2 %shard_map.120 = bf16[1024,512]{1,0:T(8,128)(2,1)} custom-call(s32[128,128]{1,0:T(8,128)} %pad.4.slots_ref, f32[512,512]{1,0:T(8,128)} %table_ref.3), custom_call_target="tpu_custom_call" | custom-call | tf_op jit(solution)/shard_map/pallas_call | solution.py:627
  30.2 24.1 %all_to_all.18 = bf16[128,8,512]{2,1,0:T(8,128)(2,1)} all-to-all(bf16[128,8,512]{2,1,0:T(8,128)(2,1)} %bitcast.15), channel_id=1, replica_groups=mesh['dp'=16,'pair'=8] {'dp','pair'}, dimensions={0} | all-to-all | bytes 2097152 | tf_op jit(solution)/shard_map/all_to_all | solution.py:634
  54.2 6.0 %shard_map.121 = (bf16[384,512]{1,0:T(8,128)(2,1)}, f32[384,2048]{1,0:T(8,128)}, bf16[384,512]{1,0:T(8,128)(2,1)}, bf16[384,512]{1,0:T(8,128)(2,1)}, bf16[384,1024]{1,0:T(8,128)(2,1)}) custom-call(bf16[1024,512]{1,0:T(8,128)(2,1)} %bitcast.14, s32[384,1]{1,0:T(8,128)} %get-tuple-element.30.tc_ref, bf16[512,2048]{1,0:T(8,128)(2,1)} %w_ref.5), custom_call_target="tpu_custom_call" | custom-call | tf_op jit(solution)/shard_map/pallas_call | solution.py:637
  60.3 84.0 %shard_map.122 = (bf16[384,512]{1,0:T(8,128)(2,1)}, f32[384,512]{1,0:T(8,128)}, f32[512,512]{1,0:T(8,128)}, f32[384,512]{1,0:T(8,128)}, f32[384,512]{1,0:T(8,128)}, /*index=5*/f32[384,512]{1,0:T(8,128)}) custom-call(s32[8,128]{1,0:T(8,128)} %get-tuple-element.28.meta_ref, bf16[384,512]{1,0:T(8,128)(2,1)} %get-tuple-element.31.q_ref, ...), custom_call_target="tpu_custom_call" | custom-call | tf_op jit(solution)/shard_map/pallas_call | solution.py:652
  144.2 9.5 %shard_map.123 = (f32[2,64,8,1280]{3,2,1,0:T(8,128)}, bf16[1024,512]{1,0:T(8,128)(2,1)}) custom-call(f32[384,2048]{1,0:T(8,128)} %get-tuple-element.36.z_ref, f32[384,512]{1,0:T(8,128)} %get-tuple-element.37.dhu_ref, f32[384,512]{1,0:T(8,128)} %get-tuple-element.38.dv_ref, f32[384,512]{1,0:T(8,128)} %get-tuple-element.39.dq_ref, ...), custom_call_target="tpu_custom_call" | custom-call | tf_op jit(solution)/shard_map/pallas_call | solution.py:681
  153.7 47.4 %shard_map.124 = (bf16[128,8,512]{2,1,0:T(8,128)(2,1)}, bf16[64,8,1280]{2,1,0:T(8,128)(2,1)}) custom-call(bf16[128,8,512]{2,1,0:T(8,128)(2,1)} %bitcast.17, f32[2,64,8,1280]{3,2,1,0:T(8,128)} %get-tuple-element.44.grads_ref), custom_call_target="tpu_custom_call" | custom-call | tf_op jit(solution)/shard_map/pallas_call | solution.py:689
  201.2 0.0 copy-start
  201.2 4.6 %shard_map.125 = (f32[512,512]{1,0:T(8,128)}, f32[1,512]{1,0:T(1,128)}, f32[4,2048]{1,0:T(4,128)}, f32[4,512]{1,0:T(4,128)}) custom-call(s32[128,128]{1,0:T(8,128)} %pad.4.slots_ref, bf16[1024,512]{1,0:T(8,128)(2,1)} %bitcast.16, f32[512,512]{1,0:T(8,128)} %table_ref.3, f32[1,512]{1,0:T(1,128)} %bitcast.20, bf16[64,8,1280]{2,1,0:T(8,128)(2,1)} %get-tuple-element.46.parts_ref), custom_call_target="tpu_custom_call" | custom-call | tf_op jit(solution)/shard_map/pallas_call | solution.py:701
  205.8 0.0 copy-done
  205.8 0.7 copy.17
Async XLA Ops:
  201.2 4.6 %copy-start = (bf16[384,512]{1,0:T(8,128)(2,1)S(1)}, bf16[384,512]{1,0:T(8,128)(2,1)}, u32[]{:S(2)}) copy-start(bf16[384,512]{1,0:T(8,128)(2,1)} %get-tuple-element.56) | copy-start | bytes 1179652

commit v4 on v3

--- a/solution.py
+++ b/solution.py
@@ -110,11 +110,12 @@
     found_ref[...] = dot(pick, table_ref[...].astype(BF16)).astype(BF16)
 
 
-def project_kernel(fetched_ref, tc_ref, w_ref, x_ref, z_ref, u_ref, q_ref, kv_ref):
-    count, width = fetched_ref.shape
+def project(fetched_ref, tc_ref, w_ref, x_ref, z_ref, u_ref, q_ref, kv_ref):
+    width = fetched_ref.shape[2]
+    count = fetched_ref.shape[0] * fetched_ref.shape[1]
     tokens = tc_ref.shape[0]
     pick = jnp.where(iota((tokens, count), 1) == tc_ref[...], 1.0, 0.0).astype(BF16)
-    rows = dot(pick, fetched_ref[...])
+    rows = dot(pick, fetched_ref[...].reshape(count, width))
     x_ref[...] = rows.astype(BF16)
     normed, _ = normalize(rows)
     low = normed.astype(BF16)
@@ -134,13 +135,16 @@
 
 
 class Ring:
-    def __init__(self, source, gathered, send, recv, local, span):
+    SENDS = ((0, 1, 2, 3, 4, 5, 7), (0, 1, 2, 4, 5, 6, 8, 9), (0, 1, 4, 5, 6, 8, 9, 12, 13), (4, 5, 7, 8, 9, 10, 11, 12, 13))
+
+    def __init__(self, source, gathered, send, recv, local, span, falling):
         self.source, self.gathered, self.send, self.recv, self.local = source, gathered, send, recv, local
         chips = span // 2
         self.g, self.p = lax.axis_index("dp"), lax.axis_index("pair")
         core, chip = self.p % 2, self.p // 2
         at = lambda step: ((chip + step) % chips) * 2 + core
-        self.up, self.down, self.far = at(1), at(chips - 1), at(2)
+        self.up, self.down, self.far = at(chips - 1 if falling else 1), at(1 if falling else chips - 1), at(2)
+        self.rank = chips - 1 - chip if falling else chip
         self.other = chip * 2 + 1 - core
 
     def copy(self, i):
@@ -175,10 +179,21 @@
     def own(self):
         return pltpu.make_async_copy(self.source, self.gathered.at[self.p], self.local)
 
+    def when(self, *ranks):
+        def decorate(steps):
+            for rank in ranks:
+                pl.when(self.rank == rank)(functools.partial(steps, rank))
+
+        return decorate
+
     def start(self):
         self.own().start()
-        for i in (0, 2, 1, 3, 4, 5):
-            self.copy(i).start()
+
+        @self.when(0, 1, 2, 3)
+        def _(rank):
+            for i in (0, 2, 1, 3, 4, 5):
+                if i in self.SENDS[rank]:
+                    self.copy(i).start()
 
     def arrive(self, *which):
         for i in which:
@@ -189,66 +204,83 @@
         for i in sent:
             self.copy(i).start()
 
-    def first(self):
-        self.after(0, 6, 8)
-        self.after(2, 7, 10)
-
-    def second(self):
-        self.after(1, 9)
-        self.after(3, 11)
-
-    def last(self):
-        self.after(6, 12)
-        self.after(7, 13)
+    def relay(self, *ranks):
+        @self.when(*ranks)
+        def _(rank):
+            if rank == 0:
+                self.after(2, 7)
+            elif rank == 3:
+                self.after(2, 7, 10)
+                self.after(0, 8)
+                self.after(3, 11)
+                self.after(1, 9)
+            else:
+                self.after(0, 6, 8)
+                self.after(1, 9)
+
+    def relay_far(self):
+        @self.when(2, 3)
+        def _(rank):
+            self.after(6, 12)
+            self.after(7, 13)
+
+    def handed(self, step):
+        if step == 1:
+            self.arrive(4, 5)
+        elif step == 3:
+
+            @self.when(1, 2, 3)
+            def _(rank):
+                self.arrive(8, 9)
+
+        elif step == 5:
+
+            @self.when(3)
+            def _(rank):
+                self.arrive(10, 11)
+
+        elif step == 7:
+
+            @self.when(2, 3)
+            def _(rank):
+                self.arrive(12, 13)
 
     def sent(self):
-        for i in range(14):
-            self.copy(i).wait_send()
-
-
-def attend_kernel(
-    meta_ref,
-    q_ref,
-    kv_ref,
-    u_ref,
-    x_ref,
-    w_ref,
-    og_ref,
-    out_ref,
-    dhu_ref,
-    gout_ref,
-    dq_ref,
-    dk_ref,
-    dv_ref,
-    kv_all,
-    q_all,
-    da_all,
-    da,
-    parts,
-    acc,
-    mask,
-    local,
-    send,
-    recv,
-    *,
-    span,
+        @self.when(0, 1, 2, 3)
+        def _(rank):
+            for i in self.SENDS[rank]:
+                self.copy(i).wait_send()
+
+
+def attend(
+    meta_ref, q_ref, kv_ref, u_ref, x_ref, w_ref, og_ref, out_ref, dhu_ref, gout_ref, dq_ref, dk_ref, dv_ref, kv_all,
+    q_all, da_all, da, parts, acc, mask, local, send, recv, *, span
 ):
     own = lax.axis_index("pair")
     chips, core, chip = span // 2, own % 2, own // 2
     size, width = q_ref.shape
     kv_ring, q_ring, da_ring = (
-        Ring(source, gathered, send.at[i], recv.at[i], local.at[i], span)
-        for i, (source, gathered) in enumerate(((kv_ref, kv_all), (q_ref, q_all), (da, da_all)))
+        Ring(source, gathered, send.at[i], recv.at[i], local.at[i], span, falling)
+        for i, (source, gathered, falling) in enumerate(
+            ((kv_ref, kv_all, False), (q_ref, q_all, True), (da, da_all, True))
+        )
     )
-    barrier = pltpu.get_barrier_semaphore()
-    for to in (kv_ring.other, kv_ring.up, kv_ring.down):
-        pl.semaphore_signal(barrier, inc=1, device_id=(kv_ring.g, to), device_id_type=MESH)
-    pl.semaphore_wait(barrier, 3)
     kv_ring.start()
-
-    def block_at(step):
+    q_ring.start()
+
+    def at_steps(step, *rings):
+        for k in (1, 3, 5, 7):
+
+            @pl.when(step == k)
+            def _():
+                for ring in rings:
+                    ring.handed(k)
+
+    def block_at(step, falling):
         turn = step // 2
         shift = (3 * turn - (turn * (turn - 1)) // 2) % 4
+        if falling:
+            shift = (chips - shift) % chips
         return ((chip + shift) % chips) * 2 + (core + step % 2) % 2
 
     def split(value, at):
@@ -276,37 +308,23 @@
     dv_ref[...] = jnp.zeros_like(dv_ref)
 
     def forward(step, carry):
-        j = block_at(step)
+        j = block_at(step, False)
 
         @pl.when(step == 0)
         def _():
             kv_ring.own().wait()
 
-        @pl.when(step == 1)
-        def _():
-            kv_ring.arrive(4, 5)
-
         @pl.when(step == 2)
         def _():
-            kv_ring.first()
-            kv_ring.second()
-            q_ring.start()
-
-        @pl.when(step == 3)
-        def _():
-            kv_ring.arrive(8, 9)
-
-        @pl.when(step == 5)
-        def _():
-            kv_ring.arrive(10, 11)
+            kv_ring.relay(0, 1, 2, 3)
+            q_ring.relay(0, 1, 2, 3)
 
         @pl.when(step == 6)
         def _():
-            kv_ring.last()
-
-        @pl.when(step == 7)
-        def _():
-            kv_ring.arrive(12, 13)
+            kv_ring.relay_far()
+            q_ring.relay_far()
+
+        at_steps(step, kv_ring)
 
         @pl.when(j <= own)
         def _():
@@ -331,20 +349,17 @@
     gated = (normed * gate).astype(BF16)
     dy = dot_t(og_ref[...], w_ref[...])
     da[...] = norm_back(dy * gate, normed, spread).astype(BF16)
-    q_ring.first()
     da_ring.start()
     split(da[...] * 0.0625, 2)
     dhu_ref[...] = dy * normed
     out_ref[...] = (dot(gated, w_ref[...]) + x_ref[...].astype(F32)).astype(BF16)
     gout_ref[...] = lax.dot_general(gated, og_ref[...], (((0,), (0,)), ((), ())), preferred_element_type=F32)
-    q_ring.second()
-
     def by_query(step, carry):
-        j = block_at(step)
-
-        @pl.when(step == 4)
-        def _():
-            q_ring.last()
+        j = block_at(step, False)
+
+        @pl.when(step == 1)
+        def _():
+            da_ring.relay(0)
 
         @pl.when(j <= own)
         def _():
@@ -368,41 +383,22 @@
     lax.fori_loop(0, span, by_query, 0)
 
     def by_key(step, carry):
-        i = block_at(step)
+        i = block_at(step, True)
 
         @pl.when(step == 0)
         def _():
             q_ring.own().wait()
             da_ring.own().wait()
 
-        @pl.when(step == 1)
-        def _():
-            q_ring.arrive(4, 5)
-            da_ring.arrive(4, 5)
-
         @pl.when(step == 2)
         def _():
-            da_ring.first()
-            da_ring.second()
-
-        @pl.when(step == 3)
-        def _():
-            q_ring.arrive(8, 9)
-            da_ring.arrive(8, 9)
-
-        @pl.when(step == 5)
-        def _():
-            q_ring.arrive(10, 11)
-            da_ring.arrive(10, 11)
+            da_ring.relay(1, 2, 3)
 
         @pl.when(step == 6)
         def _():
-            da_ring.last()
-
-        @pl.when(step == 7)
-        def _():
-            q_ring.arrive(12, 13)
-            da_ring.arrive(12, 13)
+            da_ring.relay_far()
+
+        at_steps(step, q_ring, da_ring)
 
         @pl.when(i >= own)
         def _():
@@ -430,7 +426,7 @@
         ring.sent()
 
 
-def finish_kernel(
+def finish(
     z_ref, dhu_ref, dv_ref, dq_ref, dk_ref, x_ref, w_ref, og_ref, tr_ref, gout_ref, grads_ref, send_ref, hold, *, rows
 ):
     size, width = x_ref.shape
@@ -464,9 +460,9 @@
             place(hold[...], part, 0)
         dxn += dot_t(dz, w_ref[:, cols])
     dx = norm_back(dxn, normed, spread) + og_ref[...].astype(F32)
-    count = send_ref.shape[0]
+    count = send_ref.shape[0] * send_ref.shape[1]
     pick = jnp.where(iota((count, size), 0) == tr_ref[...], 1.0, 0.0).astype(BF16)
-    send_ref[...] = dot(pick, dx.astype(BF16)).astype(BF16)
+    send_ref[...] = dot(pick, dx.astype(BF16)).astype(BF16).reshape(send_ref.shape)
 
 
 def partner(k, groups, span):
@@ -486,7 +482,7 @@
         return carry
 
     lax.fori_loop(1, groups * span, hello, 0)
-    pl.semaphore_wait(barrier, groups * span - 1)
+    return lambda: pl.semaphore_wait(barrier, groups * span - 1)
 
 
 def drain(ref, count, sem):
@@ -494,14 +490,13 @@
     pltpu.make_async_copy(part, part, sem).wait()
 
 
-def tail_kernel(rows_ref, grads_ref, back_ref, parts_ref, got, part, sems, *, groups, span):
+def exchange_gradients(rows_ref, grads_ref, back_ref, parts_ref, got, part, sems, *, groups, span):
     total = groups * span
     g, p = lax.axis_index("dp"), lax.axis_index("pair")
     me, core = g * span + p, p % 2
     chip, chips = me // 2, total // 2
     own = pltpu.make_async_copy(rows_ref.at[me], back_ref.at[me], sems.at[0])
     own.start()
-    greet(groups, span)
     swap = pltpu.make_async_remote_copy(
         src_ref=grads_ref.at[1 - core],
         dst_ref=got,
@@ -556,7 +551,7 @@
     drain(parts_ref, chips - 1, sems.at[7])
 
 
-def update_kernel(
+def update(
     slots_ref, back_ref, table_ref, accum_ref, parts_ref, tnew_ref, anew_ref, gin_ref, gout_ref, *, width, factor
 ):
     shards = slots_ref.shape[0]
@@ -569,7 +564,7 @@
     mine = iota((128, count), 0) == (iota((128, count), 1) % width)
     slot = jnp.sum(jnp.where(mine, value, 0.0), axis=0, keepdims=True).astype(I32)
     pick = jnp.where(iota((rows_dev, count), 0) == slot, 1.0, 0.0).astype(BF16)
-    total = dot(pick, back_ref[...])
+    total = dot(pick, back_ref[...].reshape(count, model))
     square = jnp.mean(total * total, axis=1, keepdims=True)
     eye = iota((rows_dev, rows_dev), 0) == iota((rows_dev, rows_dev), 1)
     accum = jnp.sum(jnp.where(eye, accum_ref[...], 0.0), axis=1, keepdims=True) + square
@@ -588,6 +583,25 @@
     gin_ref[:, 2 * model + model // 2 : 3 * model] = lower[:, 2 * model :]
     gin_ref[:, 3 * model :] = lower[:, :model]
     gout_ref[...] = lower[:, model : 2 * model]
+
+
+def layer_kernel(
+    meta_ref, fetched_ref, tc_ref, tr_ref, w_in_ref, w_out_ref, og_ref, slots_ref, table_ref, accum_ref, out_ref,
+    tnew_ref, anew_ref, gin_ref, gout_ref, x, z, u, q, kv, dhu, wgrad, dq, dk, dv, kv_all, q_all, da_all, da, parts, acc,
+    mask, grads, hold, sending, back, got, part, landed, local, send, recv, sems, *, groups, span, width, rows, factor
+):
+    ready = greet(groups, span)
+    project(fetched_ref, tc_ref, w_in_ref, x, z, u, q, kv)
+    ready()
+    attend(
+        meta_ref, q, kv, u, x, w_out_ref, og_ref, out_ref, dhu, wgrad, dq, dk, dv, kv_all, q_all, da_all, da, parts, acc,
+        mask, local, send, recv, span=span
+    )
+    finish(z, dhu, dv, dq, dk, x, w_in_ref, og_ref, tr_ref, wgrad, grads, sending, hold, rows=rows)
+    exchange_gradients(sending, grads, back, landed, got, part, sems, groups=groups, span=span)
+    update(
+        slots_ref, back, table_ref, accum_ref, landed, tnew_ref, anew_ref, gin_ref, gout_ref, width=width, factor=factor
+    )
 
 
 def shape(dims, dtype):
@@ -633,83 +647,63 @@
     )(slots, table)
     fetched = lax.all_to_all(
         found.reshape(shards, width, model), everyone, split_axis=0, concat_axis=0, tiled=True
-    ).reshape(count, model)
-    x, z, u, q, kv = pl.pallas_call(
-        project_kernel,
+    )
+    rows = model // shards
+    chunk = (2 * rows, 5 * model // 2)
+    half_grads = (shards // 2,) + chunk
+    block = lambda cols: VMEM((span, tokens, cols), BF16)
+    low = lambda cols: VMEM((tokens, cols), BF16)
+    high = lambda cols: VMEM((tokens, cols), F32)
+    layer_out, table_new, accum_new, grad_in, grad_out = pl.pallas_call(
+        functools.partial(
+            layer_kernel,
+            groups=shards // span,
+            span=span,
+            width=width,
+            rows=rows,
+            factor=1.0 / math.sqrt(tokens * shards),
+        ),
         out_shape=(
             shape((tokens, model), BF16),
-            shape((tokens, 4 * model), F32),
-            shape((tokens, model), BF16),
-            shape((tokens, model), BF16),
-            shape((tokens, 2 * model), BF16),
-        ),
-        in_specs=[whole()] * 3,
-        out_specs=[whole()] * 5,
-        compiler_params=params(),
-    )(fetched, target_c, w_in)
-
-    block = lambda cols, dtype: VMEM((span, tokens, cols), dtype)
-    layer_out, dhu, gout, dq, dk, dv = pl.pallas_call(
-        functools.partial(attend_kernel, span=span),
-        out_shape=(
-            shape((tokens, model), BF16),
-            shape((tokens, model), F32),
-            shape((model, model), F32),
-            shape((tokens, model), F32),
-            shape((tokens, model), F32),
-            shape((tokens, model), F32),
-        ),
-        in_specs=[pl.BlockSpec(memory_space=pltpu.SMEM)] + [whole()] * 6,
-        out_specs=[whole()] * 6,
-        scratch_shapes=[
-            block(2 * model, BF16),
-            block(model, BF16),
-            block(model, BF16),
-            VMEM((tokens, model), BF16),
-            VMEM((8, tokens, model), BF16),
-            VMEM((tokens, model), F32),
-            VMEM((tokens, tokens), F32),
-            pltpu.SemaphoreType.DMA((3,)),
-            pltpu.SemaphoreType.DMA((3, 14)),
-            pltpu.SemaphoreType.DMA((3, 14)),
-        ],
-        compiler_params=params(collective_id=1, has_side_effects=True),
-    )(meta, q, kv, u, x, w_out, out_grad)
-
-    rows = model // shards
-    chunk = (2 * rows, 5 * model // 2)
-    grads, send = pl.pallas_call(
-        functools.partial(finish_kernel, rows=rows),
-        out_shape=(shape((2, shards // 2) + chunk, F32), shape((count, model), BF16)),
-        in_specs=[whole()] * 10,
-        out_specs=[whole()] * 2,
-        scratch_shapes=[VMEM((model, model), F32)],
-        compiler_params=params(),
-    )(z, dhu, dv, dq, dk, x, w_in, out_grad, target_r, gout)
-    back, parts = pl.pallas_call(
-        functools.partial(tail_kernel, groups=shards // span, span=span),
-        out_shape=(shape((shards, width, model), BF16), shape((shards // 2,) + chunk, BF16)),
-        in_specs=[whole()] * 2,
-        out_specs=[whole()] * 2,
-        scratch_shapes=[
-            VMEM((shards // 2,) + chunk, F32),
-            VMEM((shards // 2,) + chunk, BF16),
-            pltpu.SemaphoreType.DMA((8,)),
-        ],
-        compiler_params=params(collective_id=0, has_side_effects=True),
-    )(send.reshape(shards, width, model), grads)
-    table_new, accum_new, grad_in, grad_out = pl.pallas_call(
-        functools.partial(update_kernel, width=width, factor=1.0 / math.sqrt(tokens * shards)),
-        out_shape=(
             shape((rows_dev, model), F32),
             shape((1, rows_dev), F32),
             shape((rows, 4 * model), F32),
             shape((rows, model), F32),
         ),
-        in_specs=[whole()] * 5,
-        out_specs=[whole()] * 4,
-        compiler_params=params(),
-    )(slots, back.reshape(count, model), table, accum.reshape(1, rows_dev), parts)
+        in_specs=[pl.BlockSpec(memory_space=pltpu.SMEM)] + [whole()] * 9,
+        out_specs=[whole()] * 5,
+        scratch_shapes=[
+            low(model),
+            high(4 * model),
+            low(model),
+            low(model),
+            low(2 * model),
+            high(model),
+            VMEM((model, model), F32),
+            high(model),
+            high(model),
+            high(model),
+            block(2 * model),
+            block(model),
+            block(model),
+            low(model),
+            VMEM((8, tokens, model), BF16),
+            high(model),
+            high(tokens),
+            VMEM((2,) + half_grads, F32),
+            VMEM((model, model), F32),
+            VMEM((shards, width, model), BF16),
+            VMEM((shards, width, model), BF16),
+            VMEM(half_grads, F32),
+            VMEM(half_grads, BF16),
+            VMEM(half_grads, BF16),
+            pltpu.SemaphoreType.DMA((3,)),
+            pltpu.SemaphoreType.DMA((3, 14)),
+            pltpu.SemaphoreType.DMA((3, 14)),
+            pltpu.SemaphoreType.DMA((8,)),
+        ],
+        compiler_params=params(collective_id=0, has_side_effects=True),
+    )(meta, fetched, target_c, target_r, w_in, w_out, out_grad, slots, table, accum.reshape(1, rows_dev))
     return layer_out, table_new, accum_new.reshape(rows_dev), grad_in, grad_out
 
 

time: 207 us -> 182 us (0.88)
  Pallas kernels: 157 us -> 125 us
  local copies, waits for them, and re-layouts: 4.11 us -> 9.2 us
    pallas_call x5 -> x1, Pallas kernels: 152 us -> 120 us  [body(): pl.pallas_call(functools.partial(layer_kernel, groups=shards // span, spa...]
    unnamed x3 -> x11, local copies, waits for them, and re-layouts: 0.75 us -> 5.84 us
where the time goes in v4:
time: 182 us; the launch traced here: 180 us
  Pallas kernels  125 us (69%)
  blocking collectives  45.1 us (25%)
  local copies, waits for them, and re-layouts  9.2 us (5%)
    pallas_call x1, Pallas kernels, body(): pl.pallas_call(functools.partial(layer_kernel, groups=shards // span, spa...  120 us
    all_to_all x1, blocking collectives, body(): lax.all_to_all(found.reshape(shards, width, model), everyone, split_axis=...  24.1 us
    all_to_all x1, blocking collectives, body(): lax.all_to_all(request[:, :width], everyone, split_axis=0, concat_axis=0,...  21.1 us
    unnamed x11, local copies, waits for them, and re-layouts  5.84 us

profile of v4, /device:TPU:1, one launch (start us, length us, event | category | flops | bytes accessed | tf_op | source)
XLA Modules:
  0.0 179.8 jit_solution(5400845244784910489)
XLA Ops:
  0.6 1.2 reshape.27.row_ref
  1.9 1.5 reshape.32.col_ref
  3.4 2.0 %shard_map.119 = (s32[128,128]{1,0:T(8,128)}, s32[1,384]{1,0:T(1,128)}, s32[384,1]{1,0:T(8,128)}, s32[8,128]{1,0:T(8,128)}) custom-call(s32[1,384]{1,0:T(1,128)} %reshape.27.row_ref, s32[384,1]{1,0:T(8,128)} %reshape.32.col_ref, s32[1,3072]{1,0:T(1,128)} %seg_ref.1, s32[2,40]{1,0:T(2,128)} %bitcast.16), custom_call_target="tpu_custom_call" | custom-call | tf_op jit(solution)/shard_map/pallas_call | solution.py:636
  5.3 21.1 %all_to_all.17 = s32[128,1,8]{2,1,0:T(1,128)S(1)} all-to-all(s32[128,1,8]{2,1,0:T(1,128)} %bitcast.13), channel_id=1, replica_groups=mesh['dp'=16,'pair'=8] {'dp','pair'}, dimensions={0} | all-to-all | bytes 8192 | tf_op jit(solution)/shard_map/all_to_all | solution.py:639
  26.4 0.6 pad.4.slots_ref
  27.0 3.2 %shard_map.120 = bf16[1024,512]{1,0:T(8,128)(2,1)} custom-call(s32[128,128]{1,0:T(8,128)} %pad.4.slots_ref, f32[512,512]{1,0:T(8,128)} %table_ref.3), custom_call_target="tpu_custom_call" | custom-call | tf_op jit(solution)/shard_map/pallas_call | solution.py:641
  30.2 24.1 %all_to_all.18.fetched_ref = bf16[128,8,512]{2,1,0:T(8,128)(2,1)} all-to-all(bf16[128,8,512]{2,1,0:T(8,128)(2,1)} %bitcast.11), channel_id=1, replica_groups=mesh['dp'=16,'pair'=8] {'dp','pair'}, dimensions={0} | all-to-all | bytes 2097152 | tf_op jit(solution)/shard_map/all_to_all | solution.py:648
  54.2 119.7 %shard_map.121 = (bf16[384,512]{1,0:T(8,128)(2,1)}, f32[512,512]{1,0:T(8,128)}, f32[1,512]{1,0:T(1,128)}, f32[4,2048]{1,0:T(4,128)}, f32[4,512]{1,0:T(4,128)}) custom-call(s32[8,128]{1,0:T(8,128)} %get-tuple-element.14.meta_ref, bf16[128,8,512]{2,1,0:T(8,128)(2,1)} %all_to_all.18.fetched_ref, s32[384,1]{1,0:T(8,128)} %get-tuple-element.16.tc_ref, ...), custom_call_target="tpu_custom_call" | custom-call | tf_op jit(solution)/shard_map/pallas_call | solution.py:657
  173.9 0.0 copy-start.2
  173.9 0.0 copy-start
  173.9 0.0 copy-start.1
  174.0 1.8 copy.21
  175.7 2.3 %copy.22 = f32[512,512]{1,0:T(8,128)} copy(f32[512,512]{1,0:T(8,128)} %get-tuple-element.29) | data formatting | bytes 2097152
  178.0 0.0 copy-done.2
  178.0 0.6 copy.23
  178.6 0.0 copy-done
  178.6 0.6 copy.24
  179.2 0.0 copy-done.1
  179.2 0.6 copy.25
Async XLA Ops:
  173.9 4.1 %copy-start.2 = (f32[1,512]{1,0:T(1,128)S(1)}, f32[1,512]{1,0:T(1,128)}, u32[]{:S(2)}) copy-start(f32[1,512]{1,0:T(1,128)} %get-tuple-element.20) | copy-start | bytes 6148
  173.9 4.6 %copy-start = (f32[4,2048]{1,0:T(4,128)S(1)}, f32[4,2048]{1,0:T(4,128)}, u32[]{:S(2)}) copy-start(f32[4,2048]{1,0:T(4,128)} %get-tuple-element.31) | copy-start | bytes 98308
  173.9 5.3 %copy-start.1 = (f32[4,512]{1,0:T(4,128)S(1)}, f32[4,512]{1,0:T(4,128)}, u32[]{:S(2)}) copy-start(f32[4,512]{1,0:T(4,128)} %get-tuple-element.32) | copy-start | bytes 24580

commit v5 on v4

--- a/solution.py
+++ b/solution.py
@@ -60,15 +60,15 @@
     return jnp.where(lane < 64, jnp.zeros_like(rows), rows)
 
 
-def route_kernel(rows_dev, row_ref, col_ref, seg_ref, pair_ref, req_ref, tr_ref, tc_ref, meta_ref, *, width):
+def route(row_ref, seg_ref, pair_ref, req_ref, tr_ref, tc_ref, meta_ref, *, rows_dev, width):
     tokens = row_ref.shape[1]
     shards = req_ref.shape[0]
     shift = rows_dev.bit_length() - 1
+    sub, lane = iota((tokens, tokens), 0), iota((tokens, tokens), 1)
     owner_r = row_ref[...] >> shift
     slot_r = (row_ref[...] & (rows_dev - 1)).astype(F32)
-    owner_c = col_ref[...] >> shift
+    owner_c = jnp.sum(jnp.where(sub == lane, owner_r.astype(F32), 0.0), axis=1, keepdims=True).astype(I32)
     same = owner_c == owner_r
-    sub, lane = iota((tokens, tokens), 0), iota((tokens, tokens), 1)
     rank_c = jnp.sum(jnp.where(same & (lane < sub), 1.0, 0.0), axis=1, keepdims=True).astype(I32)
     rank_r = jnp.sum(jnp.where(same & (sub < lane), 1.0, 0.0), axis=0, keepdims=True).astype(I32)
     tr_ref[...] = owner_r * width + rank_r
@@ -79,7 +79,7 @@
     for k in range(2 * tokens // shards):
         picked = jnp.sum(jnp.where(dest & (rank_r == k), slot_r, 0.0), axis=1, keepdims=True)
         req = jnp.where(place == k, picked, req)
-    req_ref[...] = req.astype(I32)
+    req_ref[...] = req.astype(I32).reshape(req_ref.shape)
     own = lax.axis_index("pair")
     first, second = pair_ref[0:1, :], pair_ref[1:2, :]
     span = iota((8, first.shape[1]), 0)
@@ -87,8 +87,7 @@
     as_key = jnp.max(jnp.where((second == own) & (first == span), 1.0, 0.0), axis=1, keepdims=True)
     zeros = jnp.sum(jnp.where(seg_ref[...] == 0, 1.0, 0.0), axis=1, keepdims=True)
     at = iota((8, 128), 1)
-    meta = jnp.where(at == 0, as_query, jnp.where(at == 1, as_key, jnp.where(at == 2, zeros, 0.0))).astype(I32)
-    meta_ref[...] = jnp.where(at == 3, own, meta)
+    meta_ref[...] = jnp.where(at == 0, as_query, jnp.where(at == 1, as_key, jnp.where(at == 2, zeros, 0.0)))
 
 
 def slot_halves(slots):
@@ -97,17 +96,17 @@
     return high, low
 
 
-def find_kernel(slots_ref, table_ref, found_ref, *, width):
+def find(slots_ref, table_ref, found_ref, *, width):
     shards = slots_ref.shape[0]
     rows_dev = table_ref.shape[0]
     count = shards * width
     spread = ((iota((count, shards), 0) // width) == iota((count, shards), 1)).astype(F32).astype(BF16)
-    high, low = slot_halves(slots_ref[...])
+    high, low = slot_halves(slots_ref[...].reshape(shards, 128))
     value = 2.0 * dot(spread, high) + dot(spread, low)
     mine = iota((count, 128), 1) == (iota((count, 128), 0) % width)
     slot = jnp.sum(jnp.where(mine, value, 0.0), axis=1, keepdims=True).astype(I32)
     pick = jnp.where(iota((count, rows_dev), 1) == slot, 1.0, 0.0).astype(BF16)
-    found_ref[...] = dot(pick, table_ref[...].astype(BF16)).astype(BF16)
+    found_ref[...] = dot(pick, table_ref[...].astype(BF16)).astype(BF16).reshape(found_ref.shape)
 
 
 def project(fetched_ref, tc_ref, w_ref, x_ref, z_ref, u_ref, q_ref, kv_ref):
@@ -120,11 +119,14 @@
     normed, _ = normalize(rows)
     low = normed.astype(BF16)
     outs = (u_ref.at[...], kv_ref.at[:, width:], q_ref.at[...], kv_ref.at[:, :width])
-    for g in range(4):
+
+    def group(g):
         z = dot(low, w_ref[:, g * width : (g + 1) * width])
         z_ref[:, g * width : (g + 1) * width] = z
         half = 0.5 * z
         outs[g][...] = (half + half * jnp.tanh(half)).astype(BF16)
+
+    return group
 
 
 def visible(q_axis, size, q_block, k_block, zeros):
@@ -135,7 +137,8 @@
 
 
 class Ring:
-    SENDS = ((0, 1, 2, 3, 4, 5, 7), (0, 1, 2, 4, 5, 6, 8, 9), (0, 1, 4, 5, 6, 8, 9, 12, 13), (4, 5, 7, 8, 9, 10, 11, 12, 13))
+    RISING = (0, 1, 2, 3, 4, 5, 7), (0, 1, 2, 4, 5, 6, 8, 9), (0, 1, 4, 5, 6, 8, 9, 12, 13), (4, 5, 7, 8, 9, 10, 11, 12, 13)
+    FALLING = (0, 1, 2, 3, 4, 5), (0, 1, 4, 5, 6, 8, 9), (0, 1, 4, 5, 6, 14, 8, 9, 12, 13), (4, 5, 7, 8, 9, 10, 11, 12, 13)
 
     def __init__(self, source, gathered, send, recv, local, span, falling):
         self.source, self.gathered, self.send, self.recv, self.local = source, gathered, send, recv, local
@@ -145,6 +148,7 @@
         at = lambda step: ((chip + step) % chips) * 2 + core
         self.up, self.down, self.far = at(chips - 1 if falling else 1), at(1 if falling else chips - 1), at(2)
         self.rank = chips - 1 - chip if falling else chip
+        self.falling, self.sends = falling, self.FALLING if falling else self.RISING
         self.other = chip * 2 + 1 - core
 
     def copy(self, i):
@@ -164,6 +168,7 @@
             (up, 0, other),
             (far, 0, other),
             (far, 1, other),
+            (down, 1, up),
         )[i]
         half = self.source.shape[0] // 2
         rows = pl.ds(part * half, half)
@@ -192,7 +197,7 @@
         @self.when(0, 1, 2, 3)
         def _(rank):
             for i in (0, 2, 1, 3, 4, 5):
-                if i in self.SENDS[rank]:
+                if i in self.sends[rank]:
                     self.copy(i).start()
 
     def arrive(self, *which):
@@ -204,57 +209,59 @@
         for i in sent:
             self.copy(i).start()
 
-    def relay(self, *ranks):
-        @self.when(*ranks)
+    def relay_near(self):
+        @self.when(0, 1, 2, 3)
         def _(rank):
             if rank == 0:
-                self.after(2, 7)
+                if not self.falling:
+                    self.after(2, 7)
             elif rank == 3:
-                self.after(2, 7, 10)
                 self.after(0, 8)
-                self.after(3, 11)
                 self.after(1, 9)
             else:
                 self.after(0, 6, 8)
-                self.after(1, 9)
+                self.after(1, *((14, 9) if self.falling and rank == 2 else (9,)))
+
+    def relay_wrap(self):
+        @self.when(3)
+        def _(rank):
+            self.after(2, 7, 10)
+            self.after(3, 11)
 
     def relay_far(self):
         @self.when(2, 3)
         def _(rank):
             self.after(6, 12)
-            self.after(7, 13)
-
-    def handed(self, step):
-        if step == 1:
-            self.arrive(4, 5)
-        elif step == 3:
-
-            @self.when(1, 2, 3)
-            def _(rank):
-                self.arrive(8, 9)
-
-        elif step == 5:
-
-            @self.when(3)
-            def _(rank):
-                self.arrive(10, 11)
-
-        elif step == 7:
-
-            @self.when(2, 3)
-            def _(rank):
-                self.arrive(12, 13)
+            self.after(14 if self.falling and rank == 3 else 7, 13)
+
+    def handed_own(self):
+        self.arrive(4, 5)
+
+    def handed_near(self):
+        @self.when(1, 2, 3)
+        def _(rank):
+            self.arrive(8, 9)
+
+    def handed_wrap(self):
+        @self.when(3)
+        def _(rank):
+            self.arrive(10, 11)
+
+    def handed_far(self):
+        @self.when(2, 3)
+        def _(rank):
+            self.arrive(12, 13)
 
     def sent(self):
         @self.when(0, 1, 2, 3)
         def _(rank):
-            for i in self.SENDS[rank]:
+            for i in self.sends[rank]:
                 self.copy(i).wait_send()
 
 
 def attend(
     meta_ref, q_ref, kv_ref, u_ref, x_ref, w_ref, og_ref, out_ref, dhu_ref, gout_ref, dq_ref, dk_ref, dv_ref, kv_all,
-    q_all, da_all, da, parts, acc, mask, local, send, recv, *, span
+    q_all, da_all, da, parts, acc, mask, local, send, recv, group, *, span
 ):
     own = lax.axis_index("pair")
     chips, core, chip = span // 2, own % 2, own // 2
@@ -265,22 +272,21 @@
             ((kv_ref, kv_all, False), (q_ref, q_all, True), (da, da_all, True))
         )
     )
+    for g in (3, 1, 2):
+        group(g)
     kv_ring.start()
     q_ring.start()
-
-    def at_steps(step, *rings):
-        for k in (1, 3, 5, 7):
-
-            @pl.when(step == k)
-            def _():
-                for ring in rings:
-                    ring.handed(k)
+    group(0)
+    dhu_ref[...] = dot_t(og_ref[...], w_ref[...])
+
+    def on_step(step, *actions):
+        for k, action in enumerate(actions):
+            if action:
+                pl.when(step == k)(action)
 
     def block_at(step, falling):
         turn = step // 2
-        shift = (3 * turn - (turn * (turn - 1)) // 2) % 4
-        if falling:
-            shift = (chips - shift) % chips
+        shift = turn if falling else (3 * turn - (turn * (turn - 1)) // 2) % 4
         return ((chip + shift) % chips) * 2 + (core + step % 2) % 2
 
     def split(value, at):
@@ -298,7 +304,7 @@
     def both(rows):
         return jnp.concatenate([even_half(rows), odd_half(rows)], axis=0)
 
-    zeros = meta_ref[0, 2]
+    zeros = meta_ref[0:1, 2:3].astype(I32)
     split(q_ref[...] * 0.0625, 0)
     split(kv_ref[:, :width] * 0.0625, 4)
     split(kv_ref[:, width:] * 0.0625, 6)
@@ -310,25 +316,24 @@
     def forward(step, carry):
         j = block_at(step, False)
 
-        @pl.when(step == 0)
-        def _():
-            kv_ring.own().wait()
-
-        @pl.when(step == 2)
-        def _():
-            kv_ring.relay(0, 1, 2, 3)
-            q_ring.relay(0, 1, 2, 3)
-
-        @pl.when(step == 6)
-        def _():
+        def near():
+            kv_ring.relay_wrap()
+            kv_ring.relay_near()
+            q_ring.relay_near()
+            q_ring.relay_wrap()
+
+        def far():
             kv_ring.relay_far()
             q_ring.relay_far()
 
-        at_steps(step, kv_ring)
+        on_step(
+            step, kv_ring.own().wait, kv_ring.handed_own, near, kv_ring.handed_near, None, kv_ring.handed_wrap, far,
+            kv_ring.handed_far
+        )
 
         @pl.when(j <= own)
         def _():
-            mask[...] = visible(0, size, own, j, zeros) * meta_ref[j, 0].astype(F32)
+            mask[...] = visible(0, size, own, j, zeros) * meta_ref[pl.ds(j, 1), 0:1]
 
             def work(cols, late):
                 keys = kv_all[j, :, cols]
@@ -347,7 +352,7 @@
     normed, spread = normalize(acc[...])
     gate = u_ref[...].astype(F32)
     gated = (normed * gate).astype(BF16)
-    dy = dot_t(og_ref[...], w_ref[...])
+    dy = dhu_ref[...]
     da[...] = norm_back(dy * gate, normed, spread).astype(BF16)
     da_ring.start()
     split(da[...] * 0.0625, 2)
@@ -357,13 +362,9 @@
     def by_query(step, carry):
         j = block_at(step, False)
 
-        @pl.when(step == 1)
-        def _():
-            da_ring.relay(0)
-
         @pl.when(j <= own)
         def _():
-            mask[...] = visible(0, size, own, j, zeros) * meta_ref[j, 0].astype(F32)
+            mask[...] = visible(0, size, own, j, zeros) * meta_ref[pl.ds(j, 1), 0:1]
 
             def work(cols, late):
                 keys = kv_all[j, :, cols]
@@ -385,24 +386,25 @@
     def by_key(step, carry):
         i = block_at(step, True)
 
-        @pl.when(step == 0)
-        def _():
+        def mine():
             q_ring.own().wait()
             da_ring.own().wait()
 
-        @pl.when(step == 2)
-        def _():
-            da_ring.relay(1, 2, 3)
-
-        @pl.when(step == 6)
-        def _():
-            da_ring.relay_far()
-
-        at_steps(step, q_ring, da_ring)
+        def pair(name):
+            def action():
+                getattr(q_ring, name)()
+                getattr(da_ring, name)()
+
+            return action
+
+        on_step(
+            step, mine, pair("handed_own"), da_ring.relay_near, pair("handed_near"), da_ring.relay_far, pair("handed_far"),
+            da_ring.relay_wrap, pair("handed_wrap")
+        )
 
         @pl.when(i >= own)
         def _():
-            mask[...] = visible(1, size, i, own, zeros) * meta_ref[i, 1].astype(F32)
+            mask[...] = visible(1, size, i, own, zeros) * meta_ref[pl.ds(i, 1), 1:2]
 
             def work(cols, late):
                 queries = q_all[i, :, cols]
@@ -490,13 +492,44 @@
     pltpu.make_async_copy(part, part, sem).wait()
 
 
-def exchange_gradients(rows_ref, grads_ref, back_ref, parts_ref, got, part, sems, *, groups, span):
+def push_all(source, target, send, recv, groups, span, rows):
+    me = lax.axis_index("dp") * span + lax.axis_index("pair")
+    used = pl.ds(0, rows)
+
+    def push(k, carry):
+        to_g, to_p = partner(k, groups, span)
+        pltpu.make_async_remote_copy(
+            src_ref=source.at[to_g * span + to_p, used],
+            dst_ref=target.at[me, used],
+            send_sem=send,
+            recv_sem=recv,
+            device_id=(to_g, to_p),
+            device_id_type=MESH,
+        ).start()
+        return carry
+
+    lax.fori_loop(1, groups * span, push, 0)
+
+    def wait():
+        all_of = target.at[pl.ds(0, groups * span - 1), used]
+        pltpu.make_async_copy(all_of, all_of, send).wait()
+        pltpu.make_async_copy(all_of, all_of, recv).wait()
+
+    return wait
+
+
+def keep(source, target, sem, span):
+    me = lax.axis_index("dp") * span + lax.axis_index("pair")
+    copy = pltpu.make_async_copy(source.at[me], target.at[me], sem)
+    copy.start()
+    return copy
+
+
+def exchange_gradients(rows_ref, grads_ref, back_ref, parts_ref, got, part, sems, *, groups, span, bound):
     total = groups * span
     g, p = lax.axis_index("dp"), lax.axis_index("pair")
     me, core = g * span + p, p % 2
     chip, chips = me // 2, total // 2
-    own = pltpu.make_async_copy(rows_ref.at[me], back_ref.at[me], sems.at[0])
-    own.start()
     swap = pltpu.make_async_remote_copy(
         src_ref=grads_ref.at[1 - core],
         dst_ref=got,
@@ -506,20 +539,8 @@
         device_id_type=MESH,
     )
     swap.start()
-
-    def push_rows(k, carry):
-        to_g, to_p = partner(k, groups, span)
-        pltpu.make_async_remote_copy(
-            src_ref=rows_ref.at[to_g * span + to_p],
-            dst_ref=back_ref.at[me],
-            send_sem=sems.at[3],
-            recv_sem=sems.at[4],
-            device_id=(to_g, to_p),
-            device_id_type=MESH,
-        ).start()
-        return carry
-
-    lax.fori_loop(1, total, push_rows, 0)
+    own = keep(rows_ref, back_ref, sems.at[0], span)
+    landed = push_all(rows_ref, back_ref, sems.at[3], sems.at[4], groups, span, bound)
     swap.wait()
 
     def add(m, carry):
@@ -545,8 +566,7 @@
     lax.fori_loop(1, chips, push_part, 0)
     own.wait()
     mine.wait()
-    drain(back_ref, total - 1, sems.at[3])
-    drain(back_ref, total - 1, sems.at[4])
+    landed()
     drain(parts_ref, chips - 1, sems.at[6])
     drain(parts_ref, chips - 1, sems.at[7])
 
@@ -558,7 +578,7 @@
     rows_dev, model = table_ref.shape
     count = shards * width
     spread = ((iota((shards, count), 1) // width) == iota((shards, count), 0)).astype(F32).astype(BF16)
-    high, low = slot_halves(slots_ref[...])
+    high, low = slot_halves(slots_ref[...].reshape(shards, 128))
     turn = lambda a: lax.dot_general(a, spread, (((0,), (0,)), ((), ())), preferred_element_type=F32)
     value = 2.0 * turn(high) + turn(low)
     mine = iota((128, count), 0) == (iota((128, count), 1) % width)
@@ -586,30 +606,43 @@
 
 
 def layer_kernel(
-    meta_ref, fetched_ref, tc_ref, tr_ref, w_in_ref, w_out_ref, og_ref, slots_ref, table_ref, accum_ref, out_ref,
-    tnew_ref, anew_ref, gin_ref, gout_ref, x, z, u, q, kv, dhu, wgrad, dq, dk, dv, kv_all, q_all, da_all, da, parts, acc,
-    mask, grads, hold, sending, back, got, part, landed, local, send, recv, sems, *, groups, span, width, rows, factor
+    row_ref, seg_ref, pair_ref, w_in_ref, w_out_ref, og_ref, table_ref, accum_ref, out_ref, tnew_ref, anew_ref, gin_ref,
+    gout_ref, request, slots, target_r, target_c, meta, found, fetched, x, z, u, q, kv, dhu, wgrad, dq, dk, dv, kv_all,
+    q_all, da_all, da, parts, acc, mask, grads, hold, sending, back, got, part, landed, local, send, recv, front, sems, *,
+    groups, span, width, rows, factor
 ):
+    tokens, rows_dev = row_ref.shape[1], table_ref.shape[0]
+    bound = 2 * tokens // (groups * span)
+    fetched[...] = jnp.zeros_like(fetched)
+    back[...] = jnp.zeros_like(back)
     ready = greet(groups, span)
-    project(fetched_ref, tc_ref, w_in_ref, x, z, u, q, kv)
+    route(row_ref, seg_ref, pair_ref, request, target_r, target_c, meta, rows_dev=rows_dev, width=width)
     ready()
+    own = keep(request, slots, front.at[0], span)
+    asked = push_all(request, slots, front.at[1], front.at[2], groups, span, 1)
+    own.wait()
+    asked()
+    find(slots, table_ref, found, width=width)
+    own = keep(found, fetched, front.at[3], span)
+    answered = push_all(found, fetched, front.at[4], front.at[5], groups, span, bound)
+    own.wait()
+    answered()
+    group = project(fetched, target_c, w_in_ref, x, z, u, q, kv)
     attend(
-        meta_ref, q, kv, u, x, w_out_ref, og_ref, out_ref, dhu, wgrad, dq, dk, dv, kv_all, q_all, da_all, da, parts, acc,
-        mask, local, send, recv, span=span
+        meta, q, kv, u, x, w_out_ref, og_ref, out_ref, dhu, wgrad, dq, dk, dv, kv_all, q_all, da_all, da, parts, acc,
+        mask, local, send, recv, group, span=span
     )
-    finish(z, dhu, dv, dq, dk, x, w_in_ref, og_ref, tr_ref, wgrad, grads, sending, hold, rows=rows)
-    exchange_gradients(sending, grads, back, landed, got, part, sems, groups=groups, span=span)
+    finish(z, dhu, dv, dq, dk, x, w_in_ref, og_ref, target_r, wgrad, grads, sending, hold, rows=rows)
+    exchange_gradients(
+        sending, grads, back, landed, got, part, sems, groups=groups, span=span, bound=bound
+    )
     update(
-        slots_ref, back, table_ref, accum_ref, landed, tnew_ref, anew_ref, gin_ref, gout_ref, width=width, factor=factor
+        slots, back, table_ref, accum_ref, landed, tnew_ref, anew_ref, gin_ref, gout_ref, width=width, factor=factor
     )
 
 
 def shape(dims, dtype):
     return jax.ShapeDtypeStruct(dims, dtype)
-
-
-def cost(flops, moved):
-    return pl.CostEstimate(flops=flops, bytes_accessed=moved, transcendentals=0)
 
 
 def body(table, accum, item_row, segments, pairs, w_in, w_out, out_grad):
@@ -618,36 +651,6 @@
     shards = lax.axis_size(("dp", "pair"))
     span = lax.axis_size("pair")
     width = -(-(2 * tokens // shards) // 8) * 8
-    count = shards * width
-    everyone = ("dp", "pair")
-
-    call = pl.pallas_call(
-        functools.partial(route_kernel, rows_dev, width=width),
-        out_shape=(
-            shape((shards, 128), I32),
-            shape((1, tokens), I32),
-            shape((tokens, 1), I32),
-            shape((8, 128), I32),
-        ),
-        in_specs=[whole()] * 4,
-        out_specs=[whole()] * 4,
-        compiler_params=params(),
-    )
-    request, target_r, target_c, meta = call(
-        item_row.reshape(1, tokens), item_row.reshape(tokens, 1), segments, pairs[0].T
-    )
-    asked = lax.all_to_all(request[:, :width], everyone, split_axis=0, concat_axis=0, tiled=True)
-    slots = jnp.pad(asked, ((0, 0), (0, 128 - width)))
-    found = pl.pallas_call(
-        functools.partial(find_kernel, width=width),
-        out_shape=shape((count, model), BF16),
-        in_specs=[whole()] * 2,
-        out_specs=whole(),
-        compiler_params=params(),
-    )(slots, table)
-    fetched = lax.all_to_all(
-        found.reshape(shards, width, model), everyone, split_axis=0, concat_axis=0, tiled=True
-    )
     rows = model // shards
     chunk = (2 * rows, 5 * model // 2)
     half_grads = (shards // 2,) + chunk
@@ -670,9 +673,16 @@
             shape((rows, 4 * model), F32),
             shape((rows, model), F32),
         ),
-        in_specs=[pl.BlockSpec(memory_space=pltpu.SMEM)] + [whole()] * 9,
+        in_specs=[whole()] * 8,
         out_specs=[whole()] * 5,
         scratch_shapes=[
+            VMEM((shards, 1, 128), I32),
+            VMEM((shards, 1, 128), I32),
+            VMEM((1, tokens), I32),
+            VMEM((tokens, 1), I32),
+            VMEM((8, 128), F32),
+            VMEM((shards, width, model), BF16),
+            VMEM((shards, width, model), BF16),
             low(model),
             high(4 * model),
             low(model),
@@ -698,12 +708,13 @@
             VMEM(half_grads, BF16),
             VMEM(half_grads, BF16),
             pltpu.SemaphoreType.DMA((3,)),
-            pltpu.SemaphoreType.DMA((3, 14)),
-            pltpu.SemaphoreType.DMA((3, 14)),
+            pltpu.SemaphoreType.DMA((3, 15)),
+            pltpu.SemaphoreType.DMA((3, 15)),
+            pltpu.SemaphoreType.DMA((6,)),
             pltpu.SemaphoreType.DMA((8,)),
         ],
         compiler_params=params(collective_id=0, has_side_effects=True),
-    )(meta, fetched, target_c, target_r, w_in, w_out, out_grad, slots, table, accum.reshape(1, rows_dev))
+    )(item_row.reshape(1, tokens), segments, pairs[0].T, w_in, w_out, out_grad, table, accum.reshape(1, rows_dev))
     return layer_out, table_new, accum_new.reshape(rows_dev), grad_in, grad_out
 
 

time: 182 us -> 159 us (0.87); the launches traced: 180 us -> 159 us
  blocking collectives: 45.1 us -> 0 us
  Pallas kernels: 125 us -> 151 us
  local copies, waits for them, and re-layouts: 9.2 us -> 7.09 us
    all_to_all x2 -> x0, blocking collectives: 45.1 us -> none  [the longest x1 24.1 us: body(): lax.all_to_all(found.reshape(shards, width, model), everyone, split_axis=...]
    pallas_call x1, Pallas kernels: 120 us -> 151 us  [body(): pl.pallas_call(functools.partial(layer_kernel, groups=shards // span, spa...]
    pallas_call x2 -> x0, Pallas kernels: 5.13 us -> none  [the longest x1 3.17 us: body(): pl.pallas_call(functools.partial(find_kernel, width=width), out_shape=sha...]
where the time goes in v5:
time: 159 us
  Pallas kernels  151 us (95%)
  local copies, waits for them, and re-layouts  7.09 us (4%)
    pallas_call x1, Pallas kernels, body(): pl.pallas_call(functools.partial(layer_kernel, groups=shards // span, spa...  151 us
    unnamed x11, local copies, waits for them, and re-layouts  5.84 us

profile of v5, /device:TPU:1, one launch (start us, length us, event | category | flops | bytes accessed | tf_op | source)
XLA Modules:
  0.0 159.0 jit_solution(3324689271690151296)
XLA Ops:
  0.6 1.2 reshape.19.row_ref
  1.9 151.2 %shard_map.119 = (bf16[384,512]{1,0:T(8,128)(2,1)}, f32[512,512]{1,0:T(8,128)}, f32[1,512]{1,0:T(1,128)}, f32[4,2048]{1,0:T(4,128)}, f32[4,512]{1,0:T(4,128)}) custom-call(s32[1,384]{1,0:T(1,128)} %reshape.19.row_ref, s32[1,3072]{1,0:T(1,128)} %seg_ref.1, s32[2,40]{1,0:T(2,128)} %bitcast.7, bf16[512,2048]{1,0:T(8,128)(2,1)} %w_in_ref.1, ...), custom_call_target="tpu_custom_call" | custom-call | tf_op jit(solution)/shard_map/pallas_call | solution.py:660
  153.1 0.0 copy-start.2
  153.1 0.0 copy-start
  153.1 0.0 copy-start.1
  153.1 1.8 %copy.18 = bf16[384,512]{1,0:T(8,128)(2,1)} copy(bf16[384,512]{1,0:T(8,128)(2,1)} %get-tuple-element.20) | data formatting | bytes 786432
  154.9 2.3 %copy.19 = f32[512,512]{1,0:T(8,128)} copy(f32[512,512]{1,0:T(8,128)} %get-tuple-element.21) | data formatting | bytes 2097152
  157.2 0.0 copy-done.2
  157.2 0.6 copy.20
  157.7 0.0 copy-done
  157.7 0.6 copy.21
  158.4 0.0 copy-done.1
  158.4 0.6 copy.22
Async XLA Ops:
  153.1 4.1 %copy-start.2 = (f32[1,512]{1,0:T(1,128)S(1)}, f32[1,512]{1,0:T(1,128)}, u32[]{:S(2)}) copy-start(f32[1,512]{1,0:T(1,128)} %get-tuple-element.12) | copy-start | bytes 6148
  153.1 4.6 %copy-start = (f32[4,2048]{1,0:T(4,128)S(1)}, f32[4,2048]{1,0:T(4,128)}, u32[]{:S(2)}) copy-start(f32[4,2048]{1,0:T(4,128)} %get-tuple-element.23) | copy-start | bytes 98308
  153.1 5.3 %copy-start.1 = (f32[4,512]{1,0:T(4,128)S(1)}, f32[4,512]{1,0:T(4,128)}, u32[]{:S(2)}) copy-start(f32[4,512]{1,0:T(4,128)} %get-tuple-element.24) | copy-start | bytes 24580

commit v6 on v5

--- a/solution.py
+++ b/solution.py
@@ -62,7 +62,7 @@
 
 def route(row_ref, seg_ref, pair_ref, req_ref, tr_ref, tc_ref, meta_ref, *, rows_dev, width):
     tokens = row_ref.shape[1]
-    shards = req_ref.shape[0]
+    shards = req_ref.shape[0] * req_ref.shape[1]
     shift = rows_dev.bit_length() - 1
     sub, lane = iota((tokens, tokens), 0), iota((tokens, tokens), 1)
     owner_r = row_ref[...] >> shift
@@ -97,7 +97,7 @@
 
 
 def find(slots_ref, table_ref, found_ref, *, width):
-    shards = slots_ref.shape[0]
+    shards = slots_ref.shape[0] * slots_ref.shape[1]
     rows_dev = table_ref.shape[0]
     count = shards * width
     spread = ((iota((count, shards), 0) // width) == iota((count, shards), 1)).astype(F32).astype(BF16)
@@ -340,7 +340,7 @@
                 weights = []
                 for half in range(2):
                     h = dot_t(parts[half, :, cols], keys)
-                    weights.append(((h + h * jnp.tanh(h)) * mask[...]).astype(BF16))
+                    weights.append((h * ((1.0 + jnp.tanh(h)) * mask[...])).astype(BF16))
                 acc[:, cols] += dot(jnp.concatenate(weights, axis=1), both(kv_all[j, :, late]))
 
             slabs(work)
@@ -372,9 +372,10 @@
                 grads = []
                 for half in range(2):
                     h = dot_t(parts[half, :, cols], keys)
-                    t = jnp.tanh(h)
-                    slope = (1.0 + t) * (1.0 + h * (1.0 - t))
-                    grads.append((dot_t(parts[2 + half, :, cols], values) * slope * mask[...]).astype(BF16))
+                    u = 1.0 + jnp.tanh(h)
+                    seen = u * mask[...]
+                    slope = seen + h * seen * (2.0 - u)
+                    grads.append((dot_t(parts[2 + half, :, cols], values) * slope).astype(BF16))
                 dq_ref[:, cols] += dot(jnp.concatenate(grads, axis=1), both(keys))
 
             slabs(work)
@@ -412,10 +413,12 @@
                 grads, weights = [], []
                 for half in range(2):
                     h = dot_t(parts[4 + half, :, cols], queries)
-                    t = jnp.tanh(h)
-                    weights.append(((h + h * t) * mask[...]).astype(BF16))
-                    slope = (1.0 + t) * (1.0 + h * (1.0 - t))
-                    grads.append((dot_t(parts[6 + half, :, cols], dafter) * slope * mask[...]).astype(BF16))
+                    u = 1.0 + jnp.tanh(h)
+                    seen = u * mask[...]
+                    weight = h * seen
+                    weights.append(weight.astype(BF16))
+                    slope = seen + weight * (2.0 - u)
+                    grads.append((dot_t(parts[6 + half, :, cols], dafter) * slope).astype(BF16))
                 dk_ref[:, cols] += dot(jnp.concatenate(grads, axis=1), both(queries))
                 dv_ref[:, cols] += dot(jnp.concatenate(weights, axis=1), both(dafter))
 
@@ -477,14 +480,66 @@
 
 
 def greet(groups, span):
+    g, p = lax.axis_index("dp"), lax.axis_index("pair")
     barrier = pltpu.get_barrier_semaphore()
 
-    def hello(k, carry):
-        pl.semaphore_signal(barrier, inc=1, device_id=partner(k, groups, span), device_id_type=MESH)
-        return carry
-
-    lax.fori_loop(1, groups * span, hello, 0)
-    return lambda: pl.semaphore_wait(barrier, groups * span - 1)
+    def hello(device):
+        pl.semaphore_signal(barrier, inc=1, device_id=device, device_id_type=MESH)
+
+    def hello_pair(k, carry):
+        hello((g, partner(k, groups, span)[1]))
+        return carry
+
+    def hello_group(k, carry):
+        hello((partner(k * span, groups, span)[0], p))
+        return carry
+
+    lax.fori_loop(1, span, hello_pair, 0)
+    lax.fori_loop(1, groups, hello_group, 0)
+    return lambda: pl.semaphore_wait(barrier, span + groups - 2)
+
+
+def ask(request, middle, slots, sems, groups, span):
+    g, p = lax.axis_index("dp"), lax.axis_index("pair")
+    own = pltpu.make_async_copy(request.at[:, p], middle.at[p], sems.at[0])
+    own.start()
+
+    def over_pair(k, carry):
+        to_p = partner(k, groups, span)[1]
+        pltpu.make_async_remote_copy(
+            src_ref=request.at[:, to_p],
+            dst_ref=middle.at[p],
+            send_sem=sems.at[1],
+            recv_sem=sems.at[2],
+            device_id=(g, to_p),
+            device_id_type=MESH,
+        ).start()
+        return carry
+
+    lax.fori_loop(1, span, over_pair, 0)
+    own.wait()
+    drain(middle, span - 1, sems.at[1])
+    drain(middle, span - 1, sems.at[2])
+    own = pltpu.make_async_copy(middle.at[:, g], slots.at[g], sems.at[3])
+    own.start()
+
+    def over_groups(k, carry):
+        to_g = partner(k * span, groups, span)[0]
+        pltpu.make_async_remote_copy(
+            src_ref=middle.at[:, to_g],
+            dst_ref=slots.at[g],
+            send_sem=sems.at[4],
+            recv_sem=sems.at[5],
+            device_id=(to_g, p),
+            device_id_type=MESH,
+        ).start()
+        return carry
+
+    lax.fori_loop(1, groups, over_groups, 0)
+    own.wait()
+    if groups > 1:
+        drain(slots, groups - 1, sems.at[4])
+        drain(slots, groups - 1, sems.at[5])
 
 
 def drain(ref, count, sem):
@@ -574,7 +629,7 @@
 def update(
     slots_ref, back_ref, table_ref, accum_ref, parts_ref, tnew_ref, anew_ref, gin_ref, gout_ref, *, width, factor
 ):
-    shards = slots_ref.shape[0]
+    shards = slots_ref.shape[0] * slots_ref.shape[1]
     rows_dev, model = table_ref.shape
     count = shards * width
     spread = ((iota((shards, count), 1) // width) == iota((shards, count), 0)).astype(F32).astype(BF16)
@@ -607,7 +662,7 @@
 
 def layer_kernel(
     row_ref, seg_ref, pair_ref, w_in_ref, w_out_ref, og_ref, table_ref, accum_ref, out_ref, tnew_ref, anew_ref, gin_ref,
-    gout_ref, request, slots, target_r, target_c, meta, found, fetched, x, z, u, q, kv, dhu, wgrad, dq, dk, dv, kv_all,
+    gout_ref, request, middle, slots, target_r, target_c, meta, found, fetched, x, z, u, q, kv, dhu, wgrad, dq, dk, dv, kv_all,
     q_all, da_all, da, parts, acc, mask, grads, hold, sending, back, got, part, landed, local, send, recv, front, sems, *,
     groups, span, width, rows, factor
 ):
@@ -618,13 +673,10 @@
     ready = greet(groups, span)
     route(row_ref, seg_ref, pair_ref, request, target_r, target_c, meta, rows_dev=rows_dev, width=width)
     ready()
-    own = keep(request, slots, front.at[0], span)
-    asked = push_all(request, slots, front.at[1], front.at[2], groups, span, 1)
-    own.wait()
-    asked()
+    ask(request, middle, slots, front, groups, span)
     find(slots, table_ref, found, width=width)
-    own = keep(found, fetched, front.at[3], span)
-    answered = push_all(found, fetched, front.at[4], front.at[5], groups, span, bound)
+    own = keep(found, fetched, front.at[6], span)
+    answered = push_all(found, fetched, front.at[7], front.at[8], groups, span, bound)
     own.wait()
     answered()
     group = project(fetched, target_c, w_in_ref, x, z, u, q, kv)
@@ -676,8 +728,9 @@
         in_specs=[whole()] * 8,
         out_specs=[whole()] * 5,
         scratch_shapes=[
-            VMEM((shards, 1, 128), I32),
-            VMEM((shards, 1, 128), I32),
+            VMEM((shards // span, span, 1, 128), I32),
+            VMEM((span, shards // span, 1, 128), I32),
+            VMEM((shards // span, span, 1, 128), I32),
             VMEM((1, tokens), I32),
             VMEM((tokens, 1), I32),
             VMEM((8, 128), F32),
@@ -710,7 +763,7 @@
             pltpu.SemaphoreType.DMA((3,)),
             pltpu.SemaphoreType.DMA((3, 15)),
             pltpu.SemaphoreType.DMA((3, 15)),
-            pltpu.SemaphoreType.DMA((6,)),
+            pltpu.SemaphoreType.DMA((9,)),
             pltpu.SemaphoreType.DMA((8,)),
         ],
         compiler_params=params(collective_id=0, has_side_effects=True),

time: 159 us -> 151 us (0.950)
  Pallas kernels: 151 us -> 143 us
    pallas_call x1, Pallas kernels: 151 us -> 143 us  [body(): pl.pallas_call(functools.partial(layer_kernel, groups=shards // span, spa...]
where the time goes in v6:
time: 151 us
  Pallas kernels  143 us (95%)
  local copies, waits for them, and re-layouts  7.09 us (5%)
    pallas_call x1, Pallas kernels, body(): pl.pallas_call(functools.partial(layer_kernel, groups=shards // span, spa...  143 us
    unnamed x11, local copies, waits for them, and re-layouts  5.84 us

profile of v6, /device:TPU:1, one launch (start us, length us, event | category | flops | bytes accessed | tf_op | source)
XLA Modules:
  0.0 151.1 jit_solution(8879794172991321445)
XLA Ops:
  0.6 1.2 reshape.19.row_ref
  1.9 143.3 %shard_map.119 = (bf16[384,512]{1,0:T(8,128)(2,1)}, f32[512,512]{1,0:T(8,128)}, f32[1,512]{1,0:T(1,128)}, f32[4,2048]{1,0:T(4,128)}, f32[4,512]{1,0:T(4,128)}) custom-call(s32[1,384]{1,0:T(1,128)} %reshape.19.row_ref, s32[1,3072]{1,0:T(1,128)} %seg_ref.1, s32[2,40]{1,0:T(2,128)} %bitcast.7, bf16[512,2048]{1,0:T(8,128)(2,1)} %w_in_ref.1, ...), custom_call_target="tpu_custom_call" | custom-call | tf_op jit(solution)/shard_map/pallas_call | solution.py:712
  145.2 0.0 copy-start.2
  145.2 0.0 copy-start
  145.2 0.0 copy-start.1
  145.2 1.8 %copy.18 = bf16[384,512]{1,0:T(8,128)(2,1)} copy(bf16[384,512]{1,0:T(8,128)(2,1)} %get-tuple-element.20) | data formatting | bytes 786432
  147.0 2.3 %copy.19 = f32[512,512]{1,0:T(8,128)} copy(f32[512,512]{1,0:T(8,128)} %get-tuple-element.21) | data formatting | bytes 2097152
  149.3 0.0 copy-done.2
  149.3 0.6 copy.20
  149.9 0.0 copy-done
  149.9 0.6 copy.21
  150.5 0.0 copy-done.1
  150.5 0.6 copy.22
Async XLA Ops:
  145.2 4.1 %copy-start.2 = (f32[1,512]{1,0:T(1,128)S(1)}, f32[1,512]{1,0:T(1,128)}, u32[]{:S(2)}) copy-start(f32[1,512]{1,0:T(1,128)} %get-tuple-element.12) | copy-start | bytes 6148
  145.2 4.6 %copy-start = (f32[4,2048]{1,0:T(4,128)S(1)}, f32[4,2048]{1,0:T(4,128)}, u32[]{:S(2)}) copy-start(f32[4,2048]{1,0:T(4,128)} %get-tuple-element.23) | copy-start | bytes 98308
  145.2 5.3 %copy-start.1 = (f32[4,512]{1,0:T(4,128)S(1)}, f32[4,512]{1,0:T(4,128)}, u32[]{:S(2)}) copy-start(f32[4,512]{1,0:T(4,128)} %get-tuple-element.24) | copy-start | bytes 24580

commit v7 on v6

--- a/solution.py
+++ b/solution.py
@@ -109,7 +109,7 @@
     found_ref[...] = dot(pick, table_ref[...].astype(BF16)).astype(BF16).reshape(found_ref.shape)
 
 
-def project(fetched_ref, tc_ref, w_ref, x_ref, z_ref, u_ref, q_ref, kv_ref):
+def project(fetched_ref, tc_ref, w_ref, x_ref, z_ref, u_ref, q_ref, kv_ref, turned_ref):
     width = fetched_ref.shape[2]
     count = fetched_ref.shape[0] * fetched_ref.shape[1]
     tokens = tc_ref.shape[0]
@@ -118,6 +118,7 @@
     x_ref[...] = rows.astype(BF16)
     normed, _ = normalize(rows)
     low = normed.astype(BF16)
+    turned_ref[...] = jnp.transpose(normed).astype(BF16)
     outs = (u_ref.at[...], kv_ref.at[:, width:], q_ref.at[...], kv_ref.at[:, :width])
 
     def group(g):
@@ -261,7 +262,7 @@
 
 def attend(
     meta_ref, q_ref, kv_ref, u_ref, x_ref, w_ref, og_ref, out_ref, dhu_ref, gout_ref, dq_ref, dk_ref, dv_ref, kv_all,
-    q_all, da_all, da, parts, acc, mask, local, send, recv, group, *, span
+    q_all, da_all, da, parts, acc, mask, local, send, recv, group, early, *, span
 ):
     own = lax.axis_index("pair")
     chips, core, chip = span // 2, own % 2, own // 2
@@ -359,6 +360,8 @@
     dhu_ref[...] = dy * normed
     out_ref[...] = (dot(gated, w_ref[...]) + x_ref[...].astype(F32)).astype(BF16)
     gout_ref[...] = lax.dot_general(gated, og_ref[...], (((0,), (0,)), ((), ())), preferred_element_type=F32)
+    early(0)
+
     def by_query(step, carry):
         j = block_at(step, False)
 
@@ -383,6 +386,7 @@
         return carry
 
     lax.fori_loop(0, span, by_query, 0)
+    early(1)
 
     def by_key(step, carry):
         i = block_at(step, True)
@@ -431,40 +435,30 @@
         ring.sent()
 
 
-def finish(
-    z_ref, dhu_ref, dv_ref, dq_ref, dk_ref, x_ref, w_ref, og_ref, tr_ref, gout_ref, grads_ref, send_ref, hold, *, rows
-):
-    size, width = x_ref.shape
+def interleave(upper, lower, rows, out_ref):
+    count, cols = upper.shape
+    top = (iota((count, cols), 0) % (2 * rows)) < rows
+    first = jnp.where(top, upper, pltpu.roll(lower, rows, 0))
+    second = jnp.where(top, pltpu.roll(upper, count - rows, 0), lower)
+    out_ref[0] = first.reshape(out_ref.shape[1:])
+    out_ref[1] = second.reshape(out_ref.shape[1:])
+
+
+def weigh(g, grad, z_ref, turned_ref, w_ref, dxn_ref):
+    width = grad.shape[1]
+    cols = slice(g * width, (g + 1) * width)
+    h = 0.5 * z_ref[:, cols]
+    t = jnp.tanh(h)
+    slope = 0.5 * (1.0 + t) * (1.0 + h * (1.0 - t))
+    dz = (grad * slope).astype(BF16)
+    dxn_ref[...] += dot_t(dz, w_ref[:, cols])
+    return dot(turned_ref[...], dz)
+
+
+def finish(dxn_ref, x_ref, og_ref, tr_ref, send_ref):
+    size = x_ref.shape[0]
     normed, spread = normalize(x_ref[...].astype(F32))
-    turned = jnp.transpose(normed).astype(BF16)
-    dxn = jnp.zeros((size, width), F32)
-
-    def place(upper, lower, at):
-        count, cols = upper.shape
-        top = (iota((count, cols), 0) % (2 * rows)) < rows
-        first = jnp.where(top, upper, pltpu.roll(lower, rows, 0))
-        second = jnp.where(top, pltpu.roll(upper, count - rows, 0), lower)
-        whole_shape = (count // (2 * rows), 2 * rows, cols)
-        grads_ref[0, :, :, at : at + cols] = first.reshape(whole_shape)
-        grads_ref[1, :, :, at : at + cols] = second.reshape(whole_shape)
-
-    for g, grad in enumerate((dhu_ref, dv_ref, dq_ref, dk_ref)):
-        cols = slice(g * width, (g + 1) * width)
-        h = 0.5 * z_ref[:, cols]
-        t = jnp.tanh(h)
-        slope = 0.5 * (1.0 + t) * (1.0 + h * (1.0 - t))
-        dz = (grad[...] * slope).astype(BF16)
-        part = dot(turned, dz)
-        if g == 0:
-            hold[...] = part
-        elif g == 1:
-            place(part, gout_ref[...], width)
-        elif g == 2:
-            place(part[:, : width // 2], part[:, width // 2 :], 2 * width)
-        else:
-            place(hold[...], part, 0)
-        dxn += dot_t(dz, w_ref[:, cols])
-    dx = norm_back(dxn, normed, spread) + og_ref[...].astype(F32)
+    dx = norm_back(dxn_ref[...], normed, spread) + og_ref[...].astype(F32)
     count = send_ref.shape[0] * send_ref.shape[1]
     pick = jnp.where(iota((count, size), 0) == tr_ref[...], 1.0, 0.0).astype(BF16)
     send_ref[...] = dot(pick, dx.astype(BF16)).astype(BF16).reshape(send_ref.shape)
@@ -580,7 +574,74 @@
     return copy
 
 
-def exchange_gradients(rows_ref, grads_ref, back_ref, parts_ref, got, part, sems, *, groups, span, bound):
+def push_early(early_ref, arrived_ref, cols, sems, groups, span):
+    g, p = lax.axis_index("dp"), lax.axis_index("pair")
+    count = early_ref.shape[0] // groups
+
+    def mine(to_g):
+        return early_ref.at[pl.ds(pl.multiple_of(to_g * count, count), count), cols]
+
+    own = pltpu.make_async_copy(mine(g), arrived_ref.at[g, :, cols], sems.at[0])
+    own.start()
+
+    def push(k, carry):
+        to_g = partner(k * span, groups, span)[0]
+        pltpu.make_async_remote_copy(
+            src_ref=mine(to_g),
+            dst_ref=arrived_ref.at[g, :, cols],
+            send_sem=sems.at[1],
+            recv_sem=sems.at[2],
+            device_id=(to_g, p),
+            device_id_type=MESH,
+        ).start()
+        return carry
+
+    lax.fori_loop(1, groups, push, 0)
+
+
+def wait_early(early_ref, arrived_ref, cols, sems, groups):
+    pltpu.make_async_copy(arrived_ref.at[0, :, cols], arrived_ref.at[0, :, cols], sems.at[0]).wait()
+    if groups > 1:
+        others = arrived_ref.at[pl.ds(0, groups - 1), :, cols]
+        pltpu.make_async_copy(others, others, sems.at[1]).wait()
+        pltpu.make_async_copy(others, others, sems.at[2]).wait()
+
+
+def settle(arrived_ref, halves_ref, settled_ref, sems, groups, span, rows):
+    g, p = lax.axis_index("dp"), lax.axis_index("pair")
+    count, cols = arrived_ref.shape[1:]
+
+    def add(k, summed):
+        return summed + arrived_ref[k].astype(F32)
+
+    summed = lax.fori_loop(0, groups, add, jnp.zeros((count, cols), F32))
+    interleave(summed[:, : cols // 2], summed[:, cols // 2 :], rows, halves_ref)
+    own = pltpu.make_async_copy(halves_ref.at[p % 2, p // 2], settled_ref.at[p], sems.at[0])
+    own.start()
+
+    def push(k, carry):
+        to_p = partner(k, groups, span)[1]
+        pltpu.make_async_remote_copy(
+            src_ref=halves_ref.at[to_p % 2, to_p // 2],
+            dst_ref=settled_ref.at[p],
+            send_sem=sems.at[1],
+            recv_sem=sems.at[2],
+            device_id=(g, to_p),
+            device_id_type=MESH,
+        ).start()
+        return carry
+
+    lax.fori_loop(1, span, push, 0)
+
+    def wait():
+        own.wait()
+        drain(settled_ref, span - 1, sems.at[1])
+        drain(settled_ref, span - 1, sems.at[2])
+
+    return wait
+
+
+def exchange_gradients(rows_ref, grads_ref, back_ref, parts_ref, got, part, sems, between, *, groups, span, bound):
     total = groups * span
     g, p = lax.axis_index("dp"), lax.axis_index("pair")
     me, core = g * span + p, p % 2
@@ -596,6 +657,7 @@
     swap.start()
     own = keep(rows_ref, back_ref, sems.at[0], span)
     landed = push_all(rows_ref, back_ref, sems.at[3], sems.at[4], groups, span, bound)
+    settled = between()
     swap.wait()
 
     def add(m, carry):
@@ -621,13 +683,15 @@
     lax.fori_loop(1, chips, push_part, 0)
     own.wait()
     mine.wait()
+    settled()
     landed()
     drain(parts_ref, chips - 1, sems.at[6])
     drain(parts_ref, chips - 1, sems.at[7])
 
 
 def update(
-    slots_ref, back_ref, table_ref, accum_ref, parts_ref, tnew_ref, anew_ref, gin_ref, gout_ref, *, width, factor
+    slots_ref, back_ref, table_ref, accum_ref, parts_ref, settled_ref, tnew_ref, anew_ref, gin_ref, gout_ref, *, width,
+    factor
 ):
     shards = slots_ref.shape[0] * slots_ref.shape[1]
     rows_dev, model = table_ref.shape
@@ -646,24 +710,28 @@
     anew_ref[...] = jnp.sum(jnp.where(eye, accum, 0.0), axis=0, keepdims=True)
     tnew_ref[...] = table_ref[...] - LEARN_RATE * total / jnp.sqrt(accum)
 
-    def add(m, summed):
-        return summed + parts_ref[m].astype(F32)
-
-    summed = lax.fori_loop(0, parts_ref.shape[0], add, jnp.zeros(parts_ref.shape[1:], F32)) * factor
+    def total_of(ref):
+        def add(m, summed):
+            return summed + ref[m].astype(F32)
+
+        summed = lax.fori_loop(0, ref.shape[0], add, jnp.zeros(ref.shape[1:], F32)) * factor
+        return summed[:rows], summed[rows:]
+
     rows = gin_ref.shape[0]
-    upper, lower = summed[:rows], summed[rows:]
+    half = model // 2
+    gin_ref[:, model : 2 * model], gin_ref[:, 3 * model :] = total_of(parts_ref)
+    upper, lower = total_of(settled_ref)
     gin_ref[:, :model] = upper[:, :model]
-    gin_ref[:, model : 2 * model] = upper[:, model : 2 * model]
-    gin_ref[:, 2 * model : 2 * model + model // 2] = upper[:, 2 * model :]
-    gin_ref[:, 2 * model + model // 2 : 3 * model] = lower[:, 2 * model :]
-    gin_ref[:, 3 * model :] = lower[:, :model]
-    gout_ref[...] = lower[:, model : 2 * model]
+    gin_ref[:, 2 * model : 3 * model] = lower[:, half:]
+    gout_ref[:, :half] = upper[:, model:]
+    gout_ref[:, half:] = lower[:, :half]
 
 
 def layer_kernel(
     row_ref, seg_ref, pair_ref, w_in_ref, w_out_ref, og_ref, table_ref, accum_ref, out_ref, tnew_ref, anew_ref, gin_ref,
     gout_ref, request, middle, slots, target_r, target_c, meta, found, fetched, x, z, u, q, kv, dhu, wgrad, dq, dk, dv, kv_all,
-    q_all, da_all, da, parts, acc, mask, grads, hold, sending, back, got, part, landed, local, send, recv, front, sems, *,
+    q_all, da_all, da, parts, acc, mask, turned, dxn, early, arrived, halves, settled, grads, sending, back, got, part, landed, local, send, recv, front, sems,
+    first_sems, second_sems, settle_sems, *,
     groups, span, width, rows, factor
 ):
     tokens, rows_dev = row_ref.shape[1], table_ref.shape[0]
@@ -679,17 +747,38 @@
     answered = push_all(found, fetched, front.at[7], front.at[8], groups, span, bound)
     own.wait()
     answered()
-    group = project(fetched, target_c, w_in_ref, x, z, u, q, kv)
+    group = project(fetched, target_c, w_in_ref, x, z, u, q, kv, turned)
+    dxn[...] = jnp.zeros_like(dxn)
+    model = x.shape[1]
+    stages = ((slice(0, 2 * model), first_sems), (slice(2 * model, 3 * model), second_sems))
+
+    def weight(g, grad):
+        return weigh(g, grad[...], z, turned, w_in_ref, dxn)
+
+    def begin(stage):
+        if stage == 0:
+            early[:, :model] = weight(0, dhu).astype(BF16)
+            early[:, model : 2 * model] = wgrad[...].astype(BF16)
+        else:
+            early[:, 2 * model :] = weight(2, dq).astype(BF16)
+        push_early(early, arrived, *stages[stage], groups, span)
+
+    def between():
+        for stage in stages:
+            wait_early(early, arrived, *stage, groups)
+        return settle(arrived, halves, settled, settle_sems, groups, span, rows)
+
     attend(
         meta, q, kv, u, x, w_out_ref, og_ref, out_ref, dhu, wgrad, dq, dk, dv, kv_all, q_all, da_all, da, parts, acc,
-        mask, local, send, recv, group, span=span
+        mask, local, send, recv, group, begin, span=span
     )
-    finish(z, dhu, dv, dq, dk, x, w_in_ref, og_ref, target_r, wgrad, grads, sending, hold, rows=rows)
+    interleave(weight(1, dv), weight(3, dk), rows, grads)
+    finish(dxn, x, og_ref, target_r, sending)
     exchange_gradients(
-        sending, grads, back, landed, got, part, sems, groups=groups, span=span, bound=bound
+        sending, grads, back, landed, got, part, sems, between, groups=groups, span=span, bound=bound
     )
     update(
-        slots, back, table_ref, accum_ref, landed, tnew_ref, anew_ref, gin_ref, gout_ref, width=width, factor=factor
+        slots, back, table_ref, accum_ref, landed, settled, tnew_ref, anew_ref, gin_ref, gout_ref, width=width, factor=factor
     )
 
 
@@ -704,7 +793,9 @@
     span = lax.axis_size("pair")
     width = -(-(2 * tokens // shards) // 8) * 8
     rows = model // shards
-    chunk = (2 * rows, 5 * model // 2)
+    chunk = (2 * rows, model)
+    groups = shards // span
+    settling = (2 * rows, 3 * model // 2)
     half_grads = (shards // 2,) + chunk
     block = lambda cols: VMEM((span, tokens, cols), BF16)
     low = lambda cols: VMEM((tokens, cols), BF16)
@@ -753,8 +844,13 @@
             VMEM((8, tokens, model), BF16),
             high(model),
             high(tokens),
+            VMEM((model, tokens), BF16),
+            high(model),
+            VMEM((model, 3 * model), BF16),
+            VMEM((groups, model // groups, 3 * model), BF16),
+            VMEM((2, span // 2) + settling, F32),
+            VMEM((span,) + settling, F32),
             VMEM((2,) + half_grads, F32),
-            VMEM((model, model), F32),
             VMEM((shards, width, model), BF16),
             VMEM((shards, width, model), BF16),
             VMEM(half_grads, F32),
@@ -765,6 +861,9 @@
             pltpu.SemaphoreType.DMA((3, 15)),
             pltpu.SemaphoreType.DMA((9,)),
             pltpu.SemaphoreType.DMA((8,)),
+            pltpu.SemaphoreType.DMA((3,)),
+            pltpu.SemaphoreType.DMA((3,)),
+            pltpu.SemaphoreType.DMA((3,)),
         ],
         compiler_params=params(collective_id=0, has_side_effects=True),
     )(item_row.reshape(1, tokens), segments, pairs[0].T, w_in, w_out, out_grad, table, accum.reshape(1, rows_dev))

time: 151 us -> 144 us (0.954)
  Pallas kernels: 143 us -> 136 us
    pallas_call x1, Pallas kernels: 143 us -> 136 us  [body(): pl.pallas_call(functools.partial(layer_kernel, groups=shards // span, spa...]
where the time goes in v7:
time: 144 us
  Pallas kernels  136 us (94%)
  local copies, waits for them, and re-layouts  7.09 us (5%)
    pallas_call x1, Pallas kernels, body(): pl.pallas_call(functools.partial(layer_kernel, groups=shards // span, spa...  136 us
    unnamed x11, local copies, waits for them, and re-layouts  5.84 us

profile of v7, /device:TPU:1, one launch (start us, length us, event | category | flops | bytes accessed | tf_op | source)
XLA Modules:
  0.0 143.9 jit_solution(1698166866511145296)
XLA Ops:
  0.6 1.2 reshape.19.row_ref
  1.9 136.1 %shard_map.119 = (bf16[384,512]{1,0:T(8,128)(2,1)}, f32[512,512]{1,0:T(8,128)}, f32[1,512]{1,0:T(1,128)}, f32[4,2048]{1,0:T(4,128)}, f32[4,512]{1,0:T(4,128)}) custom-call(s32[1,384]{1,0:T(1,128)} %reshape.19.row_ref, s32[1,3072]{1,0:T(1,128)} %seg_ref.1, s32[2,40]{1,0:T(2,128)} %bitcast.7, bf16[512,2048]{1,0:T(8,128)(2,1)} %w_in_ref.1, ...), custom_call_target="tpu_custom_call" | custom-call | tf_op jit(solution)/shard_map/pallas_call | solution.py:803
  138.0 0.0 copy-start.2
  138.0 0.0 copy-start
  138.0 0.0 copy-start.1
  138.0 1.8 %copy.18 = bf16[384,512]{1,0:T(8,128)(2,1)} copy(bf16[384,512]{1,0:T(8,128)(2,1)} %get-tuple-element.20) | data formatting | bytes 786432
  139.8 2.3 %copy.19 = f32[512,512]{1,0:T(8,128)} copy(f32[512,512]{1,0:T(8,128)} %get-tuple-element.21) | data formatting | bytes 2097152
  142.1 0.0 copy-done.2
  142.1 0.6 copy.20
  142.7 0.0 copy-done
  142.7 0.6 copy.21
  143.3 0.0 copy-done.1
  143.3 0.6 copy.22
Async XLA Ops:
  138.0 4.1 %copy-start.2 = (f32[1,512]{1,0:T(1,128)S(1)}, f32[1,512]{1,0:T(1,128)}, u32[]{:S(2)}) copy-start(f32[1,512]{1,0:T(1,128)} %get-tuple-element.12) | copy-start | bytes 6148
  138.0 4.6 %copy-start = (f32[4,2048]{1,0:T(4,128)S(1)}, f32[4,2048]{1,0:T(4,128)}, u32[]{:S(2)}) copy-start(f32[4,2048]{1,0:T(4,128)} %get-tuple-element.23) | copy-start | bytes 98308
  138.0 5.3 %copy-start.1 = (f32[4,512]{1,0:T(4,128)S(1)}, f32[4,512]{1,0:T(4,128)}, u32[]{:S(2)}) copy-start(f32[4,512]{1,0:T(4,128)} %get-tuple-element.24) | copy-start | bytes 24580

commit v8 on v7

--- a/solution.py
+++ b/solution.py
@@ -61,12 +61,13 @@
 
 
 def route(row_ref, seg_ref, pair_ref, req_ref, tr_ref, tc_ref, meta_ref, *, rows_dev, width):
-    tokens = row_ref.shape[1]
+    tokens = row_ref.shape[0]
     shards = req_ref.shape[0] * req_ref.shape[1]
     shift = rows_dev.bit_length() - 1
     sub, lane = iota((tokens, tokens), 0), iota((tokens, tokens), 1)
-    owner_r = row_ref[...] >> shift
-    slot_r = (row_ref[...] & (rows_dev - 1)).astype(F32)
+    row = row_ref[...].reshape(1, tokens)
+    owner_r = row >> shift
+    slot_r = (row & (rows_dev - 1)).astype(F32)
     owner_c = jnp.sum(jnp.where(sub == lane, owner_r.astype(F32), 0.0), axis=1, keepdims=True).astype(I32)
     same = owner_c == owner_r
     rank_c = jnp.sum(jnp.where(same & (lane < sub), 1.0, 0.0), axis=1, keepdims=True).astype(I32)
@@ -641,11 +642,9 @@
     return wait
 
 
-def exchange_gradients(rows_ref, grads_ref, back_ref, parts_ref, got, part, sems, between, *, groups, span, bound):
-    total = groups * span
+def swap_halves(grads_ref, got, sems):
     g, p = lax.axis_index("dp"), lax.axis_index("pair")
-    me, core = g * span + p, p % 2
-    chip, chips = me // 2, total // 2
+    core = p % 2
     swap = pltpu.make_async_remote_copy(
         src_ref=grads_ref.at[1 - core],
         dst_ref=got,
@@ -655,9 +654,18 @@
         device_id_type=MESH,
     )
     swap.start()
+    return swap
+
+
+def exchange_gradients(
+    rows_ref, grads_ref, back_ref, parts_ref, got, part, sems, swap, between, *, groups, span, bound
+):
+    total = groups * span
+    g, p = lax.axis_index("dp"), lax.axis_index("pair")
+    me, core = g * span + p, p % 2
+    chip, chips = me // 2, total // 2
     own = keep(rows_ref, back_ref, sems.at[0], span)
     landed = push_all(rows_ref, back_ref, sems.at[3], sems.at[4], groups, span, bound)
-    settled = between()
     swap.wait()
 
     def add(m, carry):
@@ -681,6 +689,7 @@
         return carry
 
     lax.fori_loop(1, chips, push_part, 0)
+    settled = between()
     own.wait()
     mine.wait()
     settled()
@@ -689,9 +698,9 @@
     drain(parts_ref, chips - 1, sems.at[7])
 
 
-def update(
-    slots_ref, back_ref, table_ref, accum_ref, parts_ref, settled_ref, tnew_ref, anew_ref, gin_ref, gout_ref, *, width,
-    factor
+def update_kernel(
+    slots_ref, back_ref, table_ref, accum_ref, parts_ref, settled_ref, layer_ref, tnew_ref, anew_ref, gin_ref, gout_ref,
+    out_ref, *, width, factor
 ):
     shards = slots_ref.shape[0] * slots_ref.shape[1]
     rows_dev, model = table_ref.shape
@@ -725,23 +734,34 @@
     gin_ref[:, 2 * model : 3 * model] = lower[:, half:]
     gout_ref[:, :half] = upper[:, model:]
     gout_ref[:, half:] = lower[:, :half]
+    out_ref[...] = layer_ref[...]
 
 
 def layer_kernel(
-    row_ref, seg_ref, pair_ref, w_in_ref, w_out_ref, og_ref, table_ref, accum_ref, out_ref, tnew_ref, anew_ref, gin_ref,
-    gout_ref, request, middle, slots, target_r, target_c, meta, found, fetched, x, z, u, q, kv, dhu, wgrad, dq, dk, dv, kv_all,
-    q_all, da_all, da, parts, acc, mask, turned, dxn, early, arrived, halves, settled, grads, sending, back, got, part, landed, local, send, recv, front, sems,
-    first_sems, second_sems, settle_sems, *,
-    groups, span, width, rows, factor
+    row_ref, seg_ref, pair_ref, w_in_hbm, w_out_hbm, og_hbm, table_hbm, out_ref, slots, back, landed, settled,
+    w_in_ref, w_out_ref, og_ref, table_ref, request, middle, target_r, target_c, meta, found, fetched, x, z, u, q, kv, dhu, wgrad, dq, dk, dv, kv_all,
+    q_all, da_all, da, parts, acc, mask, turned, dxn, early, arrived, halves, grads, sending, got, part, local, send, recv, front, sems,
+    load_sems, first_sems, second_sems, settle_sems, *,
+    groups, span, width, rows
 ):
-    tokens, rows_dev = row_ref.shape[1], table_ref.shape[0]
+    tokens, rows_dev = row_ref.shape[0], table_ref.shape[0]
     bound = 2 * tokens // (groups * span)
+    loads = [
+        pltpu.make_async_copy(source, target, load_sems.at[i])
+        for i, (source, target) in enumerate(
+            ((table_hbm, table_ref), (w_in_hbm, w_in_ref), (w_out_hbm, w_out_ref), (og_hbm, og_ref))
+        )
+    ]
+    for load in loads:
+        load.start()
     fetched[...] = jnp.zeros_like(fetched)
     back[...] = jnp.zeros_like(back)
     ready = greet(groups, span)
     route(row_ref, seg_ref, pair_ref, request, target_r, target_c, meta, rows_dev=rows_dev, width=width)
     ready()
     ask(request, middle, slots, front, groups, span)
+    for load in loads:
+        load.wait()
     find(slots, table_ref, found, width=width)
     own = keep(found, fetched, front.at[6], span)
     answered = push_all(found, fetched, front.at[7], front.at[8], groups, span, bound)
@@ -773,12 +793,10 @@
         mask, local, send, recv, group, begin, span=span
     )
     interleave(weight(1, dv), weight(3, dk), rows, grads)
+    swap = swap_halves(grads, got, sems)
     finish(dxn, x, og_ref, target_r, sending)
     exchange_gradients(
-        sending, grads, back, landed, got, part, sems, between, groups=groups, span=span, bound=bound
-    )
-    update(
-        slots, back, table_ref, accum_ref, landed, settled, tnew_ref, anew_ref, gin_ref, gout_ref, width=width, factor=factor
+        sending, grads, back, landed, got, part, sems, swap, between, groups=groups, span=span, bound=bound
     )
 
 
@@ -800,28 +818,26 @@
     block = lambda cols: VMEM((span, tokens, cols), BF16)
     low = lambda cols: VMEM((tokens, cols), BF16)
     high = lambda cols: VMEM((tokens, cols), F32)
-    layer_out, table_new, accum_new, grad_in, grad_out = pl.pallas_call(
-        functools.partial(
-            layer_kernel,
-            groups=shards // span,
-            span=span,
-            width=width,
-            rows=rows,
-            factor=1.0 / math.sqrt(tokens * shards),
-        ),
+    request = (groups, span, 1, 128)
+    parcel = (shards, width, model)
+    layer_out, slots, back, landed, settled = pl.pallas_call(
+        functools.partial(layer_kernel, groups=groups, span=span, width=width, rows=rows),
         out_shape=(
             shape((tokens, model), BF16),
-            shape((rows_dev, model), F32),
-            shape((1, rows_dev), F32),
-            shape((rows, 4 * model), F32),
-            shape((rows, model), F32),
+            shape(request, I32),
+            shape(parcel, BF16),
+            shape(half_grads, BF16),
+            shape((span,) + settling, F32),
         ),
-        in_specs=[whole()] * 8,
+        in_specs=[whole()] * 3 + [pl.BlockSpec(memory_space=pl.ANY)] * 4,
         out_specs=[whole()] * 5,
         scratch_shapes=[
-            VMEM((shards // span, span, 1, 128), I32),
-            VMEM((span, shards // span, 1, 128), I32),
-            VMEM((shards // span, span, 1, 128), I32),
+            VMEM(w_in.shape, BF16),
+            VMEM(w_out.shape, BF16),
+            VMEM(out_grad.shape, BF16),
+            VMEM(table.shape, F32),
+            VMEM(request, I32),
+            VMEM((span, groups, 1, 128), I32),
             VMEM((1, tokens), I32),
             VMEM((tokens, 1), I32),
             VMEM((8, 128), F32),
@@ -849,24 +865,35 @@
             VMEM((model, 3 * model), BF16),
             VMEM((groups, model // groups, 3 * model), BF16),
             VMEM((2, span // 2) + settling, F32),
-            VMEM((span,) + settling, F32),
             VMEM((2,) + half_grads, F32),
-            VMEM((shards, width, model), BF16),
-            VMEM((shards, width, model), BF16),
+            VMEM(parcel, BF16),
             VMEM(half_grads, F32),
-            VMEM(half_grads, BF16),
             VMEM(half_grads, BF16),
             pltpu.SemaphoreType.DMA((3,)),
             pltpu.SemaphoreType.DMA((3, 15)),
             pltpu.SemaphoreType.DMA((3, 15)),
             pltpu.SemaphoreType.DMA((9,)),
             pltpu.SemaphoreType.DMA((8,)),
+            pltpu.SemaphoreType.DMA((4,)),
             pltpu.SemaphoreType.DMA((3,)),
             pltpu.SemaphoreType.DMA((3,)),
             pltpu.SemaphoreType.DMA((3,)),
         ],
         compiler_params=params(collective_id=0, has_side_effects=True),
-    )(item_row.reshape(1, tokens), segments, pairs[0].T, w_in, w_out, out_grad, table, accum.reshape(1, rows_dev))
+    )(item_row, segments, pairs[0].T, w_in, w_out, out_grad, table)
+    table_new, accum_new, grad_in, grad_out, layer_out = pl.pallas_call(
+        functools.partial(update_kernel, width=width, factor=1.0 / math.sqrt(tokens * shards)),
+        out_shape=(
+            shape((rows_dev, model), F32),
+            shape((1, rows_dev), F32),
+            shape((rows, 4 * model), F32),
+            shape((rows, model), F32),
+            shape((tokens, model), BF16),
+        ),
+        in_specs=[whole()] * 7,
+        out_specs=[whole()] * 5,
+        compiler_params=params(),
+    )(slots, back, table, accum.reshape(1, rows_dev), landed, settled, layer_out)
     return layer_out, table_new, accum_new.reshape(rows_dev), grad_in, grad_out
 
 

time: 144 us -> 138 us (0.958)
  local copies, waits for them, and re-layouts: 7.09 us -> 0 us
  Pallas kernels: 136 us -> 138 us
    unnamed x11 -> x0, local copies, waits for them, and re-layouts: 5.84 us -> none
    pallas_call x1 -> x2, Pallas kernels: 136 us -> 138 us  [the longest x1 133 us: body(): pl.pallas_call(functools.partial(layer_kernel, groups=groups, span=span,...]
where the time goes in v8:
time: 138 us
  Pallas kernels  138 us (100%)
    pallas_call x1, Pallas kernels, body(): pl.pallas_call(functools.partial(layer_kernel, groups=groups, span=span,...  133 us
    pallas_call x1, Pallas kernels, body(): pl.pallas_call(functools.partial(update_kernel, width=width, factor=1.0 /...  4.69 us

profile of v8, /device:TPU:1, one launch (start us, length us, event | category | flops | bytes accessed | tf_op | source)
XLA Modules:
  0.0 138.3 jit_solution(7400164293556751079)
XLA Ops:
  0.6 133.0 %shard_map.119 = (bf16[384,512]{1,0:T(8,128)(2,1)}, s32[16,8,1,128]{3,2,1,0:T(1,128)}, bf16[128,8,512]{2,1,0:T(8,128)(2,1)}, bf16[64,8,512]{2,1,0:T(8,128)(2,1)}, f32[8,8,768]{2,1,0:T(8,128)}) custom-call(s32[384]{0:T(512)} %row_ref.1, s32[1,3072]{1,0:T(1,128)} %seg_ref.1, s32[2,40]{1,0:T(2,128)} %bitcast.6, bf16[512,2048]{1,0:T(8,128)(2,1)} %w_in_hbm.1, ...), custom_call_target="tpu_custom_call" | custom-call | tf_op jit(solution)/shard_map/pallas_call | solution.py:823
  133.6 4.7 %shard_map.120 = (f32[512,512]{1,0:T(8,128)}, f32[1,512]{1,0:T(1,128)}, f32[4,2048]{1,0:T(4,128)}, f32[4,512]{1,0:T(4,128)}, bf16[384,512]{1,0:T(8,128)(2,1)}) custom-call(s32[16,8,1,128]{3,2,1,0:T(1,128)} %get-tuple-element.15.slots_ref, bf16[128,8,512]{2,1,0:T(8,128)(2,1)} %get-tuple-element.16.back_ref, f32[512,512]{1,0:T(8,128)} %table_ref.1, ...), custom_call_target="tpu_custom_call" | custom-call | tf_op jit(solution)/shard_map/pallas_call | solution.py:884

commit v9 on v8

--- a/solution.py
+++ b/solution.py
@@ -301,7 +301,7 @@
             work(pl.ds(first, 128), pl.ds(pl.multiple_of(width + s * 128, 128), 128))
             return carry
 
-        lax.fori_loop(0, width // 128, one, 0)
+        lax.fori_loop(0, width // 128, one, 0, unroll=True)
 
     def both(rows):
         return jnp.concatenate([even_half(rows), odd_half(rows)], axis=0)

time: 138 us -> 134 us (0.971)
  Pallas kernels: 138 us -> 133 us
    pallas_call x1, Pallas kernels: 133 us -> 128 us  [body(): pl.pallas_call(functools.partial(layer_kernel, groups=groups, span=span,...]
where the time goes in v9:
time: 134 us
  Pallas kernels  133 us (99%)
    pallas_call x1, Pallas kernels, body(): pl.pallas_call(functools.partial(layer_kernel, groups=groups, span=span,...  128 us
    pallas_call x1, Pallas kernels, body(): pl.pallas_call(functools.partial(update_kernel, width=width, factor=1.0 /...  4.67 us

profile of v9, /device:TPU:1, one launch (start us, length us, event | category | flops | bytes accessed | tf_op | source)
XLA Modules:
  0.0 133.7 jit_solution(11454048794619684187)
XLA Ops:
  0.6 128.4 %shard_map.119 = (bf16[384,512]{1,0:T(8,128)(2,1)}, s32[16,8,1,128]{3,2,1,0:T(1,128)}, bf16[128,8,512]{2,1,0:T(8,128)(2,1)}, bf16[64,8,512]{2,1,0:T(8,128)(2,1)}, f32[8,8,768]{2,1,0:T(8,128)}) custom-call(s32[384]{0:T(512)} %row_ref.1, s32[1,3072]{1,0:T(1,128)} %seg_ref.1, s32[2,40]{1,0:T(2,128)} %bitcast.6, bf16[512,2048]{1,0:T(8,128)(2,1)} %w_in_hbm.1, ...), custom_call_target="tpu_custom_call" | custom-call | tf_op jit(solution)/shard_map/pallas_call | solution.py:823
  129.1 4.7 %shard_map.120 = (f32[512,512]{1,0:T(8,128)}, f32[1,512]{1,0:T(1,128)}, f32[4,2048]{1,0:T(4,128)}, f32[4,512]{1,0:T(4,128)}, bf16[384,512]{1,0:T(8,128)(2,1)}) custom-call(s32[16,8,1,128]{3,2,1,0:T(1,128)} %get-tuple-element.15.slots_ref, bf16[128,8,512]{2,1,0:T(8,128)(2,1)} %get-tuple-element.16.back_ref, f32[512,512]{1,0:T(8,128)} %table_ref.1, ...), custom_call_target="tpu_custom_call" | custom-call | tf_op jit(solution)/shard_map/pallas_call | solution.py:884

commit v10 on v9

--- a/solution.py
+++ b/solution.py
@@ -202,6 +202,16 @@
                 if i in self.sends[rank]:
                     self.copy(i).start()
 
+    def start_part(self, part):
+        if part == 1:
+            self.own().start()
+
+        @self.when(0, 1, 2, 3)
+        def _(rank):
+            for i in ((0, 3, 4), (1, 2, 5))[part]:
+                if i in self.sends[rank]:
+                    self.copy(i).start()
+
     def arrive(self, *which):
         for i in which:
             self.copy(i).wait_recv()
@@ -351,12 +361,15 @@
 
     lax.fori_loop(0, span, forward, 0)
 
-    normed, spread = normalize(acc[...])
-    gate = u_ref[...].astype(F32)
-    gated = (normed * gate).astype(BF16)
+    for part in range(2):
+        rows = slice(part * (size // 2), (part + 1) * (size // 2))
+        normed, spread = normalize(acc[rows])
+        acc[rows] = normed
+        da[rows] = norm_back(dhu_ref[rows] * u_ref[rows].astype(F32), normed, spread).astype(BF16)
+        da_ring.start_part(part)
+    normed = acc[...]
     dy = dhu_ref[...]
-    da[...] = norm_back(dy * gate, normed, spread).astype(BF16)
-    da_ring.start()
+    gated = (normed * u_ref[...].astype(F32)).astype(BF16)
     split(da[...] * 0.0625, 2)
     dhu_ref[...] = dy * normed
     out_ref[...] = (dot(gated, w_ref[...]) + x_ref[...].astype(F32)).astype(BF16)

time: 134 us -> 134 us (level)
  no operation moved by 1% of the time
where the time goes in v10:
time: 134 us
  Pallas kernels  133 us (99%)
    pallas_call x1, Pallas kernels, body(): pl.pallas_call(functools.partial(layer_kernel, groups=groups, span=span,...  129 us
    pallas_call x1, Pallas kernels, body(): pl.pallas_call(functools.partial(update_kernel, width=width, factor=1.0 /...  4.67 us

profile of v10, /device:TPU:1, one launch (start us, length us, event | category | flops | bytes accessed | tf_op | source)
XLA Modules:
  0.0 133.9 jit_solution(2340342185930970373)
XLA Ops:
  0.6 128.6 %shard_map.119 = (bf16[384,512]{1,0:T(8,128)(2,1)}, s32[16,8,1,128]{3,2,1,0:T(1,128)}, bf16[128,8,512]{2,1,0:T(8,128)(2,1)}, bf16[64,8,512]{2,1,0:T(8,128)(2,1)}, f32[8,8,768]{2,1,0:T(8,128)}) custom-call(s32[384]{0:T(512)} %row_ref.1, s32[1,3072]{1,0:T(1,128)} %seg_ref.1, s32[2,40]{1,0:T(2,128)} %bitcast.6, bf16[512,2048]{1,0:T(8,128)(2,1)} %w_in_hbm.1, ...), custom_call_target="tpu_custom_call" | custom-call | tf_op jit(solution)/shard_map/pallas_call | solution.py:836
  129.2 4.7 %shard_map.120 = (f32[512,512]{1,0:T(8,128)}, f32[1,512]{1,0:T(1,128)}, f32[4,2048]{1,0:T(4,128)}, f32[4,512]{1,0:T(4,128)}, bf16[384,512]{1,0:T(8,128)(2,1)}) custom-call(s32[16,8,1,128]{3,2,1,0:T(1,128)} %get-tuple-element.15.slots_ref, bf16[128,8,512]{2,1,0:T(8,128)(2,1)} %get-tuple-element.16.back_ref, f32[512,512]{1,0:T(8,128)} %table_ref.1, ...), custom_call_target="tpu_custom_call" | custom-call | tf_op jit(solution)/shard_map/pallas_call | solution.py:897
